TPU v7x, 256 devices: a whole 4x4x8 slice. The times are simulated.
256 devices in a mesh: seq: 64 (over z, x_lo, y), ch: 4 (over x_hi, core).
Axes of the slice: x: 4 (x_hi: 2, x_lo: 2; x = x_hi * 2 + x_lo), y: 4, z: 8, core: 2. Of those that a mesh axis runs over, the one named last changes fastest.
Arguments:
- hidden_in: bfloat16 [32768, 1024], P('seq'), may hold values from -6 to 6
- proj_zx: bfloat16 [512, 2, 1024], P(None, None, 'ch'), may hold values from -0.25 to 0.25
- proj_bc: bfloat16 [512, 128], replicated, may hold values from -0.0625 to 0.0625
- proj_dt: bfloat16 [512, 16], P(None, 'ch'), may hold values from -0.25 to 0.25
- conv_x: bfloat16 [4, 1024], P(None, 'ch'), may hold values from -3 to 3
- conv_bc: bfloat16 [4, 128], replicated, may hold values from -3 to 3
- dt_bias: float32 [16], P('ch'), may hold values from -7 to 1, as said below
- decay_exp: int32 [16], P('ch'), may hold values from 2 to 25
- skip_gain: float32 [16], P('ch'), may hold values from 0.5 to 1.5
- norm_gain: float32 [1024], P('ch'), may hold values from 0.5 to 2
- out_proj: bfloat16 [1024, 512], P('ch'), may hold values from -0.1875 to 0.1875
Outputs:
- hidden_out: bfloat16 [32768, 1024], P('seq', 'ch')
Inputs may be any that keep to these rules, and one draw needn't show every extreme that they name: `dt_bias`: added to each head's step size logits before the softplus.
All inputs are finite; a program needn't handle non-finite values.
Results may differ from a plain program's by a relative error of at most 0.013.
Values may be sent and summed in bfloat16 or wider, within the bound.
No kernel may reach another device: no remote copies, remote signals or barrier semaphores. Data moves between devices by JAX's collectives and lax.ppermute only.
A program may use at most 128 MiB of HBM per device.

v0:
```python
import jax
import jax.numpy as jnp
from jax import lax
from jax.sharding import Mesh
from jax.sharding import PartitionSpec as P

BLOCK = 256
SEQ = ("seq_0", "seq_1", "seq_2")


EPS = 1e-05


def padded_2(block, sides, width):
    for axis, dim in sides:
        count = lax.axis_size(axis)
        forward = [(i, i + 1) for i in range(count - 1)]
        backward = [(target, source) for source, target in forward]
        low = lax.ppermute(
            lax.slice_in_dim(block, block.shape[dim] - width, None, axis=dim), axis, forward
        )
        high = lax.ppermute(lax.slice_in_dim(block, 0, width, axis=dim), axis, backward)
        block = jnp.concatenate([low, block, high], axis=dim)
    return block


def nothing_yet(shard, identity):
    return jax.tree.map(
        lambda part, zero: jnp.zeros_like(part) + jnp.asarray(zero, part.dtype), shard, identity
    )


def prefix_by_axis(shard, axes, combine, identity, reverse):
    before = start = nothing_yet(shard, identity)
    so_far = shard
    for axis in reversed(axes):
        devices, place = (lax.axis_size(axis), lax.axis_index(axis))
        pieces = jax.tree.map(
            lambda part, kind: lax.all_gather(part.astype(kind), axis),
            so_far,
            (jnp.bfloat16, jnp.bfloat16),
        )
        inside, so_far = (start, start)
        for k in reversed(range(devices)) if reverse else range(devices):
            passed = k > place if reverse else k < place
            so_far = combine(
                so_far, jax.tree.map(lambda part, own: part[k].astype(own.dtype), pieces, shard)
            )
            inside = jax.tree.map(lambda new, old: jnp.where(passed, new, old), so_far, inside)
        before = combine(inside, before)
    return before


def split_up(shard, dim, devices):
    before, after = (shard.shape[:dim], shard.shape[dim + 1 :])
    return jnp.moveaxis(shard.reshape(*before, devices, -1, *after), dim, 0)


def sum_at_owner(shard, axis, dim):
    tiles = split_up(shard, dim, lax.axis_size(axis))
    arrived = lax.all_to_all(tiles, axis, split_axis=0, concat_axis=0, tiled=True)
    return arrived.astype(jnp.float32).sum(axis=0)


def causal_conv(padded, kernel_taps, row_count):
    accumulated = jnp.zeros((row_count, padded.shape[1]), jnp.float32)
    for offset in range(kernel_taps.shape[0]):
        accumulated = accumulated + kernel_taps[offset].astype(jnp.float32) * padded[
            offset : offset + row_count
        ].astype(jnp.float32)
    return jax.nn.silu(accumulated).astype(jnp.bfloat16)


def block_step(carry_state, values, b_rows, c_rows, dt_block, ld_block, skip_gain):
    block_rows = values.shape[0]
    cumulative = jnp.cumsum(ld_block, axis=0)
    scores = jnp.dot(c_rows, b_rows.T, preferred_element_type=jnp.float32)
    differences = cumulative.T[:, :, None] - cumulative.T[:, None, :]
    positions = jnp.arange(block_rows, dtype=jnp.int32)
    causal_mask = positions[:, None] >= positions[None, :]
    decays = jnp.exp(jnp.where(causal_mask[None], differences, -jnp.inf))
    weights = (scores[None] * decays * dt_block.T[:, None, :]).astype(jnp.bfloat16)
    within = jnp.einsum("hts,shp->thp", weights, values, preferred_element_type=jnp.float32)
    carried = jnp.exp(cumulative)[:, :, None] * jnp.einsum(
        "tn,hpn->thp", c_rows.astype(jnp.float32), carry_state, precision=lax.Precision.HIGHEST
    )
    to_end = jnp.exp(cumulative[-1:] - cumulative) * dt_block
    loaded = (values.astype(jnp.float32) * to_end[:, :, None]).astype(jnp.bfloat16)
    added_state = jnp.einsum("thp,tn->hpn", loaded, b_rows, preferred_element_type=jnp.float32)
    next_state = jnp.exp(cumulative[-1])[:, None, None] * carry_state + added_state
    result = within + carried + skip_gain[None, :, None] * values.astype(jnp.float32)
    return (next_state, result)


def local_pass(conv_out, step_size, log_decay, skip_gain, head_count, head_size, state_size):
    row_count = conv_out.shape[0]
    inner_width = head_count * head_size
    blocks = row_count // BLOCK
    values = conv_out[:, :inner_width].reshape(blocks, BLOCK, head_count, head_size)
    b_rows = conv_out[:, inner_width : inner_width + state_size].reshape(blocks, BLOCK, state_size)
    c_rows = conv_out[:, inner_width + state_size :].reshape(blocks, BLOCK, state_size)
    dt_blocks = step_size.reshape(blocks, BLOCK, head_count)
    ld_blocks = log_decay.reshape(blocks, BLOCK, head_count)

    def advance(carry_state, inputs):
        return block_step(
            carry_state, inputs[0], inputs[1], inputs[2], inputs[3], inputs[4], skip_gain
        )

    start_state = jnp.zeros((head_count, head_size, state_size), jnp.float32)
    final_state, outputs = lax.scan(
        advance, start_state, (values, b_rows, c_rows, dt_blocks, ld_blocks)
    )
    return (outputs.reshape(row_count, head_count, head_size), final_state)


def summarize(conv_out, step_size, log_decay, skip_gain, head_count, head_size, state_size):
    mixer_out, final_state = local_pass(
        conv_out, step_size, log_decay, skip_gain, head_count, head_size, state_size
    )
    cumulative = jnp.cumsum(log_decay, axis=0)
    c_rows = conv_out[:, head_count * head_size + state_size :]
    return (mixer_out, final_state, cumulative, c_rows)


def finish(pass_result, incoming):
    mixer_out, final_state, cumulative, c_rows = pass_result
    carried = jnp.einsum(
        "tn,hpn->thp", c_rows.astype(jnp.float32), incoming, precision=lax.Precision.HIGHEST
    )
    return mixer_out + jnp.exp(cumulative)[:, :, None] * carried


def combine_states(first_part, second_part):
    joined_total = first_part[0] + second_part[0]
    joined_state = jnp.exp(second_part[0])[:, None, None] * first_part[1] + second_part[1]
    return (joined_total, joined_state)


def gate_norm(mixer_out, gate_z, norm_gain):
    row_count, head_count, head_size = mixer_out.shape
    gated_out = mixer_out * jax.nn.silu(gate_z.astype(jnp.float32)).reshape(
        row_count, head_count, head_size
    )
    mean_square = jnp.mean(gated_out * gated_out, axis=2, keepdims=True)
    return (gated_out * lax.rsqrt(mean_square + EPS)).reshape(
        row_count, head_count * head_size
    ) * norm_gain


def shards(
    hidden_in,
    proj_zx,
    proj_bc,
    proj_dt,
    conv_x,
    conv_bc,
    dt_bias,
    decay_exp,
    skip_gain,
    norm_gain,
    out_proj,
):
    row_count = hidden_in.shape[0]
    model_width = hidden_in.shape[1] // 2
    state_size = proj_bc.shape[1] // 2
    conv_reach = conv_x.shape[0] - 1
    decay_rate = jnp.exp2(-decay_exp.astype(jnp.float32))
    forward_rows = hidden_in[:, :model_width]
    reverse_rows = hidden_in[:, model_width:][:, ::-1]
    strand_inputs = [forward_rows, reverse_rows]
    mixer_in, step_proj, taps_local, out_rows = (proj_zx, proj_dt, conv_x, out_proj)
    bias_heads, rate_heads, skip_heads, gain_cols = (dt_bias, decay_rate, skip_gain, norm_gain)
    heads_local = bias_heads.shape[0]
    inner_local = mixer_in.shape[2]
    head_size = inner_local // heads_local
    strand_count = len(strand_inputs)
    all_weights = jnp.concatenate(
        [mixer_in.reshape(model_width, 2 * inner_local), proj_bc, step_proj], axis=1
    )
    kernel_taps = jnp.concatenate([taps_local, conv_bc], axis=1)
    stacked = jnp.concatenate(strand_inputs, axis=0)
    projected = jnp.dot(stacked, all_weights, preferred_element_type=jnp.float32)
    conv_end = 2 * inner_local + 2 * state_size
    gate_z = projected[:, :inner_local].astype(jnp.bfloat16)
    conv_input = (
        projected[:, inner_local:conv_end]
        .astype(jnp.bfloat16)
        .reshape(strand_count, row_count, conv_end - inner_local)
    )
    step_size = jax.nn.softplus(projected[:, conv_end:] + bias_heads).reshape(
        strand_count, row_count, heads_local
    )
    log_decay = -step_size * rate_heads
    padded = padded_2(conv_input, ((SEQ, 1),), conv_reach)
    passes = []
    for strand in range(strand_count):
        ahead_conv = causal_conv(padded[strand], kernel_taps, row_count)
        behind_conv = causal_conv(padded[strand][::-1], kernel_taps, row_count)
        passes.append(
            summarize(
                ahead_conv,
                step_size[strand],
                log_decay[strand],
                skip_heads,
                heads_local,
                head_size,
                state_size,
            )
        )
        passes.append(
            summarize(
                behind_conv,
                step_size[strand][::-1],
                log_decay[strand][::-1],
                skip_heads,
                heads_local,
                head_size,
                state_size,
            )
        )
    up_totals = jnp.concatenate(
        [passes[2 * strand][2][-1] for strand in range(strand_count)], axis=0
    )
    up_states = jnp.concatenate([passes[2 * strand][1] for strand in range(strand_count)], axis=0)
    down_totals = jnp.concatenate(
        [passes[2 * strand + 1][2][-1] for strand in range(strand_count)], axis=0
    )
    down_states = jnp.concatenate(
        [passes[2 * strand + 1][1] for strand in range(strand_count)], axis=0
    )
    start_value = (jnp.zeros_like(up_totals), jnp.zeros_like(up_states))
    rising = prefix_by_axis((up_totals, up_states), SEQ, combine_states, start_value, False)
    falling = prefix_by_axis((down_totals, down_states), SEQ, combine_states, start_value, True)
    mixed_rows = []
    for strand in range(strand_count):
        head_first = strand * heads_local
        gate_rows = gate_z[strand * row_count : (strand + 1) * row_count]
        ahead_out = finish(passes[2 * strand], rising[1][head_first : head_first + heads_local])
        behind_out = finish(
            passes[2 * strand + 1], falling[1][head_first : head_first + heads_local]
        )[::-1]
        mixed_rows.append(
            (
                gate_norm(ahead_out, gate_rows, gain_cols)
                + gate_norm(behind_out, gate_rows, gain_cols)
            ).astype(jnp.bfloat16)
        )
    forward_part = jnp.dot(mixed_rows[0], out_rows, preferred_element_type=jnp.float32)
    reverse_part = jnp.dot(mixed_rows[1], out_rows[:, ::-1], preferred_element_type=jnp.float32)
    summed = sum_at_owner(
        jnp.concatenate([forward_part, reverse_part], axis=1).astype(jnp.bfloat16), "ch", 1
    )
    column_count = summed.shape[1]
    residual_cols = lax.dynamic_slice_in_dim(
        hidden_in, lax.axis_index("ch") * column_count, column_count, 1
    )
    return (residual_cols.astype(jnp.float32) + summed).astype(jnp.bfloat16)


def solution(mesh):
    torus = Mesh(mesh.devices.reshape(8, 2, 4, mesh.shape["ch"]), ("seq_0", "seq_1", "seq_2", "ch"))
    placed = (
        P(SEQ, None),
        P(None, None, "ch"),
        P(),
        P(None, "ch"),
        P(None, "ch"),
        P(),
        P("ch"),
        P("ch"),
        P("ch"),
        P("ch"),
        P("ch", None),
    )
    return jax.shard_map(
        shards, mesh=torus, in_specs=placed, out_specs=P(SEQ, "ch"), check_vma=False
    )
```

profile of v0, /device:TPU:1, one launch (start us, length us, event | category | flops | bytes accessed | tf_op | source)
XLA Modules:
  0.0 355.7 jit_solution(4972883150097845813)
XLA Ops:
  7.8 4.7 %collective-permute-start = (bf16[2,3,384]{1,2,0:T(8,128)(2,1)}, bf16[2,3,384]{1,2,0:T(8,128)(2,1)}, u32[]{:S(2)}, u32[]{:S(2)}) collective-permute-start(bf16[2,3,384]{1,2,0:T(8,128)(2,1)} %get-tuple-element.629), channel_id=1, source_target_pairs={{0,4},{4,8},{8,12},{12,16},{16,20},{20,24},{24,28},{28,32},{32,36}... | collective-permute-start | bytes 13832 | tf_op jit(solution)/shard_map/ppermute | solution.py:19
  23.6 8.0 %all-gather.3 = bf16[4,1,8]{2,1,0:T(2,128)(2,1)S(1)} all-gather(bf16[1,1,8]{2,1,0:T(2,128)(2,1)S(1)} %maximum_bitcast_fusion.2), channel_id=1, replica_groups=mesh['seq_0'=8,'seq_1'=2,'seq_2'=4,'ch'=4] {'seq_2'}, dimensions={0}, use_global_device_ids=true | all-gather | bytes 80 | tf_op jit(solution)/shard_map/all_gather | solution.py:39
  38.3 5.2 %all-gather = bf16[4,1,8]{2,1,0:T(2,128)(2,1)S(1)} all-gather(bf16[1,1,8]{2,1,0:T(2,128)(2,1)S(1)} %maximum_bitcast_fusion.1), channel_id=1, replica_groups=mesh['seq_0'=8,'seq_1'=2,'seq_2'=4,'ch'=4] {'seq_2'}, dimensions={0}, use_global_device_ids=true | all-gather | bytes 80 | tf_op jit(solution)/shard_map/all_gather | solution.py:39
  50.1 16.4 %all-gather.5 = bf16[8,1,8]{2,1,0:T(2,128)(2,1)S(1)} all-gather(bf16[1,1,8]{2,1,0:T(2,128)(2,1)S(1)} %get-tuple-element.685), channel_id=1, replica_groups=mesh['seq_0'=8,'seq_1'=2,'seq_2'=4,'ch'=4] {'seq_0'}, dimensions={0}, use_global_device_ids=true | all-gather | bytes 144 | tf_op jit(solution)/shard_map/all_gather | solution.py:39
  71.9 10.6 %all-gather.2 = bf16[8,1,8]{2,1,0:T(2,128)(2,1)S(1)} all-gather(bf16[1,1,8]{2,1,0:T(2,128)(2,1)S(1)} %get-tuple-element.682), channel_id=1, replica_groups=mesh['seq_0'=8,'seq_1'=2,'seq_2'=4,'ch'=4] {'seq_0'}, dimensions={0}, use_global_device_ids=true | all-gather | bytes 144 | tf_op jit(solution)/shard_map/all_gather | solution.py:39
  83.7 6.7 %slice.582 = bf16[512,384]{0,1:T(8,128)(2,1)} reverse(bf16[512,384]{0,1:T(8,128)(2,1)} %get-tuple-element.619), dimensions={0} | reverse | bytes 786432 | tf_op jit(solution)/shard_map/slice | solution.py:68
  94.4 4.3 %slice.615 = bf16[512,384]{0,1:T(8,128)(2,1)} reverse(bf16[512,384]{0,1:T(8,128)(2,1)S(1)} %get-tuple-element.620), dimensions={0} | reverse | bytes 786432 | tf_op jit(solution)/shard_map/slice | solution.py:68
  116.1 6.7 %slice.581 = bf16[512,384]{0,1:T(8,128)(2,1)} reverse(bf16[512,384]{0,1:T(8,128)(2,1)} %get-tuple-element.625), dimensions={0} | reverse | bytes 786432 | tf_op jit(solution)/shard_map/slice | solution.py:68
  122.8 6.7 %slice.578 = bf16[512,384]{0,1:T(8,128)(2,1)} reverse(bf16[512,384]{0,1:T(8,128)(2,1)} %get-tuple-element.624), dimensions={0} | reverse | bytes 786432 | tf_op jit(solution)/shard_map/slice | solution.py:68
  129.5 4.3 %slice.575 = bf16[512,384]{0,1:T(8,128)(2,1)} reverse(bf16[512,384]{0,1:T(8,128)(2,1)S(1)} %get-tuple-element.623), dimensions={0} | reverse | bytes 786432 | tf_op jit(solution)/shard_map/slice | solution.py:68
  133.8 4.0 %multiply_convert_fusion.15 = (bf16[512,384]{0,1:T(8,128)(2,1)}, bf16[512,384]{0,1:T(8,128)(2,1)S(1)}, bf16[512,384]{0,1:T(8,128)(2,1)S(1)}) fusion(bf16[2,512,384]{1,2,0:T(8,128)(2,1)S(1)} %copy.237, bf16[2,3,384]{1,2,0:T(8,128)(2,1)} %collective-permute-done, f32[384]{0:T(512)} %get-tuple-element.506, f32[384]{0:T(512)} %get-tuple-element.507, ...), kind=kLoop, calls=%fused_computation.242 | loop fusion | flops 14155776 | bytes 4336128 | tf_op jit(solution)/shard_map/convert_element_type | solution.py:71
  138.6 5.2 %slice.614 = bf16[512,384]{0,1:T(8,128)(2,1)S(1)} reverse(bf16[512,384]{0,1:T(8,128)(2,1)} %get-tuple-element.626), dimensions={0} | reverse | bytes 786432 | tf_op jit(solution)/shard_map/slice | solution.py:68
  143.8 4.3 %slice.611 = bf16[512,384]{0,1:T(8,128)(2,1)} reverse(bf16[512,384]{0,1:T(8,128)(2,1)S(1)} %copy-done.9), dimensions={0} | reverse | bytes 786432 | tf_op jit(solution)/shard_map/slice | solution.py:68
  152.8 15.5 %while.54 = (s32[]{:T(128)}, f32[4,64,64]{2,1,0:T(8,128)S(1)}, f32[2,256,4,64]{1,0,3,2:T(2,128)S(1)}, f32[2,256,4]{1,2,0:T(4,128)}, bf16[2,256,4,64]{1,3,2,0:T(8...) while((s32[]{:T(128)}, f32[4,64,64]{2,1,0:T(8,128)S(1)}, ...), condition=%wide.region_16.17_spmd.clone, body=%wide.region_13.16_spmd.clone.sunk | while | flops 102762512 | bytes 3434078 | solution.py:111
  156.9 3.7 %dynamic_update_slice.23 = f32[2,256,4,64]{1,0,3,2:T(2,128)S(1)} dynamic-update-slice(f32[2,256,4,64]{1,0,3,2:T(2,128)S(1)} %get-tuple-element.974, f32[1,256,4,64]{1,0,3,2:T(1,128)S(1)} %copy.403, s32[]{:T(128)S(6)} %copy.417, s32[]{:T(128)} %constant.119.clone.1..sunk.2, s32[]{:T(128)} %constant.119.clone.1..sunk.2, s32[]{:T(128)} %constant.119.clone.1..sunk.2) | dynamic-update-slice | bytes 524292 | tf_op jit(solution)/shard_map/while/body/jit(dynamic_update_index_in_dim)/dynamic_update_slice | solution.py:111
  164.6 3.7 %dynamic_update_slice.23 = f32[2,256,4,64]{1,0,3,2:T(2,128)S(1)} dynamic-update-slice(f32[2,256,4,64]{1,0,3,2:T(2,128)S(1)} %get-tuple-element.974, f32[1,256,4,64]{1,0,3,2:T(1,128)S(1)} %copy.403, s32[]{:T(128)S(6)} %copy.417, s32[]{:T(128)} %constant.119.clone.1..sunk.2, s32[]{:T(128)} %constant.119.clone.1..sunk.2, s32[]{:T(128)} %constant.119.clone.1..sunk.2) | dynamic-update-slice | bytes 524292 | tf_op jit(solution)/shard_map/while/body/jit(dynamic_update_index_in_dim)/dynamic_update_slice | solution.py:111
  169.1 14.2 %while.55 = (s32[]{:T(128)}, f32[4,64,64]{2,1,0:T(8,128)S(1)}, f32[2,256,4,64]{1,0,3,2:T(2,128)S(1)}, f32[2,256,4]{1,2,0:T(4,128)S(1)}, bf16[2,256,4,64]{1,3,2,0...) while((s32[]{:T(128)}, f32[4,64,64]{2,1,0:T(8,128)S(1)}, ...), condition=%wide.region_24.25_spmd.clone, body=%wide.region_21.24_spmd.clone.sunk | while | flops 102762512 | bytes 3434078 | solution.py:111
  172.5 3.7 %dynamic_update_slice.24 = f32[2,256,4,64]{1,0,3,2:T(2,128)S(1)} dynamic-update-slice(f32[2,256,4,64]{1,0,3,2:T(2,128)S(1)} %get-tuple-element.1010, f32[1,256,4,64]{1,0,3,2:T(1,128)S(1)} %copy.408, s32[]{:T(128)S(6)} %copy.426, s32[]{:T(128)} %constant.119.clone.1..sunk.3, s32[]{:T(128)} %constant.119.clone.1..sunk.3, s32[]{:T(128)} %constant.119.clone.1..sunk.3) | dynamic-update-slice | bytes 524292 | tf_op jit(solution)/shard_map/while/body/jit(dynamic_update_index_in_dim)/dynamic_update_slice | solution.py:111
  179.6 3.7 %dynamic_update_slice.24 = f32[2,256,4,64]{1,0,3,2:T(2,128)S(1)} dynamic-update-slice(f32[2,256,4,64]{1,0,3,2:T(2,128)S(1)} %get-tuple-element.1010, f32[1,256,4,64]{1,0,3,2:T(1,128)S(1)} %copy.408, s32[]{:T(128)S(6)} %copy.426, s32[]{:T(128)} %constant.119.clone.1..sunk.3, s32[]{:T(128)} %constant.119.clone.1..sunk.3, s32[]{:T(128)} %constant.119.clone.1..sunk.3) | dynamic-update-slice | bytes 524292 | tf_op jit(solution)/shard_map/while/body/jit(dynamic_update_index_in_dim)/dynamic_update_slice | solution.py:111
  183.5 10.0 %all_gather.57 = bf16[4,8,64,64]{3,2,1,0:T(8,128)(2,1)S(1)} all-gather(bf16[1,8,64,64]{3,2,1,0:T(8,128)(2,1)S(1)} %pad_maximum_fusion.3), channel_id=1, replica_groups=mesh['seq_0'=8,'seq_1'=2,'seq_2'=4,'ch'=4] {'seq_2'}, dimensions={0}, use_global_device_ids=true | all-gather | bytes 327680 | tf_op jit(solution)/shard_map/all_gather | solution.py:39
  193.8 4.5 %all_gather.58 = bf16[2,8,64,64]{3,2,1,0:T(8,128)(2,1)S(1)} all-gather(bf16[1,8,64,64]{3,2,1,0:T(8,128)(2,1)S(1)} %fusion.223), channel_id=1, replica_groups=mesh['seq_0'=8,'seq_1'=2,'seq_2'=4,'ch'=4] {'seq_1'}, dimensions={0}, use_global_device_ids=true | all-gather | bytes 196608 | tf_op jit(solution)/shard_map/all_gather | solution.py:39
  198.4 20.3 %all_gather.59 = bf16[8,8,64,64]{3,2,1,0:T(8,128)(2,1)S(1)} all-gather(bf16[1,8,64,64]{3,2,1,0:T(8,128)(2,1)S(1)} %fusion.232), channel_id=1, replica_groups=mesh['seq_0'=8,'seq_1'=2,'seq_2'=4,'ch'=4] {'seq_0'}, dimensions={0}, use_global_device_ids=true | all-gather | bytes 589824 | tf_op jit(solution)/shard_map/all_gather | solution.py:39
  222.5 14.2 %while.52 = (s32[]{:T(128)}, f32[4,64,64]{2,1,0:T(8,128)S(1)}, f32[2,256,4,64]{1,0,3,2:T(2,128)S(1)}, f32[2,256,4]{1,2,0:T(4,128)S(1)}, bf16[2,256,4,64]{1,3,2,0...) while((s32[]{:T(128)}, f32[4,64,64]{2,1,0:T(8,128)S(1)}, ...), condition=%wide.region_3.4_spmd.clone, body=%wide.region_0.3_spmd.clone.sunk | while | flops 102762512 | bytes 3434078 | solution.py:111
  225.9 3.7 %dynamic_update_slice.21 = f32[2,256,4,64]{1,0,3,2:T(2,128)S(1)} dynamic-update-slice(f32[2,256,4,64]{1,0,3,2:T(2,128)S(1)} %get-tuple-element.1046, f32[1,256,4,64]{1,0,3,2:T(1,128)S(1)} %copy.393, s32[]{:T(128)S(6)} %copy.435, s32[]{:T(128)} %constant.119.clone.1..sunk, s32[]{:T(128)} %constant.119.clone.1..sunk, s32[]{:T(128)} %constant.119.clone.1..sunk) | dynamic-update-slice | bytes 524292 | tf_op jit(solution)/shard_map/while/body/jit(dynamic_update_index_in_dim)/dynamic_update_slice | solution.py:111
  232.9 3.7 %dynamic_update_slice.21 = f32[2,256,4,64]{1,0,3,2:T(2,128)S(1)} dynamic-update-slice(f32[2,256,4,64]{1,0,3,2:T(2,128)S(1)} %get-tuple-element.1046, f32[1,256,4,64]{1,0,3,2:T(1,128)S(1)} %copy.393, s32[]{:T(128)S(6)} %copy.435, s32[]{:T(128)} %constant.119.clone.1..sunk, s32[]{:T(128)} %constant.119.clone.1..sunk, s32[]{:T(128)} %constant.119.clone.1..sunk) | dynamic-update-slice | bytes 524292 | tf_op jit(solution)/shard_map/while/body/jit(dynamic_update_index_in_dim)/dynamic_update_slice | solution.py:111
  237.7 14.2 %while.53 = (s32[]{:T(128)}, f32[4,64,64]{2,1,0:T(8,128)S(1)}, f32[2,256,4,64]{1,0,3,2:T(2,128)S(1)}, f32[2,256,4]{1,2,0:T(4,128)S(1)}, bf16[2,256,4,64]{1,3,2,0...) while((s32[]{:T(128)}, f32[4,64,64]{2,1,0:T(8,128)S(1)}, ...), condition=%wide.region_11.12_spmd.clone, body=%wide.region_8.11_spmd.clone.sunk | while | flops 102762512 | bytes 3434078 | solution.py:111
  241.1 3.7 %dynamic_update_slice.22 = f32[2,256,4,64]{1,0,3,2:T(2,128)S(1)} dynamic-update-slice(f32[2,256,4,64]{1,0,3,2:T(2,128)S(1)} %get-tuple-element.1082, f32[1,256,4,64]{1,0,3,2:T(1,128)S(1)} %copy.398, s32[]{:T(128)S(6)} %copy.444, s32[]{:T(128)} %constant.119.clone.1..sunk.1, s32[]{:T(128)} %constant.119.clone.1..sunk.1, s32[]{:T(128)} %constant.119.clone.1..sunk.1) | dynamic-update-slice | bytes 524292 | tf_op jit(solution)/shard_map/while/body/jit(dynamic_update_index_in_dim)/dynamic_update_slice | solution.py:111
  252.0 10.0 %all_gather.51 = bf16[4,8,64,64]{3,2,1,0:T(8,128)(2,1)S(1)} all-gather(bf16[1,8,64,64]{3,2,1,0:T(8,128)(2,1)S(1)} %pad_maximum_fusion.2), channel_id=1, replica_groups=mesh['seq_0'=8,'seq_1'=2,'seq_2'=4,'ch'=4] {'seq_2'}, dimensions={0}, use_global_device_ids=true | all-gather | bytes 327680 | tf_op jit(solution)/shard_map/all_gather | solution.py:39
  262.2 4.5 %all_gather.52 = bf16[2,8,64,64]{3,2,1,0:T(8,128)(2,1)S(1)} all-gather(bf16[1,8,64,64]{3,2,1,0:T(8,128)(2,1)S(1)} %fusion.199), channel_id=1, replica_groups=mesh['seq_0'=8,'seq_1'=2,'seq_2'=4,'ch'=4] {'seq_1'}, dimensions={0}, use_global_device_ids=true | all-gather | bytes 196608 | tf_op jit(solution)/shard_map/all_gather | solution.py:39
  267.0 20.0 %all_gather.53 = bf16[8,8,64,64]{3,2,1,0:T(8,128)(2,1)S(1)} all-gather(bf16[1,8,64,64]{3,2,1,0:T(8,128)(2,1)S(1)} %fusion.208), channel_id=1, replica_groups=mesh['seq_0'=8,'seq_1'=2,'seq_2'=4,'ch'=4] {'seq_0'}, dimensions={0}, use_global_device_ids=true | all-gather | bytes 589824 | tf_op jit(solution)/shard_map/all_gather | solution.py:39
  299.2 39.6 %all-to-all-start = ((bf16[4,512,256]{2,1,0:T(8,128)(2,1)}), bf16[4,512,256]{2,1,0:T(8,128)(2,1)S(1)}, u32[]{:S(2)}, u32[]{:S(2)}) async-start(bf16[4,512,256]{2,1,0:T(8,128)(2,1)} %maximum_bitcast_fusion), calls=%async_computation | async-start | bytes 2097152 | tf_op jit(solution)/shard_map/all_to_all | solution.py:61
  338.8 15.1 %all-to-all-done = bf16[4,512,256]{2,1,0:T(8,128)(2,1)S(1)} async-done(((bf16[4,512,256]{2,1,0:T(8,128)(2,1)}), bf16[4,512,256]{2,1,0:T(8,128)(2,1)S(1)}, u32[]{:S(2)}, u32[]{:S(2)}) %all-to-all-start) | async-done | bytes 1048608 | tf_op jit(solution)/shard_map/all_to_all | solution.py:61
  (456 shorter events, 116.7 us)
Async XLA Ops:
  7.8 126.0 %collective-permute-start = (bf16[2,3,384]{1,2,0:T(8,128)(2,1)}, bf16[2,3,384]{1,2,0:T(8,128)(2,1)}, u32[]{:S(2)}, u32[]{:S(2)}) collective-permute-start(bf16[2,3,384]{1,2,0:T(8,128)(2,1)} %get-tuple-element.629), channel_id=1, source_target_pairs={{0,4},{4,8},{8,12},{12,16},{16,20},{20,24},{24,28},{28,32},{32,36}... | collective-permute-start | bytes 13832 | tf_op jit(solution)/shard_map/ppermute | solution.py:19
  12.5 100.2 %collective-permute-start.1 = (bf16[2,3,384]{1,2,0:T(8,128)(2,1)}, bf16[2,3,384]{1,2,0:T(8,128)(2,1)}, u32[]{:S(2)}, u32[]{:S(2)}) collective-permute-start(bf16[2,3,384]{1,2,0:T(8,128)(2,1)} %get-tuple-element.630), channel_id=1, source_target_pairs={{4,0},{8,4},{12,8},{16,12},{20,16},{24,20},{28,24},{32,28},{36,32}... | collective-permute-start | bytes 13832 | tf_op jit(solution)/shard_map/ppermute | solution.py:22
  22.8 21.3 %copy-start.73 = (bf16[4,256]{1,0:T(4,128)(2,1)S(1)}, bf16[4,256]{1,0:T(4,128)(2,1)}, u32[]{:S(2)}) copy-start(bf16[4,256]{1,0:T(4,128)(2,1)} %param.23) | copy-start | bytes 6148
  22.8 60.2 %copy-start.74 = (bf16[4,128]{1,0:T(4,128)(2,1)S(1)}, bf16[4,128]{1,0:T(4,128)(2,1)}, u32[]{:S(2)}) copy-start(bf16[4,128]{1,0:T(4,128)(2,1)} %param.24) | copy-start | bytes 3076
  169.1 24.4 %copy-start.50 = (f32[8]{0:T(128)S(1)}, f32[8]{0:T(128)}, u32[]{:S(2)}) copy-start(f32[8]{0:T(128)} %get-tuple-element.679) | copy-start | bytes 100
  169.1 24.4 %copy-start.51 = (f32[8]{0:T(128)S(1)}, f32[8]{0:T(128)}, u32[]{:S(2)}) copy-start(f32[8]{0:T(128)} %get-tuple-element.680) | copy-start | bytes 100
  169.1 24.4 %copy-start.52 = (f32[8]{0:T(128)S(1)}, f32[8]{0:T(128)}, u32[]{:S(2)}) copy-start(f32[8]{0:T(128)} %get-tuple-element.681) | copy-start | bytes 100
  169.1 24.4 %copy-start.54 = (f32[8]{0:T(128)S(1)}, f32[8]{0:T(128)}, u32[]{:S(2)}) copy-start(f32[8]{0:T(128)} %get-tuple-element.678) | copy-start | bytes 100
  183.3 35.4 %copy-start.1 = (f32[2,256,4,64]{1,0,3,2:T(2,128)}, f32[2,256,4,64]{1,0,3,2:T(2,128)S(1)}, u32[]{:S(2)}) copy-start(f32[2,256,4,64]{1,0,3,2:T(2,128)S(1)} %get-tuple-element.204) | copy-start | bytes 1572868
  183.4 35.3 %copy-start.63 = (f32[8]{0:T(128)S(1)}, f32[8]{0:T(128)}, u32[]{:S(2)}) copy-start(f32[8]{0:T(128)} %get-tuple-element.664) | copy-start | bytes 100
  183.4 35.3 %copy-start.64 = (f32[8]{0:T(128)S(1)}, f32[8]{0:T(128)}, u32[]{:S(2)}) copy-start(f32[8]{0:T(128)} %get-tuple-element.665) | copy-start | bytes 100
  183.4 35.3 %copy-start.65 = (f32[8]{0:T(128)S(1)}, f32[8]{0:T(128)}, u32[]{:S(2)}) copy-start(f32[8]{0:T(128)} %get-tuple-element.666) | copy-start | bytes 100
  183.4 35.3 %copy-start.66 = (f32[8]{0:T(128)S(1)}, f32[8]{0:T(128)}, u32[]{:S(2)}) copy-start(f32[8]{0:T(128)} %get-tuple-element.667) | copy-start | bytes 100
  183.5 35.3 %copy-start.67 = (f32[8]{0:T(128)S(1)}, f32[8]{0:T(128)}, u32[]{:S(2)}) copy-start(f32[8]{0:T(128)} %get-tuple-element.668) | copy-start | bytes 100
  183.5 35.3 %copy-start.68 = (f32[8]{0:T(128)S(1)}, f32[8]{0:T(128)}, u32[]{:S(2)}) copy-start(f32[8]{0:T(128)} %get-tuple-element.669) | copy-start | bytes 100
  183.5 35.3 %copy-start.69 = (f32[8]{0:T(128)S(1)}, f32[8]{0:T(128)}, u32[]{:S(2)}) copy-start(f32[8]{0:T(128)} %get-tuple-element.670) | copy-start | bytes 100
  183.5 35.3 %copy-start.70 = (f32[8]{0:T(128)S(1)}, f32[8]{0:T(128)}, u32[]{:S(2)}) copy-start(f32[8]{0:T(128)} %get-tuple-element.671) | copy-start | bytes 100
  183.5 35.3 %copy-start.72 = (f32[8]{0:T(128)S(1)}, f32[8]{0:T(128)}, u32[]{:S(2)}) copy-start(f32[8]{0:T(128)} %get-tuple-element.587) | copy-start | bytes 100
  183.5 35.3 %copy-start.77 = (f32[8]{0:T(128)S(1)}, f32[8]{0:T(128)}, u32[]{:S(2)}) copy-start(f32[8]{0:T(128)} %exponential_bitcast_fusion.12) | copy-start | bytes 100
  198.4 21.9 %copy-start.37 = (f32[1,4,4,128]{3,1,2,0:T(4,128)S(1)}, f32[1,4,4,128]{3,1,2,0:T(4,128)}, u32[]{:S(2)}) copy-start(f32[1,4,4,128]{3,1,2,0:T(4,128)} %copy.367) | copy-start | bytes 24580
  237.7 24.3 %copy-start.47 = (f32[8]{0:T(128)S(1)}, f32[8]{0:T(128)}, u32[]{:S(2)}) copy-start(f32[8]{0:T(128)} %get-tuple-element.675) | copy-start | bytes 100
  237.7 24.3 %copy-start.48 = (f32[8]{0:T(128)S(1)}, f32[8]{0:T(128)}, u32[]{:S(2)}) copy-start(f32[8]{0:T(128)} %get-tuple-element.676) | copy-start | bytes 100
  237.7 24.3 %copy-start.49 = (f32[8]{0:T(128)S(1)}, f32[8]{0:T(128)}, u32[]{:S(2)}) copy-start(f32[8]{0:T(128)} %get-tuple-element.677) | copy-start | bytes 100
  237.7 24.3 %copy-start.53 = (f32[8]{0:T(128)S(1)}, f32[8]{0:T(128)}, u32[]{:S(2)}) copy-start(f32[8]{0:T(128)} %get-tuple-element.674) | copy-start | bytes 100
  252.0 35.0 %copy-start = (f32[512,256]{0,1:T(8,128)S(1)}, f32[512,256]{0,1:T(8,128)}, u32[]{:S(2)}) copy-start(f32[512,256]{0,1:T(8,128)} %get-tuple-element.617) | copy-start | bytes 1572868
  266.8 20.4 %copy-start.57 = (f32[8]{0:T(128)S(1)}, f32[8]{0:T(128)}, u32[]{:S(2)}) copy-start(f32[8]{0:T(128)} %get-tuple-element.658) | copy-start | bytes 100
  266.8 20.4 %copy-start.58 = (f32[8]{0:T(128)S(1)}, f32[8]{0:T(128)}, u32[]{:S(2)}) copy-start(f32[8]{0:T(128)} %get-tuple-element.659) | copy-start | bytes 100
  266.8 20.4 %copy-start.59 = (f32[8]{0:T(128)S(1)}, f32[8]{0:T(128)}, u32[]{:S(2)}) copy-start(f32[8]{0:T(128)} %get-tuple-element.660) | copy-start | bytes 100
  266.8 20.4 %copy-start.60 = (f32[8]{0:T(128)S(1)}, f32[8]{0:T(128)}, u32[]{:S(2)}) copy-start(f32[8]{0:T(128)} %get-tuple-element.661) | copy-start | bytes 100
  266.8 20.4 %copy-start.61 = (f32[8]{0:T(128)S(1)}, f32[8]{0:T(128)}, u32[]{:S(2)}) copy-start(f32[8]{0:T(128)} %get-tuple-element.662) | copy-start | bytes 100
  266.8 20.4 %copy-start.62 = (f32[8]{0:T(128)S(1)}, f32[8]{0:T(128)}, u32[]{:S(2)}) copy-start(f32[8]{0:T(128)} %get-tuple-element.663) | copy-start | bytes 100
  299.2 54.7 %all-to-all-start = ((bf16[4,512,256]{2,1,0:T(8,128)(2,1)}), bf16[4,512,256]{2,1,0:T(8,128)(2,1)S(1)}, u32[]{:S(2)}, u32[]{:S(2)}) async-start(bf16[4,512,256]{2,1,0:T(8,128)(2,1)} %maximum_bitcast_fusion), calls=%async_computation | async-start | bytes 2097152 | tf_op jit(solution)/shard_map/all_to_all | solution.py:61
  (51 other events, 315.0 us)
where the time goes:
time: 360 us; the launch traced here: 356 us
  local copies, waits for them, and re-layouts  116 us (32%)
  blocking collectives  116 us (32%)
  starting transfers between devices  45.6 us (13%)
  other arithmetic  42.2 us (12%)
  matrix products  18 us (5%)
  waiting for transfers between devices  15.1 us (4%)
    all_gather x12, blocking collectives, prefix_by_axis(): lax.all_gather(part.astype(kind), axis)  116 us
    slice x9, local copies, waits for them, and re-layouts, causal_conv(): padded[offset:offset + row_count].astype(jnp.float32)  40.3 us
    all_to_all x1, starting transfers between devices, sum_at_owner(): lax.all_to_all(tiles, axis, split_axis=0, concat_axis=0, tiled=True)  39.6 us
    dynamic_update_slice x16, local copies, waits for them, and re-layouts, local_pass(): lax.scan(advance, start_state, (values, b_rows, c_rows, dt_blocks, ld_blo...  31.5 us
    another operation x26, other arithmetic  17 us
    all_to_all x1, waiting for transfers between devices, sum_at_owner(): lax.all_to_all(tiles, axis, split_axis=0, concat_axis=0, tiled=True)  15.1 us
    another operation x58, local copies, waits for them, and re-layouts  11.4 us
    unnamed x171, local copies, waits for them, and re-layouts  9.74 us
  transfers between devices with their start and end apart: 3, of which 1 were waited for; matrix products, arithmetic and copies ran while one was open for 21% of the time, Pallas kernels for 0%

commit v1 on v0

v1 whole, which is shorter than its diff:
```python
import functools
import math

import jax
import jax.numpy as jnp
from jax import lax
from jax.experimental import pallas as pl
from jax.experimental.pallas import tpu as pltpu
from jax.sharding import Mesh
from jax.sharding import PartitionSpec as P

BLOCK = 256
STATE = 64
HEADP = 64
REACH = 3
HALO = 8
LANES = 128
SEQ = ("seq_0", "seq_1", "seq_2")
CH = ("x_hi", "core")
EPS = 1e-05
LOG2E = math.log2(math.e)
F32 = jnp.float32
BF16 = jnp.bfloat16

VMEM = pl.BlockSpec(memory_space=pltpu.VMEM)
SMEM = pl.BlockSpec(memory_space=pltpu.SMEM)


def params():
    return pltpu.CompilerParams(vmem_limit_bytes=40 * 1024 * 1024)


def cost(flops, transcendentals, bytes_accessed):
    return pl.CostEstimate(
        flops=flops, transcendentals=transcendentals, bytes_accessed=bytes_accessed
    )


def iota(shape, dim):
    return lax.broadcasted_iota(jnp.int32, shape, dim)


def dot(a, b):
    return jnp.dot(a, b, preferred_element_type=F32)


def dot_nt(a, b):
    return lax.dot_general(a, b, (((1,), (1,)), ((), ())), preferred_element_type=F32)


def sigmoid(v):
    return 0.5 * jnp.tanh(0.5 * v) + 0.5


def flipper(n):
    return (iota((n, n), 0) + iota((n, n), 1) == n - 1).astype(BF16)


def head_row(ref, lanes):
    heads = ref.shape[0]
    lane = iota((1, lanes), 1) % heads
    row = jnp.full((1, lanes), ref[0], ref.dtype)
    for h in range(1, heads):
        row = jnp.where(lane == h, ref[h], row)
    return row


def channel_row(ref):
    heads = ref.shape[0]
    lane = iota((1, heads * HEADP), 1) // HEADP
    row = jnp.full((1, heads * HEADP), ref[0], ref.dtype)
    for h in range(1, heads):
        row = jnp.where(lane == h, ref[h], row)
    return row


def three_parts(value):
    hi = value.astype(BF16).astype(F32)
    rest = value - hi
    mid = rest.astype(BF16).astype(F32)
    low = rest - mid
    lane = iota(value.shape, 1)
    packed = jnp.where(
        lane < 16,
        hi,
        jnp.where(lane < 32, pltpu.roll(mid, 16, 1), pltpu.roll(low, 32, 1)),
    )
    return jnp.where(lane < 48, packed, 0.0).astype(BF16)


def add_parts(value):
    return value + pltpu.roll(value, LANES - 16, 1) + pltpu.roll(value, LANES - 32, 1)


def project_kernel(
    hidden_ref, zx_ref, bc_ref, dtw_ref, bias_ref, exp_ref, z_ref, xbc_ref, cols_ref, rows_ref
):
    row_count, width = hidden_ref.shape[0], hidden_ref.shape[1] // 2
    inner = zx_ref.shape[1] // 2
    forward = hidden_ref[:, :width]
    reverse = dot(hidden_ref[:, width:], flipper(width)).astype(BF16)
    raw = []
    for strand, u in enumerate((forward, reverse)):
        z_ref[strand] = dot(u, zx_ref[:, :inner]).astype(BF16)
        xbc_ref[strand, :, :inner] = dot(u, zx_ref[:, inner:]).astype(BF16)
        xbc_ref[strand, :, inner:] = dot(u, bc_ref[...]).astype(BF16)
        raw.append(dot(u, dtw_ref[...]))
    lane = iota((row_count, LANES), 1)
    bias = head_row(bias_ref, LANES)
    rate = jnp.exp2(-head_row(exp_ref, LANES).astype(F32)) * LOG2E
    v = jnp.where(lane % 8 < 4, raw[0], raw[1]) + bias
    step = jnp.maximum(v, 0.0) + jnp.log1p(jnp.exp(-jnp.abs(v)))
    parts = three_parts(-step * rate)
    down = (iota((BLOCK, BLOCK), 0) >= iota((BLOCK, BLOCK), 1)).astype(BF16)
    up = (iota((BLOCK, BLOCK), 0) <= iota((BLOCK, BLOCK), 1)).astype(BF16)
    ahead_lane = iota((BLOCK, LANES), 1) % 16 < 8
    cums, totals = [], []
    for b in range(row_count // BLOCK):
        piece = parts[b * BLOCK : (b + 1) * BLOCK]
        cum = jnp.where(ahead_lane, add_parts(dot(down, piece)), add_parts(dot(up, piece)))
        cums.append(cum)
        last = jnp.where(iota((1, LANES), 1) % 16 < 8, cum[BLOCK - 1 :], cum[:1])
        totals.append(jnp.broadcast_to(last, (BLOCK, LANES)))
    cum = jnp.concatenate(cums, axis=0)
    total = jnp.concatenate(totals, axis=0)
    cols_ref[...] = cum
    to_end = jnp.exp2(jnp.minimum(total - cum, 0.0)) * step
    source = cum - jnp.log2(step)
    packed = jnp.where(
        lane < 16,
        cum,
        jnp.where(lane < 32, pltpu.roll(source, 16, 1), pltpu.roll(to_end, 32, 1)),
    )
    rows_ref[...] = packed.T[: rows_ref.shape[0]]


def conv_kernel(
    xbc_ref,
    prev_ref,
    next_ref,
    zx_ref,
    bc_ref,
    tapx_ref,
    tapbc_ref,
    rows_ref,
    cols_ref,
    x_ref,
    b_ref,
    c_ref,
    first_ref,
    send_ref,
    pad_ref,
):
    row_count, width = xbc_ref.shape[1], zx_ref.shape[0]
    inner = zx_ref.shape[1] // 2
    edge = jnp.concatenate([prev_ref[...].astype(F32), next_ref[...].astype(F32)], axis=0)
    edge = edge.astype(BF16)
    edges = (edge[:, :width], dot(edge[:, width:], flipper(width)).astype(BF16))
    taps = jnp.concatenate([tapx_ref[...].astype(F32), tapbc_ref[...].astype(F32)], axis=1)
    groups = taps.shape[1] // LANES
    lane = iota((BLOCK, LANES), 1)
    chunk = 32
    for strand in range(2):
        u = edges[strand]
        outer = jnp.concatenate([dot(u, zx_ref[:, inner:]), dot(u, bc_ref[...])], axis=1)
        outer = outer.astype(BF16).astype(F32)
        pad_ref[strand, :HALO] = outer[:HALO]
        pad_ref[strand, HALO + row_count :] = outer[HALO:]
        pad_ref[strand, HALO : HALO + row_count] = xbc_ref[strand].astype(F32)
        for group in range(groups):
            at = slice(group * LANES, (group + 1) * LANES)
            tap = [taps[j : j + 1, at] for j in range(REACH + 1)]
            for r in range(0, row_count, chunk):
                start = r + HALO - REACH
                window = [
                    pad_ref[strand, start + k : start + k + chunk, at]
                    for k in range(2 * REACH + 1)
                ]
                for way in range(2):
                    pick = (lambda j: j) if way == 0 else (lambda j: 2 * REACH - j)
                    acc = tap[0] * window[pick(0)]
                    for j in range(1, REACH + 1):
                        acc = acc + tap[j] * window[pick(j)]
                    value = (acc * sigmoid(acc)).astype(BF16)
                    if group < groups - 1:
                        x_ref[way, strand, r : r + chunk, at] = value
                    else:
                        b_ref[way, strand, r : r + chunk, :] = value
                        swapped = pltpu.roll(value.astype(F32), LANES - STATE, 1)
                        c_ref[way, strand, r : r + chunk, :] = jnp.where(
                            lane[:chunk] < STATE, swapped, 0.0
                        ).astype(BF16)
    half = iota((STATE, LANES), 1) < HEADP
    row_half = iota((1, LANES), 1) < HEADP
    for way in range(2):
        for strand in range(2):
            sd = way * 2 + strand
            states = []
            for b in range(2):
                block = slice(b * BLOCK, (b + 1) * BLOCK)
                bt = b_ref[way, strand, block, :].astype(F32).T[:STATE]
                scaled = jnp.concatenate(
                    [
                        (bt * rows_ref[32 + sd * 4 + h : 33 + sd * 4 + h, block]).astype(BF16)
                        for h in range(4)
                    ],
                    axis=0,
                )
                full = dot(scaled, x_ref[way, strand, block, :])
                states.append(
                    jnp.concatenate(
                        [
                            jnp.where(half, full[:64, :128], full[64:128, :128]),
                            jnp.where(half, full[128:192, 128:], full[192:, 128:]),
                        ],
                        axis=1,
                    )
                )
            first, last, end = (0, 1, row_count - 1) if way == 0 else (1, 0, 0)
            factor = [
                jnp.exp2(
                    jnp.broadcast_to(rows_ref[sd * 4 + h : sd * 4 + h + 1, end : end + 1], (1, LANES))
                )
                for h in range(4)
            ]
            factor = jnp.concatenate(
                [
                    jnp.where(row_half, factor[0], factor[1]),
                    jnp.where(row_half, factor[2], factor[3]),
                ],
                axis=1,
            )
            first_ref[way, strand] = states[first]
            send_ref[:, sd * 256 : (sd + 1) * 256] = (
                factor * states[first] + states[last]
            ).astype(BF16)
    total = jnp.where(
        iota((8, LANES), 1) % 16 < 8,
        jnp.broadcast_to(cols_ref[BLOCK - 1 : BLOCK] + cols_ref[row_count - 1 :], (8, LANES)),
        jnp.broadcast_to(cols_ref[:1] + cols_ref[BLOCK : BLOCK + 1], (8, LANES)),
    )
    send_ref[:, 1024:] = jnp.broadcast_to(
        three_parts(total).astype(F32)[:1], (STATE, LANES)
    ).astype(BF16)


def scan_kernel(got_ref, out_ref):
    count = got_ref.shape[0]
    parts = got_ref[:, 1024:]
    row, col = iota((count, count), 0), iota((count, count), 1)

    def summed(mask):
        return add_parts(dot(mask.astype(BF16), parts))

    ahead_lane = iota((count, LANES), 1) % 16 < 8
    upto = jnp.where(ahead_lane, summed(row >= col), summed(row <= col))
    before = jnp.where(ahead_lane, summed(row > col), summed(row < col))
    upto_t = upto.T
    half = iota((count, LANES), 1) < HEADP
    for sd in range(4):
        seen = row > col if sd < 2 else row < col
        factors = []
        for h in range(4):
            i = sd * 4 + h
            gap = before[:, i : i + 1] - upto_t[i : i + 1, :]
            factors.append(jnp.exp2(jnp.where(seen, gap, -jnp.inf)).astype(BF16))
        full = dot(jnp.concatenate(factors, axis=0), got_ref[:, sd * 256 : (sd + 1) * 256])
        out_ref[:, sd * 256 : (sd + 1) * 256] = jnp.concatenate(
            [
                jnp.where(half, full[:count, :128], full[count : 2 * count, :128]),
                jnp.where(half, full[2 * count : 3 * count, 128:], full[3 * count :, 128:]),
            ],
            axis=1,
        ).astype(BF16)


def inside_kernel(x_ref, b_ref, c_ref, rows_ref, cols_ref, skip_ref, y_ref):
    skip = channel_row(skip_ref)
    size = 128
    low = iota((size, size), 0) >= iota((size, size), 1)
    high = iota((size, size), 0) <= iota((size, size), 1)
    half = iota((size, LANES), 1) < HEADP
    for way in range(2):
        for strand in range(2):
            sd = way * 2 + strand
            for b in range(x_ref.shape[2] // BLOCK):
                block = slice(b * BLOCK, (b + 1) * BLOCK)
                scores = dot_nt(c_ref[way, strand, block, :], b_ref[way, strand, block, :])
                for pair in range(2):
                    at = slice(pair * LANES, (pair + 1) * LANES)
                    for t in range(2):
                        here = slice(b * BLOCK + t * size, b * BLOCK + (t + 1) * size)
                        seen = [s for s in range(2) if (s <= t if way == 0 else s >= t)]
                        outs = []
                        for h in (2 * pair, 2 * pair + 1):
                            i = sd * 4 + h
                            gone = jnp.broadcast_to(cols_ref[here, i : i + 1], (size, size))
                            tiles = []
                            for s in seen:
                                there = slice(b * BLOCK + s * size, b * BLOCK + (s + 1) * size)
                                gap = gone - rows_ref[16 + i : 17 + i, there]
                                if s == t:
                                    gap = jnp.where(low if way == 0 else high, gap, -jnp.inf)
                                part = scores[t * size : (t + 1) * size, s * size : (s + 1) * size]
                                tiles.append((part * jnp.exp2(gap)).astype(BF16))
                            weights = tiles[0] if len(tiles) == 1 else jnp.concatenate(tiles, axis=1)
                            lo = b * BLOCK + seen[0] * size
                            hi = b * BLOCK + (seen[-1] + 1) * size
                            outs.append(dot(weights, x_ref[way, strand, lo:hi, at]))
                        y_ref[way, strand, here, at] = (
                            jnp.where(half, outs[0], outs[1])
                            + skip[:, at] * x_ref[way, strand, here, at].astype(F32)
                        )


def finish_kernel(
    strand_ref, y_ref, c_ref, ahead_ref, behind_ref, first_ref, cols_ref, z_ref, gain_ref, out_ref
):
    strand = strand_ref[0]
    inner = z_ref.shape[2]
    same = (iota((inner, inner), 0) // HEADP == iota((inner, inner), 1) // HEADP).astype(BF16)
    half = iota((BLOCK, LANES), 1) < HEADP
    row_half = iota((1, LANES), 1) < HEADP
    gain = gain_ref[...]
    lane_of = iota((BLOCK, LANES), 1)
    for b in range(2):
        block = slice(b * BLOCK, (b + 1) * BLOCK)
        z = z_ref[0, block, :].astype(F32)
        gate = z * sigmoid(z)
        normed = []
        for way in range(2):
            came = (ahead_ref if way == 0 else behind_ref)[...].astype(F32)
            cols = jnp.where(
                strand == 0,
                cols_ref[...],
                pltpu.roll(cols_ref[...], LANES - 4, 1),
            ) if False else cols_ref[...]
            decay_all = jnp.exp2(cols[block])
            spread = []
            for h in range(4):
                i = way * 8 + h
                column = jnp.where(
                    strand == 0, decay_all[:, i : i + 1], decay_all[:, i + 4 : i + 5]
                )
                spread.append(jnp.broadcast_to(column, (BLOCK, LANES)))
            decay = jnp.concatenate(
                [jnp.where(half, spread[0], spread[1]), jnp.where(half, spread[2], spread[3])],
                axis=1,
            )
            if b == way:
                state = came
            else:
                edge = slice(BLOCK - 1, BLOCK) if way == 0 else slice(BLOCK, BLOCK + 1)
                total = jnp.exp2(cols[edge])
                picks = []
                for h in range(4):
                    i = way * 8 + h
                    value = jnp.where(strand == 0, total[:, i : i + 1], total[:, i + 4 : i + 5])
                    picks.append(jnp.broadcast_to(value, (1, LANES)))
                factor = jnp.concatenate(
                    [jnp.where(row_half, picks[0], picks[1]), jnp.where(row_half, picks[2], picks[3])],
                    axis=1,
                )
                state = factor * came + first_ref[way, 0]
            state = jnp.concatenate([state, jnp.zeros_like(state)], axis=0).astype(BF16)
            mixer = y_ref[way, 0, block, :] + decay * dot(c_ref[way, 0, block, :], state)
            gated = mixer * gate
            mean = dot((gated * gated).astype(BF16), same) * (1.0 / HEADP)
            normed.append(gated * lax.rsqrt(mean + EPS))
        out_ref[block, :] = ((normed[0] + normed[1]) * gain).astype(BF16)


def weights_kernel(place_ref, own_ref, other_ref, out_ref):
    rows, columns = own_ref.shape
    part = columns // 2
    source, target = iota((columns, columns), 0), iota((columns, columns), 1)
    core = place_ref[1]
    column = jnp.where(target < part, target + core * part, target - core * part)
    wanted = jnp.where(place_ref[0] == 0, column, columns - 1 - column)
    chosen = (source == wanted).astype(BF16)
    out_ref[:rows] = dot(own_ref[...], chosen).astype(BF16)
    out_ref[rows:] = dot(other_ref[...], chosen).astype(BF16)


def output_kernel(place_ref, own_ref, got_ref, w_ref, hidden_ref, keep_ref, send_ref):
    rows = own_ref.shape[1]
    part = w_ref.shape[1] // 2
    send_ref[...] = (
        dot(own_ref[...], w_ref[:rows, part:]) + dot(got_ref[...], w_ref[rows:, part:])
    ).astype(BF16)
    keep_ref[...] = (
        dot(own_ref[...], w_ref[:rows, :part])
        + dot(got_ref[...], w_ref[rows:, :part])
        + hidden_ref[...].astype(F32)
    )


def call(kernel, out_shape, specs, out_specs, estimate, scratch=()):
    return pl.pallas_call(
        kernel,
        out_shape=out_shape,
        in_specs=specs,
        out_specs=out_specs,
        scratch_shapes=scratch,
        compiler_params=params(),
        cost_estimate=estimate,
    )


def struct(shape, dtype):
    return jax.ShapeDtypeStruct(shape, dtype)


def shards(
    hidden_in,
    proj_zx,
    proj_bc,
    proj_dt,
    conv_x,
    conv_bc,
    dt_bias,
    decay_exp,
    skip_gain,
    norm_gain,
    out_proj,
):
    rows = hidden_in.shape[0]
    inner = proj_zx.shape[2]
    count = math.prod(lax.axis_size(axis) for axis in SEQ)
    rise = [(i, i + 1) for i in range(count - 1)]
    fall = [(i + 1, i) for i in range(count - 1)]
    swap = [(0, 1), (1, 0)]
    prev = lax.ppermute(hidden_in[rows - HALO :], SEQ, rise)
    following = lax.ppermute(hidden_in[:HALO], SEQ, fall)
    x_hi, core = lax.axis_index("x_hi"), lax.axis_index("core")
    place = jnp.stack([x_hi, core]).astype(jnp.int32)
    zx = proj_zx.reshape(proj_zx.shape[0], 2 * inner)
    dtw = jnp.tile(proj_dt, (1, LANES // proj_dt.shape[1]))

    z, xbc, cols, turned = call(
        project_kernel,
        (
            struct((2, rows, inner), BF16),
            struct((2, rows, inner + LANES), BF16),
            struct((rows, LANES), F32),
            struct((48, rows), F32),
        ),
        [VMEM] * 4 + [SMEM] * 2,
        (VMEM,) * 4,
        cost(2_000_000_000, 300_000, 4_000_000),
    )(hidden_in, zx, proj_bc, dtw, dt_bias, decay_exp)

    x, b, c, first, send = call(
        conv_kernel,
        (
            struct((2, 2, rows, inner), BF16),
            struct((2, 2, rows, LANES), BF16),
            struct((2, 2, rows, LANES), BF16),
            struct((2, 2, STATE, inner), F32),
            struct((STATE, 4 * inner + LANES), BF16),
        ),
        [VMEM] * 9,
        (VMEM,) * 5,
        cost(2_000_000_000, 800_000, 6_000_000),
        [pltpu.VMEM((2, rows + 2 * HALO, inner + LANES), F32)],
    )(xbc, prev, following, zx, proj_bc, conv_x, conv_bc, turned, cols)

    got = lax.all_to_all(send, SEQ, 0, 0, tiled=True)
    other_proj = lax.ppermute(out_proj, "x_hi", swap)
    y = call(
        inside_kernel,
        struct((2, 2, rows, inner), F32),
        [VMEM] * 5 + [SMEM],
        VMEM,
        cost(4_000_000_000, 2_000_000, 6_000_000),
    )(x, b, c, turned, cols, skip_gain)
    weights = call(
        weights_kernel,
        struct((2 * inner, 2 * inner), BF16),
        [SMEM, VMEM, VMEM],
        VMEM,
        cost(500_000_000, 0, 1_000_000),
    )(place, out_proj, other_proj)

    scanned = call(
        scan_kernel,
        struct((count, 4 * inner), BF16),
        [VMEM],
        VMEM,
        cost(100_000_000, 70_000, 300_000),
    )(got)
    came = lax.all_to_all(scanned, SEQ, 0, 0, tiled=True)

    gain = norm_gain.reshape(1, inner)

    def finish(strand):
        return pl.pallas_call(
            finish_kernel,
            out_shape=struct((rows, inner), BF16),
            grid_spec=pltpu.PrefetchScalarGridSpec(
                num_scalar_prefetch=1,
                grid=(1,),
                in_specs=[
                    pl.BlockSpec((2, 1, rows, inner), lambda i, s: (0, s[0], 0, 0)),
                    pl.BlockSpec((2, 1, rows, LANES), lambda i, s: (0, s[0], 0, 0)),
                    pl.BlockSpec((STATE, inner), lambda i, s: (0, s[0])),
                    pl.BlockSpec((STATE, inner), lambda i, s: (0, 2 + s[0])),
                    pl.BlockSpec((2, 1, STATE, inner), lambda i, s: (0, s[0], 0, 0)),
                    pl.BlockSpec((rows, LANES), lambda i, s: (0, 0)),
                    pl.BlockSpec((1, rows, inner), lambda i, s: (s[0], 0, 0)),
                    pl.BlockSpec((1, inner), lambda i, s: (0, 0)),
                ],
                out_specs=pl.BlockSpec((rows, inner), lambda i, s: (0, 0)),
            ),
            compiler_params=params(),
            cost_estimate=cost(1_000_000_000, 500_000, 3_000_000),
        )(strand.reshape(1).astype(jnp.int32), y, c, came, came, first, cols, z, gain)

    away = finish(1 - x_hi)
    arrived = lax.ppermute(away, "x_hi", swap)
    own = finish(x_hi)

    keep, give = pl.pallas_call(
        output_kernel,
        out_shape=(struct((rows, inner), F32), struct((rows, inner), BF16)),
        grid_spec=pltpu.PrefetchScalarGridSpec(
            num_scalar_prefetch=1,
            grid=(1,),
            in_specs=[
                pl.BlockSpec((rows, inner), lambda i, p: (0, 0)),
                pl.BlockSpec((rows, inner), lambda i, p: (0, 0)),
                pl.BlockSpec((2 * inner, 2 * inner), lambda i, p: (0, 0)),
                pl.BlockSpec((rows, inner), lambda i, p: (0, 2 * p[0] + p[1])),
            ],
            out_specs=(
                pl.BlockSpec((rows, inner), lambda i, p: (0, 0)),
                pl.BlockSpec((rows, inner), lambda i, p: (0, 0)),
            ),
        ),
        compiler_params=params(),
        cost_estimate=cost(600_000_000, 0, 2_000_000),
    )(place, own, arrived, weights, hidden_in)
    taken = lax.ppermute(give, "core", swap)
    return (keep + taken.astype(F32)).astype(BF16)


def solution(mesh):
    torus = Mesh(mesh.devices.reshape(8, 2, 4, 2, 2), SEQ + CH)
    placed = (
        P(SEQ, None),
        P(None, None, CH),
        P(),
        P(None, CH),
        P(None, CH),
        P(),
        P(CH),
        P(CH),
        P(CH),
        P(CH),
        P(CH, None),
    )
    return jax.shard_map(
        shards, mesh=torus, in_specs=placed, out_specs=P(SEQ, CH), check_vma=False
    )
```

time: 360 us -> 87.5 us (0.24)
  blocking collectives: 116 us -> 0 us
  local copies, waits for them, and re-layouts: 116 us -> 18.2 us
  other arithmetic: 42.2 us -> 2.18 us
  matrix products: 18 us -> 0 us
  Pallas kernels: 0 us -> 17.2 us
  starting transfers between devices: 45.6 us -> 35.7 us
    all_gather x12 -> x0, blocking collectives: 116 us -> none  [prefix_by_axis(): lax.all_gather(part.astype(kind), axis)]
    slice x39 -> x1, local copies, waits for them, and re-layouts: 46.8 us -> 0.74 us  [shards(): following = lax.ppermute(hidden_in[:HALO], SEQ, fall)]
    dynamic_update_slice x16 -> x0, local copies, waits for them, and re-layouts: 31.5 us -> none  [local_pass(): lax.scan(advance, start_state, (values, b_rows, c_rows, dt_blocks, ld_blo...]
    all_to_all x1 -> x2, starting transfers between devices: 39.6 us -> 19.8 us  [the longest x1 14.2 us: shards(): got = lax.all_to_all(send, SEQ, 0, 0, tiled=True)]
    dot_general x39 -> x0, matrix products: 18 us -> none  [the longest x4 5.88 us: finish(): jnp.einsum('tn,hpn->thp', c_rows.astype(jnp.float32), incoming, precision...]
    pallas_call x0 -> x8, Pallas kernels: none -> 17.2 us  [the longest x1 4.33 us: shards(): call(conv_kernel, (struct((2, 2, rows, inner), BF16), struct((2, 2, rows,...]
    another operation x26 -> x1, other arithmetic: 17 us -> 0.07 us  [shards(): place = jnp.stack([x_hi, core]).astype(jnp.int32)]
    another operation x58 -> x3, local copies, waits for them, and re-layouts: 11.4 us -> 0.88 us  [shards(): dtw = jnp.tile(proj_dt, (1, LANES // proj_dt.shape[1]))]
  transfers between devices with their start and end apart: 3 -> 7, of which waited for: 1 -> 4; matrix products, arithmetic and copies ran while one was open for 21% -> 8% of each run, Pallas kernels for 0% -> 13%
where the time goes in v1:
time: 87.5 us; the launch traced here: 86.7 us
  starting transfers between devices  35.7 us (41%)
  local copies, waits for them, and re-layouts  18.2 us (21%)
  Pallas kernels  17.2 us (20%)
  waiting for transfers between devices  13.1 us (15%)
  other arithmetic  2.18 us (2%)
    unnamed x45, local copies, waits for them, and re-layouts  16.1 us
    all_to_all x1, starting transfers between devices, shards(): got = lax.all_to_all(send, SEQ, 0, 0, tiled=True)  14.2 us
    all_to_all x1, waiting for transfers between devices, shards(): got = lax.all_to_all(send, SEQ, 0, 0, tiled=True)  7.08 us
    all_to_all x1, starting transfers between devices, shards(): came = lax.all_to_all(scanned, SEQ, 0, 0, tiled=True)  5.61 us
    ppermute x1, starting transfers between devices, shards(): taken = lax.ppermute(give, 'core', swap)  5.06 us
    pallas_call x1, Pallas kernels, shards(): call(conv_kernel, (struct((2, 2, rows, inner), BF16), struct((2, 2, rows,...  4.33 us
    all_to_all x1, waiting for transfers between devices, shards(): came = lax.all_to_all(scanned, SEQ, 0, 0, tiled=True)  4.27 us
    ppermute x1, starting transfers between devices, shards(): prev = lax.ppermute(hidden_in[rows - HALO:], SEQ, rise)  4.02 us
  transfers between devices with their start and end apart: 7, of which 4 were waited for; matrix products, arithmetic and copies ran while one was open for 8% of the time, Pallas kernels for 13%

profile of v1, /device:TPU:1, one launch (start us, length us, event | category | flops | bytes accessed | tf_op | source)
XLA Modules:
  0.0 86.7 jit_solution(13532979587598726917)
XLA Ops:
  0.0 0.7 fusion
  0.7 4.0 %collective-permute-start = (bf16[8,1024]{1,0:T(8,128)(2,1)S(1)}, bf16[8,1024]{1,0:T(8,128)(2,1)S(1)}, u32[]{:S(2)}, u32[]{:S(2)}) collective-permute-start(bf16[8,1024]{1,0:T(8,128)(2,1)S(1)} %get-tuple-element.28), channel_id=1, source_target_pairs={{0,4},{4,8},{8,12},{12,16},{16,20},{20,24},{24,28},{28,32},{32,36}... | collective-permute-start | bytes 49160 | tf_op jit(solution)/shard_map/ppermute | solution.py:433
  4.8 1.3 %collective-permute-start.1 = (bf16[8,1024]{1,0:T(8,128)(2,1)S(1)}, bf16[8,1024]{1,0:T(8,128)(2,1)S(1)}, u32[]{:S(2)}, u32[]{:S(2)}) collective-permute-start(bf16[8,1024]{1,0:T(8,128)(2,1)S(1)} %get-tuple-element.27), channel_id=1, source_target_pairs={{4,0},{8,4},{12,8},{16,12},{20,16},{24,20},{28,24},{32,28},{36,32}... | collective-permute-start | bytes 49160 | tf_op jit(solution)/shard_map/ppermute | solution.py:434
  6.1 1.1 %copy.22 = bf16[64,8,2,256]{3,1,2,0:T(8,128)(2,1)S(1)} copy(bf16[64,8,2,256]{3,2,1,0:T(2,128)(2,1)} %bitcast.27) | data formatting | bytes 1048576
  8.1 1.2 %copy-done.4 = bf16[512,1024]{1,0:T(8,128)(2,1)S(1)} copy-done((bf16[512,1024]{1,0:T(8,128)(2,1)S(1)}, bf16[512,1024]{1,0:T(8,128)(2,1)}, u32[]{:S(2)}) %copy-start.4) | copy-done | bytes 1048600
  9.3 0.9 %copy-done.6 = bf16[512,128]{1,0:T(8,128)(2,1)S(1)} copy-done((bf16[512,128]{1,0:T(8,128)(2,1)S(1)}, bf16[512,128]{1,0:T(8,128)(2,1)}, u32[]{:S(2)}) %copy-start.6) | copy-done | bytes 131096
  11.5 2.9 %shard_map.109 = (bf16[2,512,256]{2,1,0:T(8,128)(2,1)S(1)}, bf16[2,512,384]{2,1,0:T(8,128)(2,1)S(1)}, f32[512,128]{1,0:T(8,128)S(1)}, f32[48,512]{1,0:T(8,128)S(1)}) custom-call(bf16[512,1024]{1,0:T(8,128)(2,1)S(1)} %copy-done.4, bf16[512,512]{1,0:T(8,128)(2,1)S(1)} %bitcast.20, bf16[512,128]{1,0:T(8,128)(2,1)S(1)} %copy-done.6, ...), custom_call_target="tpu_custom_call" | custom-call | flops 2000000000 | bytes 4000000 | tf_op jit(solution)/shard_map/pallas_call | solution.py:440
  14.5 4.3 %shard_map.110 = (bf16[2,2,512,256]{3,2,1,0:T(8,128)(2,1)S(1)}, bf16[2,2,512,128]{3,2,1,0:T(8,128)(2,1)S(1)}, bf16[2,2,512,128]{3,2,1,0:T(8,128)(2,1)S(1)}, f32[...) custom-call(bf16[2,512,384]{2,1,0:T(8,128)(2,1)S(1)} %get-tuple-element.16.xbc_ref, ...), custom_call_target="tpu_custom_call" | custom-call | flops 2000000000 | bytes 6000000 | tf_op jit(solution)/shard_map/pallas_call | solution.py:453
  19.6 1.0 %copy-done.13 = bf16[2,2,512,256]{3,2,1,0:T(8,128)(2,1)} copy-done((bf16[2,2,512,256]{3,2,1,0:T(8,128)(2,1)}, bf16[2,2,512,256]{3,2,1,0:T(8,128)(2,1)S(1)}, u32[]{:S(2)}) %copy-start.13) | copy-done | bytes 1048600
  20.6 0.8 copy-done.15
  22.6 0.9 reshape.21
  23.5 14.2 %all-to-all-start = ((bf16[64,2,576]{2,1,0:T(2,128)(2,1)}), bf16[64,2,576]{2,1,0:T(2,128)(2,1)S(1)}, u32[]{:S(2)}, u32[]{:S(2)}) async-start(bf16[64,2,576]{2,1,0:T(2,128)(2,1)} %reshape.21), calls=%async_computation | async-start | bytes 327680 | tf_op jit(solution)/shard_map/all_to_all | solution.py:468
  37.7 2.8 %collective-permute-start.3 = (bf16[256,512]{1,0:T(8,128)(2,1)}, bf16[256,512]{1,0:T(8,128)(2,1)}, u32[]{:S(2)}, u32[]{:S(2)}) collective-permute-start(bf16[256,512]{1,0:T(8,128)(2,1)} %own_ref.1), channel_id=1, source_target_pairs={{0,2},{2,0},{1,3},{3,1},{4,6},{6,4},{5,7},{7,5},{8,10},{10,8},{9,1... | collective-permute-start | bytes 786440 | tf_op jit(solution)/shard_map/ppermute | solution.py:469
  40.5 7.1 %all-to-all-done = bf16[64,2,576]{2,1,0:T(2,128)(2,1)S(1)} async-done(((bf16[64,2,576]{2,1,0:T(2,128)(2,1)}), bf16[64,2,576]{2,1,0:T(2,128)(2,1)S(1)}, u32[]{:S(2)}, u32[]{:S(2)}) %all-to-all-start) | async-done | bytes 147488 | tf_op jit(solution)/shard_map/all_to_all | solution.py:468
  49.2 0.7 reshape.23
  50.0 5.6 %all-to-all-start.1 = ((bf16[64,2,512]{2,1,0:T(2,128)(2,1)}), bf16[64,2,512]{2,1,0:T(2,128)(2,1)}, u32[]{:S(2)}, u32[]{:S(2)}) async-start(bf16[64,2,512]{2,1,0:T(2,128)(2,1)} %reshape.23), calls=%async_computation.1 | async-start | bytes 262144 | tf_op jit(solution)/shard_map/all_to_all | solution.py:492
  55.6 1.2 %copy-done.14 = bf16[2,2,512,256]{3,2,1,0:T(8,128)(2,1)S(1)} copy-done((bf16[2,2,512,256]{3,2,1,0:T(8,128)(2,1)S(1)}, bf16[2,2,512,256]{3,2,1,0:T(8,128)(2,1)}, u32[]{:S(2)}) %copy-start.14) | copy-done | bytes 1048600
  56.8 1.0 %copy-done.16 = bf16[2,2,512,128]{3,2,1,0:T(8,128)(2,1)S(1)} copy-done((bf16[2,2,512,128]{3,2,1,0:T(8,128)(2,1)S(1)}, bf16[2,2,512,128]{3,2,1,0:T(8,128)(2,1)}, u32[]{:S(2)}) %copy-start.16) | copy-done | bytes 524312
  57.9 2.8 %shard_map.111.y_ref = f32[2,2,512,256]{3,2,1,0:T(8,128)S(1)} custom-call(bf16[2,2,512,256]{3,2,1,0:T(8,128)(2,1)S(1)} %copy-done.14, bf16[2,2,512,128]{3,2,1,0:T(8,128)(2,1)S(1)} %copy-done.16, bf16[2,2,512,128]{3,2,1,0:T(8,128)(2,1)S(1)} %get-tuple-element.21.c_ref, f32[48,512]{1,0:T(8,128)S(1)} %copy-done.18, f32[512,128]{1,0:T(8,128)S(1)} %get-tuple-element.18.cols_ref, ...), custom_call_target="tpu_custom_call" | custom-call | flops 4000000000 | bytes 6000000 | tf_op jit(solution)/shard_map/pallas_call | solution.py:470
  60.7 4.3 %all-to-all-done.1 = bf16[64,2,512]{2,1,0:T(2,128)(2,1)} async-done(((bf16[64,2,512]{2,1,0:T(2,128)(2,1)}), bf16[64,2,512]{2,1,0:T(2,128)(2,1)}, u32[]{:S(2)}, u32[]{:S(2)}) %all-to-all-start.1) | async-done | bytes 131104 | tf_op jit(solution)/shard_map/all_to_all | solution.py:492
  65.0 2.0 %reshape.24 = bf16[64,1,1024]{2,1,0:T(2,128)(2,1)} reshape(bf16[64,2,512]{2,1,0:T(2,128)(2,1)} %all-to-all-done.1) | data formatting | bytes 262144
  66.9 1.0 %copy.26 = bf16[64,1,1024]{2,0,1:T(8,128)(2,1)S(1)} copy(bf16[64,1,1024]{2,1,0:T(2,128)(2,1)} %reshape.24) | data formatting | bytes 262144
  67.9 0.9 %copy-done.1 = f32[2,2,64,256]{3,2,1,0:T(8,128)S(1)} copy-done((f32[2,2,64,256]{3,2,1,0:T(8,128)S(1)}, f32[2,2,64,256]{3,2,1,0:T(8,128)}, u32[]{:S(2)}) %copy-start.1) | copy-done | bytes 262168
  68.9 1.9 %shard_map.114 = bf16[512,256]{1,0:T(8,128)(2,1)} custom-call(s32[1]{0:T(128)} %bitcast.5.strand_ref, f32[2,2,512,256]{3,2,1,0:T(8,128)S(1)} %shard_map.111.y_ref, bf16[2,2,512,128]{3,2,1,0:T(8,128)(2,1)S(1)} %get-tuple-element.21.c_ref, bf16[64,1024]{1,0:T(8,128)(2,1)S(1)} %bitcast.16, bf16[64,1024]{1,0:T(8,128)(2,1)S(1)} %bitcast.17, ...), custom_call_target="tpu_custom_call" | custom-call | flops 1000000000 | bytes 3000000 | tf_op jit(solution)/shard_map/pallas_call | solution.py:497
  70.8 2.7 %collective-permute-start.2 = (bf16[512,256]{1,0:T(8,128)(2,1)}, bf16[512,256]{1,0:T(8,128)(2,1)}, u32[]{:S(2)}, u32[]{:S(2)}) collective-permute-start(bf16[512,256]{1,0:T(8,128)(2,1)} %shard_map.114), channel_id=1, source_target_pairs={{0,2},{2,0},{1,3},{3,1},{4,6},{6,4},{5,7},{7,5},{8,10},{10,8},{9,1... | collective-permute-start | bytes 786440 | tf_op jit(solution)/shard_map/ppermute | solution.py:520
  73.6 1.5 %shard_map.115.w_ref = bf16[512,512]{1,0:T(8,128)(2,1)S(1)} custom-call(s32[2]{0:T(128)S(1)} %pad_add_fusion.place_ref, bf16[256,512]{1,0:T(8,128)(2,1)} %own_ref.1, bf16[256,512]{1,0:T(8,128)(2,1)} %collective-permute-done.3.other_ref), custom_call_target="tpu_custom_call" | custom-call | flops 500000000 | bytes 1000000 | tf_op jit(solution)/shard_map/pallas_call | solution.py:477
  75.1 0.9 %copy-done.2 = f32[2,2,64,256]{3,2,1,0:T(8,128)S(1)} copy-done((f32[2,2,64,256]{3,2,1,0:T(8,128)S(1)}, f32[2,2,64,256]{3,2,1,0:T(8,128)}, u32[]{:S(2)}) %copy-start.2) | copy-done | bytes 262168
  76.1 1.2 %shard_map.113.own_ref = bf16[512,256]{1,0:T(8,128)(2,1)S(1)} custom-call(s32[1]{0:T(128)} %bitcast.strand_ref, f32[2,2,512,256]{3,2,1,0:T(8,128)S(1)} %shard_map.111.y_ref, bf16[2,2,512,128]{3,2,1,0:T(8,128)(2,1)S(1)} %get-tuple-element.21.c_ref, bf16[64,1024]{1,0:T(8,128)(2,1)S(1)} %bitcast.18, bf16[64,1024]{1,0:T(8,128)(2,1)S(1)} %bitcast.19, ...), custom_call_target="tpu_custom_call" | custom-call | flops 1000000000 | bytes 3000000 | tf_op jit(solution)/shard_map/pallas_call | solution.py:497
  77.8 1.9 %shard_map.116 = (f32[512,256]{1,0:T(8,128)S(1)}, bf16[512,256]{1,0:T(8,128)(2,1)S(1)}) custom-call(s32[2]{0:T(128)S(1)} %pad_add_fusion.place_ref, bf16[512,256]{1,0:T(8,128)(2,1)S(1)} %shard_map.113.own_ref, bf16[512,256]{1,0:T(8,128)(2,1)} %collective-permute-done.2.got_ref, bf16[512,512]{1,0:T(8,128)(2,1)S(1)} %shard_map.115.w_ref, ...), custom_call_target="tpu_custom_call" | custom-call | flops 600000000 | bytes 2000000 | tf_op jit(solution)/shard_map/pallas_call | solution.py:523
  79.7 5.1 %collective-permute-start.4 = (bf16[512,256]{1,0:T(8,128)(2,1)S(1)}, bf16[512,256]{1,0:T(8,128)(2,1)S(1)}, u32[]{:S(2)}, u32[]{:S(2)}) collective-permute-start(bf16[512,256]{1,0:T(8,128)(2,1)S(1)} %get-tuple-element.26), channel_id=1, source_target_pairs={{0,1},{1,0},{2,3},{3,2},{4,5},{5,4},{6,7},{7,6},{8,9},{9,8},{10,11... | collective-permute-start | bytes 786440 | tf_op jit(solution)/shard_map/ppermute | solution.py:543
  84.8 1.2 %collective-permute-done.4 = bf16[512,256]{1,0:T(8,128)(2,1)S(1)} collective-permute-done((bf16[512,256]{1,0:T(8,128)(2,1)S(1)}, bf16[512,256]{1,0:T(8,128)(2,1)S(1)}, u32[]{:S(2)}, u32[]{:S(2)}) %collective-permute-start.4) | collective-permute-done | bytes 262176 | tf_op jit(solution)/shard_map/ppermute | solution.py:543
  86.0 0.8 add_convert_fusion
  (44 shorter events, 6.4 us)
Async XLA Ops:
  0.7 13.7 %collective-permute-start = (bf16[8,1024]{1,0:T(8,128)(2,1)S(1)}, bf16[8,1024]{1,0:T(8,128)(2,1)S(1)}, u32[]{:S(2)}, u32[]{:S(2)}) collective-permute-start(bf16[8,1024]{1,0:T(8,128)(2,1)S(1)} %get-tuple-element.28), channel_id=1, source_target_pairs={{0,4},{4,8},{8,12},{12,16},{16,20},{20,24},{24,28},{28,32},{32,36}... | collective-permute-start | bytes 49160 | tf_op jit(solution)/shard_map/ppermute | solution.py:433
  4.8 9.7 %collective-permute-start.1 = (bf16[8,1024]{1,0:T(8,128)(2,1)S(1)}, bf16[8,1024]{1,0:T(8,128)(2,1)S(1)}, u32[]{:S(2)}, u32[]{:S(2)}) collective-permute-start(bf16[8,1024]{1,0:T(8,128)(2,1)S(1)} %get-tuple-element.27), channel_id=1, source_target_pairs={{4,0},{8,4},{12,8},{16,12},{20,16},{24,20},{28,24},{32,28},{36,32}... | collective-permute-start | bytes 49160 | tf_op jit(solution)/shard_map/ppermute | solution.py:434
  8.1 1.2 %copy-start.4 = (bf16[512,1024]{1,0:T(8,128)(2,1)S(1)}, bf16[512,1024]{1,0:T(8,128)(2,1)}, u32[]{:S(2)}) copy-start(bf16[512,1024]{1,0:T(8,128)(2,1)} %hidden_ref.3) | copy-start | bytes 3145732
  9.3 0.9 %copy-start.6 = (bf16[512,128]{1,0:T(8,128)(2,1)S(1)}, bf16[512,128]{1,0:T(8,128)(2,1)}, u32[]{:S(2)}) copy-start(bf16[512,128]{1,0:T(8,128)(2,1)} %bc_ref.3) | copy-start | bytes 393220
  10.2 0.7 copy-start.10
  10.9 0.7 copy-start.11
  11.5 2.9 %copy-start.7 = (bf16[512,128]{1,0:T(8,128)(2,1)S(1)}, bf16[512,128]{1,0:T(8,128)(2,1)}, u32[]{:S(2)}) copy-start(bf16[512,128]{1,0:T(8,128)(2,1)} %bc_ref.3) | copy-start | bytes 393220
  11.5 2.9 %copy-start.8 = (bf16[4,256]{1,0:T(4,128)(2,1)S(1)}, bf16[4,256]{1,0:T(4,128)(2,1)}, u32[]{:S(2)}) copy-start(bf16[4,256]{1,0:T(4,128)(2,1)} %tapx_ref.1) | copy-start | bytes 6148
  11.5 3.0 %copy-start.9 = (bf16[4,128]{1,0:T(4,128)(2,1)S(1)}, bf16[4,128]{1,0:T(4,128)(2,1)}, u32[]{:S(2)}) copy-start(bf16[4,128]{1,0:T(4,128)(2,1)} %tapbc_ref.1) | copy-start | bytes 3076
  14.4 4.4 %copy-start.17 = (f32[48,512]{1,0:T(8,128)}, f32[48,512]{1,0:T(8,128)S(1)}, u32[]{:S(2)}) copy-start(f32[48,512]{1,0:T(8,128)S(1)} %get-tuple-element.17.rows_ref) | copy-start | bytes 294916
  18.9 0.7 copy-start
  19.6 1.0 %copy-start.13 = (bf16[2,2,512,256]{3,2,1,0:T(8,128)(2,1)}, bf16[2,2,512,256]{3,2,1,0:T(8,128)(2,1)S(1)}, u32[]{:S(2)}) copy-start(bf16[2,2,512,256]{3,2,1,0:T(8,128)(2,1)S(1)} %get-tuple-element.19.x_ref) | copy-start | bytes 3145732
  20.6 0.8 copy-start.15
  21.4 34.2 %copy-start.12 = (f32[4]{0:T(128)S(1)}, f32[4]{0:T(128)}, u32[]{:S(2)}) copy-start(f32[4]{0:T(128)} %skip_ref.1) | copy-start | bytes 52
  21.4 34.2 %copy-start.18 = (f32[48,512]{1,0:T(8,128)S(1)}, f32[48,512]{1,0:T(8,128)}, u32[]{:S(2)}) copy-start(f32[48,512]{1,0:T(8,128)} %copy-done.17) | copy-start | bytes 294916
  23.5 24.1 %all-to-all-start = ((bf16[64,2,576]{2,1,0:T(2,128)(2,1)}), bf16[64,2,576]{2,1,0:T(2,128)(2,1)S(1)}, u32[]{:S(2)}, u32[]{:S(2)}) async-start(bf16[64,2,576]{2,1,0:T(2,128)(2,1)} %reshape.21), calls=%async_computation | async-start | bytes 327680 | tf_op jit(solution)/shard_map/all_to_all | solution.py:468
  37.7 35.9 %collective-permute-start.3 = (bf16[256,512]{1,0:T(8,128)(2,1)}, bf16[256,512]{1,0:T(8,128)(2,1)}, u32[]{:S(2)}, u32[]{:S(2)}) collective-permute-start(bf16[256,512]{1,0:T(8,128)(2,1)} %own_ref.1), channel_id=1, source_target_pairs={{0,2},{2,0},{1,3},{3,1},{4,6},{6,4},{5,7},{7,5},{8,10},{10,8},{9,1... | collective-permute-start | bytes 786440 | tf_op jit(solution)/shard_map/ppermute | solution.py:469
  50.0 15.0 %all-to-all-start.1 = ((bf16[64,2,512]{2,1,0:T(2,128)(2,1)}), bf16[64,2,512]{2,1,0:T(2,128)(2,1)}, u32[]{:S(2)}, u32[]{:S(2)}) async-start(bf16[64,2,512]{2,1,0:T(2,128)(2,1)} %reshape.23), calls=%async_computation.1 | async-start | bytes 262144 | tf_op jit(solution)/shard_map/all_to_all | solution.py:492
  55.6 1.2 %copy-start.14 = (bf16[2,2,512,256]{3,2,1,0:T(8,128)(2,1)S(1)}, bf16[2,2,512,256]{3,2,1,0:T(8,128)(2,1)}, u32[]{:S(2)}) copy-start(bf16[2,2,512,256]{3,2,1,0:T(8,128)(2,1)} %copy-done.13) | copy-start | bytes 3145732
  56.8 1.0 %copy-start.16 = (bf16[2,2,512,128]{3,2,1,0:T(8,128)(2,1)S(1)}, bf16[2,2,512,128]{3,2,1,0:T(8,128)(2,1)}, u32[]{:S(2)}) copy-start(bf16[2,2,512,128]{3,2,1,0:T(8,128)(2,1)} %copy-done.15) | copy-start | bytes 1572868
  57.9 10.1 %copy-start.3 = (f32[256]{0:T(256)S(1)}, f32[256]{0:T(256)}, u32[]{:S(2)}) copy-start(f32[256]{0:T(256)} %param.20) | copy-start | bytes 3076
  67.9 1.0 %copy-start.1 = (f32[2,2,64,256]{3,2,1,0:T(8,128)S(1)}, f32[2,2,64,256]{3,2,1,0:T(8,128)}, u32[]{:S(2)}) copy-start(f32[2,2,64,256]{3,2,1,0:T(8,128)} %copy-done) | copy-start | bytes 786436
  70.8 7.0 %collective-permute-start.2 = (bf16[512,256]{1,0:T(8,128)(2,1)}, bf16[512,256]{1,0:T(8,128)(2,1)}, u32[]{:S(2)}, u32[]{:S(2)}) collective-permute-start(bf16[512,256]{1,0:T(8,128)(2,1)} %shard_map.114), channel_id=1, source_target_pairs={{0,2},{2,0},{1,3},{3,1},{4,6},{6,4},{5,7},{7,5},{8,10},{10,8},{9,1... | collective-permute-start | bytes 786440 | tf_op jit(solution)/shard_map/ppermute | solution.py:520
  75.1 1.0 %copy-start.2 = (f32[2,2,64,256]{3,2,1,0:T(8,128)S(1)}, f32[2,2,64,256]{3,2,1,0:T(8,128)}, u32[]{:S(2)}) copy-start(f32[2,2,64,256]{3,2,1,0:T(8,128)} %copy-done) | copy-start | bytes 786436
  76.1 1.8 %copy-start.5 = (bf16[512,1024]{1,0:T(8,128)(2,1)S(1)}, bf16[512,1024]{1,0:T(8,128)(2,1)}, u32[]{:S(2)}) copy-start(bf16[512,1024]{1,0:T(8,128)(2,1)} %hidden_ref.3) | copy-start | bytes 3145732
  79.7 6.2 %collective-permute-start.4 = (bf16[512,256]{1,0:T(8,128)(2,1)S(1)}, bf16[512,256]{1,0:T(8,128)(2,1)S(1)}, u32[]{:S(2)}, u32[]{:S(2)}) collective-permute-start(bf16[512,256]{1,0:T(8,128)(2,1)S(1)} %get-tuple-element.26), channel_id=1, source_target_pairs={{0,1},{1,0},{2,3},{3,2},{4,5},{5,4},{6,7},{7,6},{8,9},{9,8},{10,11... | collective-permute-start | bytes 786440 | tf_op jit(solution)/shard_map/ppermute | solution.py:543

commit v2 on v0

v2 whole, which is shorter than its diff:
```python
import math

import jax
import jax.numpy as jnp
from jax import lax
from jax.experimental import pallas as pl
from jax.experimental.pallas import tpu as pltpu
from jax.sharding import Mesh
from jax.sharding import PartitionSpec as P

BLOCK = 256
STATE = 64
HEADP = 64
REACH = 3
HALO = 8
LANES = 128
SEQ = ("seq_0", "seq_1", "seq_2")
CH = ("x_hi", "core")
EPS = 1e-05
LOG2E = math.log2(math.e)
F32 = jnp.float32
BF16 = jnp.bfloat16

VMEM = pl.BlockSpec(memory_space=pltpu.VMEM)
HBM = pl.BlockSpec(memory_space=pltpu.HBM)
SMEM = pl.BlockSpec(memory_space=pltpu.SMEM)


def cost(flops, transcendentals, bytes_accessed):
    return pl.CostEstimate(
        flops=flops, transcendentals=transcendentals, bytes_accessed=bytes_accessed
    )


def struct(shape, dtype):
    return jax.ShapeDtypeStruct(shape, dtype)


def stored(shape, dtype):
    return pltpu.HBM(shape, dtype)


def lying(*arrays):
    return [pltpu.with_memory_space_constraint(array, pltpu.HBM) for array in arrays]


def start_copies(pairs, sems):
    copies = [
        pltpu.make_async_copy(source, target, sems.at[i]) for i, (source, target) in enumerate(pairs)
    ]
    for copy in copies:
        copy.start()
    return copies


def dma(n):
    return pltpu.SemaphoreType.DMA((n,))


def call(kernel, out_shape, specs, out_specs, estimate, mib=16, scratch=()):
    return pl.pallas_call(
        kernel,
        out_shape=out_shape,
        in_specs=specs,
        out_specs=out_specs,
        scratch_shapes=scratch,
        compiler_params=pltpu.CompilerParams(vmem_limit_bytes=mib * 1024 * 1024),
        cost_estimate=estimate,
    )


def iota(shape, dim):
    return lax.broadcasted_iota(jnp.int32, shape, dim)


def dot(a, b):
    return jnp.dot(a, b, preferred_element_type=F32)


def dot_nt(a, b):
    return lax.dot_general(a, b, (((1,), (1,)), ((), ())), preferred_element_type=F32)


def sigmoid(v):
    return 0.5 * jnp.tanh(0.5 * v) + 0.5


def parts_of(value):
    hi = value.astype(BF16).astype(F32)
    rest = value - hi
    mid = rest.astype(BF16).astype(F32)
    return hi, mid, rest - mid


def orient(n, strand):
    source, target = iota((n, n), 0), iota((n, n), 1)
    return (source == jnp.where(strand == 0, target, n - 1 - target)).astype(BF16)


DT_AT, TAP_AT, SMALL_AT, PACKED = 512, 520, 528, 544


def pack_kernel(
    place_ref, x_ref, dt_hbm, taps_hbm, bias_hbm, exp_hbm, skip_hbm, gain_hbm, hidden_hbm,
    pack_ref, head_ref, tail_ref,
    dt_ref, taps_ref, bias_ref, exp_ref, skip_ref, gain_ref, sems,
):
    inner, heads = x_ref.shape[1], dt_ref.shape[0]
    rows, width = hidden_hbm.shape[0], hidden_hbm.shape[1] // 2
    columns = pl.ds(pl.multiple_of(place_ref[0] * width, width), width)
    copies = start_copies(
        (
            (dt_hbm, dt_ref),
            (taps_hbm, taps_ref),
            (bias_hbm, bias_ref),
            (exp_hbm, exp_ref),
            (skip_hbm, skip_ref),
            (gain_hbm, gain_ref),
            (hidden_hbm.at[pl.ds(0, HALO), columns], head_ref),
            (hidden_hbm.at[pl.ds(rows - HALO, HALO), columns], tail_ref),
        ),
        sems,
    )
    pack_ref[:DT_AT] = x_ref[...]
    for copy in copies:
        copy.wait()
    lane = iota((1, inner), 1)
    small = jnp.zeros((1, inner), F32)
    for h in range(heads):
        for k, ref in enumerate((bias_ref, exp_ref, skip_ref)):
            value = ref[:, h : h + 1].astype(F32)
            small = jnp.where(lane == k * heads + h, jnp.broadcast_to(value, (1, inner)), small)
    packed = [dt_ref[:, :inner].astype(F32), dt_ref[:, inner:].astype(F32), taps_ref[...].astype(F32)]
    packed.append(jnp.zeros((SMALL_AT - TAP_AT - taps_ref.shape[0], inner), F32))
    packed += parts_of(small) + parts_of(gain_ref[...])
    packed.append(jnp.zeros((PACKED - SMALL_AT - 6, inner), F32))
    pack_ref[DT_AT:] = jnp.concatenate(packed, axis=0).astype(BF16)


def unpack(ref):
    tail = ref[SMALL_AT:].astype(F32)
    return tail[0:1] + tail[1:2] + tail[2:3], tail[3:4] + tail[4:5] + tail[5:6]


def column_of(smalls, at):
    row = iota((8, 1), 0)
    out = jnp.zeros((8, 1), F32)
    for g in range(2):
        for h in range(4):
            out = jnp.where(row == g * 4 + h, smalls[g][:, at + h : at + h + 1], out)
    return out


def spread(pieces, rows):
    half = iota((rows, LANES), 1) < HEADP
    wide = [jnp.broadcast_to(piece, (rows, LANES)) for piece in pieces]
    return jnp.concatenate(
        [jnp.where(half, wide[2 * q], wide[2 * q + 1]) for q in range(4)], axis=1
    )


def front_kernel(
    place_ref, hidden_ref, prev_ref, next_ref, own_ref, other_ref, bc_ref, tapbc_ref,
    u_hbm, x_hbm, b_hbm, c_hbm, cols_hbm, rows_hbm, first_hbm, gains_hbm, send_hbm,
    u_ref, x_ref, b_ref, c_ref, cols_ref, rows_ref, first_ref, gains_ref, send_ref, pad_ref, sems,
):
    copies = []

    def keep(source, target):
        copies.append(pltpu.make_async_copy(source, target, sems.at[len(copies)]))
        copies[-1].start()

    row_count, width = hidden_ref.shape[0], hidden_ref.shape[1] // 2
    inner = own_ref.shape[1]
    strand, position, count = place_ref[0], place_ref[2], place_ref[3]
    packs = (own_ref, other_ref)
    turn = orient(width, strand)
    u = dot(hidden_ref[:, pl.ds(pl.multiple_of(strand * width, width), width)], turn).astype(BF16)
    u_ref[...] = u
    keep(u_ref, u_hbm)
    before = jnp.where(position > 0, prev_ref[...].astype(F32), 0.0)
    after = jnp.where(position < count - 1, next_ref[...].astype(F32), 0.0)
    edge = dot(jnp.concatenate([before, after], axis=0).astype(BF16), turn).astype(BF16)

    raw = jnp.concatenate(
        [
            dot_nt(
                jnp.concatenate(
                    [ref[DT_AT : DT_AT + 4].astype(F32), ref[DT_AT + 4 : DT_AT + 8].astype(F32)],
                    axis=1,
                ).astype(BF16),
                u,
            )
            for ref in packs
        ],
        axis=0,
    )
    smalls, gains = zip(*[unpack(ref) for ref in packs])
    gains_ref[...] = jnp.concatenate(
        [
            jnp.concatenate(gains, axis=1),
            spread([smalls[g][:, 8 + h : 9 + h] for g in range(2) for h in range(4)], 1),
            jnp.zeros((6, 2 * inner), F32),
        ],
        axis=0,
    )
    keep(gains_ref, gains_hbm)
    v = raw + column_of(smalls, 0)
    rate = jnp.exp2(-column_of(smalls, 4)) * LOG2E
    step = jnp.maximum(v, 0.0) + jnp.log1p(jnp.exp(-jnp.abs(v)))
    parts = jnp.concatenate(parts_of(-step * rate), axis=0).astype(BF16)
    ahead = (iota((BLOCK, BLOCK), 0) <= iota((BLOCK, BLOCK), 1)).astype(BF16)
    behind = (iota((BLOCK, BLOCK), 0) >= iota((BLOCK, BLOCK), 1)).astype(BF16)
    cums, ends = [], []
    for b in range(2):
        piece = parts[:, b * BLOCK : (b + 1) * BLOCK]
        both = []
        for mask in (ahead, behind):
            full = dot(piece, mask)
            both.append(full[:8] + full[8:16] + full[16:])
        cums.append(jnp.concatenate(both, axis=0))
        last = jnp.concatenate([both[0][:, BLOCK - 1 :], both[1][:, :1]], axis=0)
        ends.append(jnp.broadcast_to(last, (16, BLOCK)))
    cum = jnp.concatenate(cums, axis=1)
    end = jnp.concatenate(ends, axis=1)
    step = jnp.concatenate([step, step], axis=0)
    rows_ref[:16] = cum
    rows_ref[16:32] = cum - jnp.log2(step)
    rows_ref[32:] = jnp.exp2(jnp.minimum(end - cum, 0.0)) * step
    cols_ref[...] = jnp.concatenate([cum, jnp.zeros((LANES - 16, row_count), F32)], axis=0).T
    totals = [ends[b][:, :1] for b in range(2)]
    keep(rows_ref, rows_hbm)
    keep(cols_ref, cols_hbm)

    chunk = 32
    mains = [(u, slice(HALO, HALO + row_count)), (edge, None)]
    for piece, where in mains:
        for g in range(3):
            w = packs[g][:DT_AT] if g < 2 else bc_ref[...]
            full = dot(piece, w).astype(BF16).astype(F32)
            for k in range(w.shape[1] // LANES):
                value, at = full[:, k * LANES : (k + 1) * LANES], g * inner // LANES + k
                if where is not None:
                    pad_ref[at, where] = value
                else:
                    pad_ref[at, :HALO] = value[:HALO]
                    pad_ref[at, HALO + row_count :] = value[HALO:]
    taps = jnp.concatenate(
        [ref[TAP_AT : TAP_AT + REACH + 1].astype(F32) for ref in packs]
        + [tapbc_ref[...].astype(F32)],
        axis=1,
    )
    groups = taps.shape[1] // LANES
    low_lane = iota((chunk, LANES), 1) < STATE
    for group in range(groups):
        at = slice(group * LANES, (group + 1) * LANES)
        tap = [taps[j : j + 1, at] for j in range(REACH + 1)]
        for r in range(0, row_count, chunk):
            start = r + HALO - REACH
            window = [
                pad_ref[group, start + k : start + k + chunk] for k in range(2 * REACH + 1)
            ]
            for way in range(2):
                acc = tap[0] * window[0 if way == 0 else 2 * REACH]
                for j in range(1, REACH + 1):
                    acc = acc + tap[j] * window[j if way == 0 else 2 * REACH - j]
                value = (acc * sigmoid(acc)).astype(BF16)
                if group < groups - 1:
                    x_ref[way, r : r + chunk, at] = value
                else:
                    b_ref[way, r : r + chunk, :] = value
                    swapped = pltpu.roll(value.astype(F32), LANES - STATE, 1)
                    c_ref[way, r : r + chunk, :] = jnp.where(low_lane, swapped, 0.0).astype(BF16)

    keep(x_ref, x_hbm)
    keep(b_ref, b_hbm)
    keep(c_ref, c_hbm)

    half = iota((STATE, LANES), 1) < HEADP
    row8 = iota((8, LANES), 0)
    for way in range(2):
        states = []
        for b in range(2):
            block = slice(b * BLOCK, (b + 1) * BLOCK)
            bt = b_ref[way, block, :].astype(F32).T[:STATE]
            tiles = []
            for g in range(2):
                at = 32 + way * 8 + g * 4
                scaled = jnp.concatenate(
                    [
                        (bt * rows_ref[at + h : at + h + 1, block]).astype(BF16)
                        for h in range(4)
                    ],
                    axis=0,
                )
                full = dot(scaled, x_ref[way, block, g * inner : (g + 1) * inner])
                tiles.append(jnp.where(half, full[:64, :128], full[64:128, :128]))
                tiles.append(jnp.where(half, full[128:192, 128:], full[192:, 128:]))
            states.append(tiles)
        first, last = (0, 1) if way == 0 else (1, 0)
        at = slice(way * 8, way * 8 + 8)
        last_total = jnp.exp2(totals[last][at])
        both_total = jnp.exp2(totals[0][at] + totals[1][at])
        factor = spread([last_total[i : i + 1] for i in range(8)], 1)
        whole = spread([both_total[i : i + 1] for i in range(8)], 8)
        for q in range(4):
            lanes = slice(q * LANES, (q + 1) * LANES)
            state = factor[:, lanes] * states[first][q] + states[last][q]
            first_ref[way, :, lanes] = states[first][q]
            hi, mid, low = parts_of(whole[:, lanes])
            decay = jnp.where(
                row8 == 0, hi, jnp.where(row8 == 1, mid, jnp.where(row8 == 2, low, 0.0))
            )
            for n in range(8):
                send_ref[way * 32 + n * 4 + q] = jnp.concatenate(
                    [state[n * 8 : n * 8 + 8], decay], axis=0
                ).astype(BF16)
        keep(send_ref.at[pl.ds(way * 32, 32)], send_hbm.at[pl.ds(way * 32, 32)])
    keep(first_ref, first_hbm)
    for copy in copies:
        copy.wait()


def scan_kernel(place_ref, got_ref, after_hbm, out_ref):
    count = got_ref.shape[0]
    backward = place_ref[2] >= count // 2
    state = jnp.zeros((8, LANES), F32)
    for i in range(count):
        k = jnp.where(backward, count - 1 - i, i)
        piece = got_ref[k].astype(F32)
        out_ref[k] = state.astype(BF16)
        decay = jnp.sum(piece[8:], axis=0, keepdims=True)
        state = decay * state + piece[:8]


def inside_kernel(
    x_hbm, b_hbm, c_hbm, rows_hbm, cols_hbm, gains_hbm, y_hbm,
    x_ref, b_ref, c_ref, rows_ref, cols_ref, gains_ref, y_ref, sems,
):
    copies = start_copies(
        (
            (b_hbm, b_ref),
            (c_hbm, c_ref),
            (rows_hbm, rows_ref),
            (cols_hbm, cols_ref),
            (gains_hbm, gains_ref),
            (x_hbm.at[0], x_ref.at[0]),
            (x_hbm.at[1], x_ref.at[1]),
        ),
        sems,
    )
    for copy in copies[:-1]:
        copy.wait()
    results = []
    size = 128
    low = iota((size, size), 0) >= iota((size, size), 1)
    high = iota((size, size), 0) <= iota((size, size), 1)
    half = iota((size, LANES), 1) < HEADP
    skip = gains_ref[1:2]
    for way in range(2):
        if way == 1:
            copies[-1].wait()
        for b in range(2):
            block = slice(b * BLOCK, (b + 1) * BLOCK)
            scores = dot_nt(c_ref[way, block, :], b_ref[way, block, :])
            for pair in range(4):
                at = slice(pair * LANES, (pair + 1) * LANES)
                for t in range(2):
                    here = slice(b * BLOCK + t * size, b * BLOCK + (t + 1) * size)
                    seen = [s for s in range(2) if (s <= t if way == 0 else s >= t)]
                    lo = b * BLOCK + seen[0] * size
                    hi = b * BLOCK + (seen[-1] + 1) * size
                    outs = []
                    for h in (2 * pair, 2 * pair + 1):
                        i = way * 8 + h
                        gone = jnp.broadcast_to(cols_ref[here, i : i + 1], (size, size))
                        tiles = []
                        for s in seen:
                            there = slice(b * BLOCK + s * size, b * BLOCK + (s + 1) * size)
                            gap = gone - rows_ref[16 + i : 17 + i, there]
                            if s == t:
                                gap = jnp.where(low if way == 0 else high, gap, -jnp.inf)
                            part = scores[t * size : (t + 1) * size, s * size : (s + 1) * size]
                            tiles.append((part * jnp.exp2(gap)).astype(BF16))
                        weights = tiles[0] if len(tiles) == 1 else jnp.concatenate(tiles, axis=1)
                        outs.append(dot(weights, x_ref[way, lo:hi, at]))
                    y_ref[way, here, at] = (
                        jnp.where(half, outs[0], outs[1])
                        + skip[:, at] * x_ref[way, here, at].astype(F32)
                    ).astype(BF16)
            results.append(
                pltpu.make_async_copy(
                    y_ref.at[way, block, :], y_hbm.at[way, block, :], sems.at[7 + 2 * way + b]
                )
            )
            results[-1].start()
    for copy in results:
        copy.wait()


def ready_kernel(
    place_ref, u_hbm, own_z_ref, other_z_ref, own_out_ref, other_out_ref, after_hbm,
    gate_hbm, w_hbm,
    u_ref, gate_ref, w_ref, sems,
):
    loading = pltpu.make_async_copy(u_hbm, u_ref, sems.at[0])
    loading.start()
    rows, columns = own_out_ref.shape
    part = columns // 2
    source, target = iota((columns, columns), 0), iota((columns, columns), 1)
    core = place_ref[1]
    column = jnp.where(target < part, target + core * part, target - core * part)
    wanted = jnp.where(place_ref[0] == 0, column, columns - 1 - column)
    chosen = (source == wanted).astype(BF16)
    w_ref[:rows] = dot(own_out_ref[...], chosen).astype(BF16)
    w_ref[rows:] = dot(other_out_ref[...], chosen).astype(BF16)
    copies = [pltpu.make_async_copy(w_ref, w_hbm, sems.at[1])]
    copies[0].start()
    loading.wait()
    inner = own_z_ref.shape[1]
    for g, ref in enumerate((own_z_ref, other_z_ref)):
        z = dot(u_ref[...], ref[...]).astype(BF16).astype(F32)
        gate_ref[:, g * inner : (g + 1) * inner] = (z * sigmoid(z)).astype(BF16)
    copies.append(pltpu.make_async_copy(gate_ref, gate_hbm, sems.at[2]))
    copies[1].start()
    for copy in copies:
        copy.wait()


def back_kernel(
    place_ref, y_hbm, c_hbm, came_ref, first_hbm, cols_hbm, gate_hbm, gains_hbm, w_hbm, hidden_hbm,
    keep_ref, give_ref,
    y_ref, c_ref, first_ref, cols_ref, gate_ref, gains_ref, w_ref, hidden_ref, state_ref, sems,
):
    part = w_hbm.shape[1] // 2
    inner = y_hbm.shape[2] // 2
    ours = pl.multiple_of((2 * place_ref[0] + place_ref[1]) * part, part)
    blocks = [slice(b * BLOCK, (b + 1) * BLOCK) for b in range(2)]
    copies = start_copies(
        (
            (cols_hbm, cols_ref),
            (first_hbm, first_ref),
            (c_hbm, c_ref),
            (gains_hbm, gains_ref),
            (gate_hbm.at[blocks[0]], gate_ref.at[blocks[0]]),
            (y_hbm.at[:, blocks[0]], y_ref.at[:, blocks[0]]),
            (w_hbm, w_ref),
            (hidden_hbm.at[:, pl.ds(ours, part)], hidden_ref),
            (gate_hbm.at[blocks[1]], gate_ref.at[blocks[1]]),
            (y_hbm.at[:, blocks[1]], y_ref.at[:, blocks[1]]),
        ),
        sems,
    )
    same = (iota((inner, inner), 0) // HEADP == iota((inner, inner), 1) // HEADP).astype(BF16)
    for way in range(2):
        for n in range(8):
            for q in range(4):
                state_ref[way, n * 8 : n * 8 + 8, q * LANES : (q + 1) * LANES] = came_ref[
                    way * 32 + n * 4 + q
                ].astype(F32)
    for copy in copies[:4]:
        copy.wait()
    for b, block in enumerate(blocks):
        decays = jnp.exp2(cols_ref[block])
        for copy in copies[4:6] if b == 0 else copies[8:]:
            copy.wait()
        gate = gate_ref[block, :].astype(F32)
        total = None
        for way in range(2):
            state = state_ref[way]
            if b != way:
                edge = BLOCK - 1 if way == 0 else BLOCK
                passed = jnp.exp2(cols_ref[edge : edge + 1])
                factor = spread(
                    [passed[:, way * 8 + i : way * 8 + i + 1] for i in range(8)], 1
                )
                state = factor * state + first_ref[way]
            state = jnp.concatenate([state, jnp.zeros_like(state)], axis=0).astype(BF16)
            decay = spread([decays[:, way * 8 + i : way * 8 + i + 1] for i in range(8)], BLOCK)
            mixer = y_ref[way, block, :].astype(F32) + decay * dot(c_ref[way, block, :], state)
            gated = mixer * gate
            square = (gated * gated).astype(BF16)
            mean = jnp.concatenate(
                [dot(square[:, g * inner : (g + 1) * inner], same) for g in range(2)], axis=1
            ) * (1.0 / HEADP)
            normed = gated * lax.rsqrt(mean + EPS)
            total = normed if total is None else total + normed
        mixed = (total * gains_ref[0:1]).astype(BF16)
        for copy in copies[6:8] if b == 0 else ():
            copy.wait()
        give_ref[block, :] = dot(mixed, w_ref[:, part:]).astype(BF16)
        keep_ref[block, :] = dot(mixed, w_ref[:, :part]) + hidden_ref[block, :].astype(F32)


def shards(
    hidden_in,
    proj_zx,
    proj_bc,
    proj_dt,
    conv_x,
    conv_bc,
    dt_bias,
    decay_exp,
    skip_gain,
    norm_gain,
    out_proj,
):
    rows, width = hidden_in.shape[0], hidden_in.shape[1] // 2
    inner = proj_zx.shape[2]
    count = math.prod(lax.axis_size(axis) for axis in SEQ)
    rise = [(i, (i + 1) % count) for i in range(count)]
    fall = [((i + 1) % count, i) for i in range(count)]
    swap = [(0, 1), (1, 0)]
    x_hi, core = lax.axis_index("x_hi"), lax.axis_index("core")
    place = jnp.stack([x_hi, core, lax.axis_index(SEQ), jnp.int32(count)]).astype(jnp.int32)
    zx = proj_zx.reshape(width, 2 * inner)

    pack, head, tail = call(
        pack_kernel,
        (
            struct((PACKED, inner), BF16),
            struct((HALO, width), BF16),
            struct((HALO, width), BF16),
        ),
        [SMEM, VMEM] + [HBM] * 7,
        (VMEM,) * 3,
        cost(1_000_000, 0, 1_000_000),
        scratch=[
            pltpu.VMEM((4, width), BF16),
            pltpu.VMEM((REACH + 1, inner), BF16),
            pltpu.VMEM((1, 4), F32),
            pltpu.VMEM((1, 4), jnp.int32),
            pltpu.VMEM((1, 4), F32),
            pltpu.VMEM((1, inner), F32),
            dma(8),
        ],
    )(
        place,
        zx[:, inner:],
        *lying(
            proj_dt.T,
            conv_x,
            dt_bias.reshape(1, 4),
            decay_exp.reshape(1, 4),
            skip_gain.reshape(1, 4),
            norm_gain.reshape(1, inner),
            hidden_in,
        ),
    )
    beside = (("seq_1", "x_hi"), [(0, 3), (3, 0), (1, 2), (2, 1)])
    other_pack = lax.ppermute(pack, *beside)
    prev = lax.ppermute(tail, SEQ, rise)
    following = lax.ppermute(head, SEQ, fall)

    kept = (
        ((rows, width), BF16),
        ((2, rows, 2 * inner), BF16),
        ((2, rows, LANES), BF16),
        ((2, rows, LANES), BF16),
        ((rows, LANES), F32),
        ((48, rows), F32),
        ((2, STATE, 2 * inner), F32),
        ((8, 2 * inner), F32),
        ((count, 16, LANES), BF16),
    )
    own_z, own_out, prev, following = lax.optimization_barrier(
        (zx[:, :inner], out_proj, prev, following)
    )
    other_z = lax.ppermute(own_z, *beside)
    other_out = lax.ppermute(own_out, *beside)
    u, x, b, c, cols, turned, first, gains, send = call(
        front_kernel,
        tuple(stored(*k) for k in kept),
        [SMEM] + [VMEM] * 7,
        (HBM,) * 9,
        cost(8_000_000_000, 1_000_000, 24_000_000),
        scratch=[pltpu.VMEM(*k) for k in kept]
        + [pltpu.VMEM((2 * inner // LANES + 1, rows + 2 * HALO, LANES), F32), dma(10)],
    )(place, hidden_in, prev, following, pack, other_pack, proj_bc, conv_bc)

    got = lax.all_to_all(send, SEQ, 0, 0, tiled=True)
    y = call(
        inside_kernel,
        stored((2, rows, 2 * inner), BF16),
        [HBM] * 6,
        HBM,
        cost(4_000_000_000, 2_000_000, 6_000_000),
        scratch=[
            pltpu.VMEM((2, rows, 2 * inner), BF16),
            pltpu.VMEM((2, rows, LANES), BF16),
            pltpu.VMEM((2, rows, LANES), BF16),
            pltpu.VMEM((48, rows), F32),
            pltpu.VMEM((rows, LANES), F32),
            pltpu.VMEM((8, 2 * inner), F32),
            pltpu.VMEM((2, rows, 2 * inner), BF16),
            dma(11),
        ],
    )(*lying(x, b, c, turned, cols, gains))
    scanned = call(
        scan_kernel,
        struct((count, 8, LANES), BF16),
        [SMEM, VMEM, HBM],
        VMEM,
        cost(1_000_000, 0, 400_000),
    )(place, got, *lying(y))
    gate, weights = call(
        ready_kernel,
        (stored((rows, 2 * inner), BF16), stored((2 * inner, 2 * inner), BF16)),
        [SMEM, HBM] + [VMEM] * 4 + [HBM],
        (HBM, HBM),
        cost(1_000_000_000, 300_000, 3_000_000),
        scratch=[
            pltpu.VMEM((rows, width), BF16),
            pltpu.VMEM((rows, 2 * inner), BF16),
            pltpu.VMEM((2 * inner, 2 * inner), BF16),
            dma(3),
        ],
    )(place, *lying(u), own_z, other_z, own_out, other_out, *lying(scanned))
    came = lax.all_to_all(scanned, SEQ, 0, 0, tiled=True)

    keep, give = call(
        back_kernel,
        (struct((rows, inner), F32), struct((rows, inner), BF16)),
        [SMEM, HBM, HBM, VMEM] + [HBM] * 6,
        (VMEM, VMEM),
        cost(2_000_000_000, 600_000, 6_000_000),
        scratch=[
            pltpu.VMEM((2, rows, 2 * inner), BF16),
            pltpu.VMEM((2, rows, LANES), BF16),
            pltpu.VMEM((2, STATE, 2 * inner), F32),
            pltpu.VMEM((rows, LANES), F32),
            pltpu.VMEM((rows, 2 * inner), BF16),
            pltpu.VMEM((8, 2 * inner), F32),
            pltpu.VMEM((2 * inner, 2 * inner), BF16),
            pltpu.VMEM((rows, inner), BF16),
            pltpu.VMEM((2, STATE, 2 * inner), F32),
            dma(10),
        ],
    )(
        place,
        *lying(y, c),
        came,
        *lying(first, cols, gate, gains, weights, hidden_in),
    )
    taken = lax.ppermute(give, "core", swap)
    return (keep + taken.astype(F32)).astype(BF16)


def solution(mesh):
    torus = Mesh(mesh.devices.reshape(8, 2, 4, 2, 2), SEQ + CH)
    placed = (
        P(SEQ, None),
        P(None, None, CH),
        P(),
        P(None, CH),
        P(None, CH),
        P(),
        P(CH),
        P(CH),
        P(CH),
        P(CH),
        P(CH, None),
    )
    return jax.shard_map(
        shards, mesh=torus, in_specs=placed, out_specs=P(SEQ, CH), check_vma=False
    )
```

time: 360 us -> 69.8 us (0.19); the launches traced: 356 us -> 69.4 us
  blocking collectives: 116 us -> 0 us
  local copies, waits for them, and re-layouts: 116 us -> 1.18 us
  other arithmetic: 42.2 us -> 0.84 us
  Pallas kernels: 0 us -> 19.1 us
  matrix products: 18 us -> 0 us
  starting transfers between devices: 45.6 us -> 35.7 us
    all_gather x12 -> x0, blocking collectives: 116 us -> none  [prefix_by_axis(): lax.all_gather(part.astype(kind), axis)]
    slice x39 -> x1, local copies, waits for them, and re-layouts: 46.8 us -> 0.04 us  [shards(): zx[:, inner:]]
    dynamic_update_slice x16 -> x0, local copies, waits for them, and re-layouts: 31.5 us -> none  [local_pass(): lax.scan(advance, start_state, (values, b_rows, c_rows, dt_blocks, ld_blo...]
    all_to_all x1 -> x2, starting transfers between devices: 39.6 us -> 16.8 us  [the longest x1 10.6 us: shards(): got = lax.all_to_all(send, SEQ, 0, 0, tiled=True)]
    pallas_call x0 -> x6, Pallas kernels: none -> 19.1 us  [the longest x1 4.84 us: shards(): call(front_kernel, tuple((stored(*k) for k in kept)), [SMEM] + [VMEM] * 7...]
    dot_general x39 -> x0, matrix products: 18 us -> none  [the longest x4 5.88 us: finish(): jnp.einsum('tn,hpn->thp', c_rows.astype(jnp.float32), incoming, precision...]
    another operation x26 -> x1, other arithmetic: 17 us -> 0.08 us  [shards(): jnp.stack([x_hi, core, lax.axis_index(SEQ), jnp.int32(count)])]
    ppermute x2 -> x6, starting transfers between devices: 5.99 us -> 18.9 us  [the longest x1 6.39 us: shards(): following = lax.ppermute(head, SEQ, fall)]
  transfers between devices with their start and end apart: 3 -> 8, of which waited for: 1 -> 4; matrix products, arithmetic and copies ran while one was open for 21% -> 0% of each run, Pallas kernels for 0% -> 12%
where the time goes in v2:
time: 69.8 us; the launch traced here: 69.4 us
  starting transfers between devices  35.7 us (51%)
  Pallas kernels  19.1 us (27%)
  waiting for transfers between devices  12.5 us (18%)
  local copies, waits for them, and re-layouts  1.18 us (2%)
  other arithmetic  0.84 us (1%)
    all_to_all x1, starting transfers between devices, shards(): got = lax.all_to_all(send, SEQ, 0, 0, tiled=True)  10.6 us
    all_to_all x1, waiting for transfers between devices, shards(): came = lax.all_to_all(scanned, SEQ, 0, 0, tiled=True)  6.53 us
    ppermute x1, starting transfers between devices, shards(): following = lax.ppermute(head, SEQ, fall)  6.39 us
    all_to_all x1, starting transfers between devices, shards(): came = lax.all_to_all(scanned, SEQ, 0, 0, tiled=True)  6.17 us
    ppermute x1, starting transfers between devices, shards(): taken = lax.ppermute(give, 'core', swap)  5.02 us
    pallas_call x1, Pallas kernels, shards(): call(front_kernel, tuple((stored(*k) for k in kept)), [SMEM] + [VMEM] * 7...  4.84 us
    pallas_call x1, Pallas kernels, shards(): call(back_kernel, (struct((rows, inner), F32), struct((rows, inner), BF16...  4.3 us
    pallas_call x1, Pallas kernels, shards(): call(inside_kernel, stored((2, rows, 2 * inner), BF16), [HBM] * 6, HBM, c...  4.13 us
  transfers between devices with their start and end apart: 8, of which 4 were waited for; matrix products, arithmetic and copies ran while one was open for 0% of the time, Pallas kernels for 12%

profile of v2, /device:TPU:1, one launch (start us, length us, event | category | flops | bytes accessed | tf_op | source)
XLA Modules:
  0.0 69.4 jit_solution(10405866736319031739)
XLA Ops:
  0.0 1.1 %copy.12 = bf16[64,8,2,256]{3,1,2,0:T(8,128)(2,1)S(1)} copy(bf16[64,8,2,256]{3,2,1,0:T(2,128)(2,1)} %bitcast.11) | data formatting | bytes 1048576
  1.1 0.0 copy-start
  1.2 0.1 pad_add_fusion.place_ref
  1.3 0.0 copy-start.2
  1.3 1.5 %shard_map.109 = (bf16[544,256]{1,0:T(8,128)(2,1)S(1)}, bf16[8,512]{1,0:T(8,128)(2,1)S(1)}, bf16[8,512]{1,0:T(8,128)(2,1)S(1)}) custom-call(s32[4]{0:T(128)S(1)} %pad_add_fusion.place_ref, bf16[512,256]{1,0:T(8,128)(2,1)S(1)} %get-tuple-element.45.x_ref, bf16[4,512]{1,0:T(4,128)(2,1)} %bitcast.12, bf16[4,256]{1,0:T(4,128)(2,1)} %taps_hbm.1, ...), custom_call_target="tpu_custom_call" | custom-call | flops 1000000 | bytes 1000000 | tf_op jit(solution)/shard_map/pallas_call | solution.py:518
  2.8 3.4 %collective-permute-start.2 = (bf16[544,256]{1,0:T(8,128)(2,1)S(1)}, bf16[544,256]{1,0:T(8,128)(2,1)S(1)}, u32[]{:S(2)}, u32[]{:S(2)}) collective-permute-start(bf16[544,256]{1,0:T(8,128)(2,1)S(1)} %get-tuple-element.29.own_ref), channel_id=1, source_target_pairs={{0,18},{18,0},{2,16},{16,2},{1,19},{19,1},{3,17},{17,3},{4,22},{22... | collective-permute-start | bytes 835592 | tf_op jit(solution)/shard_map/ppermute | solution.py:551
  6.2 1.3 %collective-permute-start = (bf16[8,512]{1,0:T(8,128)(2,1)S(1)}, bf16[8,512]{1,0:T(8,128)(2,1)S(1)}, u32[]{:S(2)}, u32[]{:S(2)}) collective-permute-start(bf16[8,512]{1,0:T(8,128)(2,1)S(1)} %get-tuple-element.25), channel_id=1, source_target_pairs={{0,4},{4,8},{8,12},{12,16},{16,20},{20,24},{24,28},{28,32},{32,36}... | collective-permute-start | bytes 24584 | tf_op jit(solution)/shard_map/ppermute | solution.py:552
  7.5 6.4 %collective-permute-start.1 = (bf16[8,512]{1,0:T(8,128)(2,1)S(1)}, bf16[8,512]{1,0:T(8,128)(2,1)S(1)}, u32[]{:S(2)}, u32[]{:S(2)}) collective-permute-start(bf16[8,512]{1,0:T(8,128)(2,1)S(1)} %get-tuple-element.26), channel_id=1, source_target_pairs={{4,0},{8,4},{12,8},{16,12},{20,16},{24,20},{28,24},{32,28},{36,32}... | collective-permute-start | bytes 24584 | tf_op jit(solution)/shard_map/ppermute | solution.py:553
  13.9 1.0 %collective-permute-done.prev_ref = bf16[8,512]{1,0:T(8,128)(2,1)S(1)} collective-permute-done((bf16[8,512]{1,0:T(8,128)(2,1)S(1)}, bf16[8,512]{1,0:T(8,128)(2,1)S(1)}, u32[]{:S(2)}, u32[]{:S(2)}) %collective-permute-start) | collective-permute-done | bytes 8224 | tf_op jit(solution)/shard_map/ppermute | solution.py:552
  14.9 0.0 collective-permute-done.1.next_ref
  14.9 0.0 collective-permute-done.2.other_ref
  14.9 0.0 copy-done
  14.9 0.0 copy-done.2
  14.9 0.0 copy-done.3
  15.0 4.8 %shard_map.110 = (bf16[512,512]{1,0:T(8,128)(2,1)}, bf16[2,512,512]{2,1,0:T(8,128)(2,1)}, bf16[2,512,128]{2,1,0:T(8,128)(2,1)}, bf16[2,512,128]{2,1,0:T(8,128)(2...) custom-call(s32[4]{0:T(128)S(1)} %pad_add_fusion.place_ref, ...), custom_call_target="tpu_custom_call" | custom-call | flops 8000000000 | bytes 24000000 | tf_op jit(solution)/shard_map/pallas_call | solution.py:571
  19.8 0.0 copy-start.1
  19.8 10.6 %all-to-all-start = ((bf16[64,16,128]{2,1,0:T(8,128)(2,1)}), bf16[64,16,128]{2,1,0:T(8,128)(2,1)S(1)}, u32[]{:S(2)}, u32[]{:S(2)}) async-start(bf16[64,16,128]{2,1,0:T(8,128)(2,1)} %get-tuple-element.36), calls=%async_computation | async-start | bytes 524288 | tf_op jit(solution)/shard_map/all_to_all | solution.py:581
  30.4 2.2 %collective-permute-start.3 = (bf16[512,256]{1,0:T(8,128)(2,1)S(1)}, bf16[512,256]{1,0:T(8,128)(2,1)S(1)}, u32[]{:S(2)}, u32[]{:S(2)}) collective-permute-start(bf16[512,256]{1,0:T(8,128)(2,1)S(1)} %get-tuple-element.39.own_z_ref), channel_id=1, source_target_pairs={{0,18},{18,0},{2,16},{16,2},{1,19},{19,1},{3,17},{17,3},{4,22},{22... | collective-permute-start | bytes 786440 | tf_op jit(solution)/shard_map/ppermute | solution.py:569
  32.6 0.0 copy-done.1
  32.6 0.6 collective-permute-start.4
  33.2 4.1 %shard_map.111.after_hbm.y_hbm = bf16[2,512,512]{2,1,0:T(8,128)(2,1)} custom-call(bf16[2,512,512]{2,1,0:T(8,128)(2,1)} %get-tuple-element.30.x_hbm, bf16[2,512,128]{2,1,0:T(8,128)(2,1)} %get-tuple-element.31.b_hbm, bf16[2,512,128]{2,1,0:T(8,128)(2,1)} %get-tuple-element.32.c_hbm, f32[48,512]{1,0:T(8,128)} %get-tuple-element.33.rows_hbm, ...), custom_call_target="tpu_custom_call" | custom-call | flops 4000000000 | bytes 6000000 | tf_op jit(solution)/shard_map/pallas_call | solution.py:582
  37.3 3.7 %all-to-all-done.got_ref = bf16[64,16,128]{2,1,0:T(8,128)(2,1)S(1)} async-done(((bf16[64,16,128]{2,1,0:T(8,128)(2,1)}), bf16[64,16,128]{2,1,0:T(8,128)(2,1)S(1)}, u32[]{:S(2)}, u32[]{:S(2)}) %all-to-all-start) | async-done | bytes 262176 | tf_op jit(solution)/shard_map/all_to_all | solution.py:581
  41.1 1.3 %shard_map.112.after_hbm = bf16[64,8,128]{2,1,0:T(8,128)(2,1)} custom-call(s32[4]{0:T(128)S(1)} %pad_add_fusion.place_ref, bf16[64,16,128]{2,1,0:T(8,128)(2,1)S(1)} %all-to-all-done.got_ref, bf16[2,512,512]{2,1,0:T(8,128)(2,1)} %shard_map.111.after_hbm.y_hbm), custom_call_target="tpu_custom_call" | custom-call | flops 1000000 | bytes 400000 | tf_op jit(solution)/shard_map/pallas_call | solution.py:599
  42.4 6.2 %all-to-all-start.1 = ((bf16[64,8,128]{2,1,0:T(8,128)(2,1)}), bf16[64,8,128]{2,1,0:T(8,128)(2,1)S(1)}, u32[]{:S(2)}, u32[]{:S(2)}) async-start(bf16[64,8,128]{2,1,0:T(8,128)(2,1)} %shard_map.112.after_hbm), calls=%async_computation.1 | async-start | bytes 262144 | tf_op jit(solution)/shard_map/all_to_all | solution.py:619
  48.6 0.0 collective-permute-done.3.other_z_ref
  48.6 0.0 collective-permute-done.4.other_out_ref
  48.6 3.0 %shard_map.113 = (bf16[512,512]{1,0:T(8,128)(2,1)}, bf16[512,512]{1,0:T(8,128)(2,1)}) custom-call(s32[4]{0:T(128)S(1)} %pad_add_fusion.place_ref, bf16[512,512]{1,0:T(8,128)(2,1)} %get-tuple-element.38.u_hbm, bf16[512,256]{1,0:T(8,128)(2,1)S(1)} %get-tuple-element.39.own_z_ref, bf16[512,256]{1,0:T(8,128)(2,1)S(1)} %collective-permute-done.3.other_z_ref, ...), custom_call_target="tpu_custom_call" | custom-call | flops 1000000000 | bytes 3000000 | tf_op jit(solution)/shard_map/pallas_call | solution.py:606
  51.7 6.5 %all-to-all-done.1.came_ref = bf16[64,8,128]{2,1,0:T(8,128)(2,1)S(1)} async-done(((bf16[64,8,128]{2,1,0:T(8,128)(2,1)}), bf16[64,8,128]{2,1,0:T(8,128)(2,1)S(1)}, u32[]{:S(2)}, u32[]{:S(2)}) %all-to-all-start.1) | async-done | bytes 131104 | tf_op jit(solution)/shard_map/all_to_all | solution.py:619
  58.2 4.3 %shard_map.114 = (f32[512,256]{1,0:T(8,128)S(1)}, bf16[512,256]{1,0:T(8,128)(2,1)S(1)}) custom-call(s32[4]{0:T(128)S(1)} %pad_add_fusion.place_ref, bf16[2,512,512]{2,1,0:T(8,128)(2,1)} %shard_map.111.after_hbm.y_hbm, bf16[2,512,128]{2,1,0:T(8,128)(2,1)} %get-tuple-element.32.c_hbm, bf16[64,8,128]{2,1,0:T(8,128)(2,1)S(1)} %all-to-all-done.1.came_ref, ...), custom_call_target="tpu_custom_call" | custom-call | flops 2000000000 | bytes 6000000 | tf_op jit(solution)/shard_map/pallas_call | solution.py:621
  62.5 5.0 %collective-permute-start.5 = (bf16[512,256]{1,0:T(8,128)(2,1)S(1)}, bf16[512,256]{1,0:T(8,128)(2,1)S(1)}, u32[]{:S(2)}, u32[]{:S(2)}) collective-permute-start(bf16[512,256]{1,0:T(8,128)(2,1)S(1)} %get-tuple-element.44), channel_id=1, source_target_pairs={{0,1},{1,0},{2,3},{3,2},{4,5},{5,4},{6,7},{7,6},{8,9},{9,8},{10,11... | collective-permute-start | bytes 786440 | tf_op jit(solution)/shard_map/ppermute | solution.py:645
  67.5 1.2 %collective-permute-done.5 = bf16[512,256]{1,0:T(8,128)(2,1)S(1)} collective-permute-done((bf16[512,256]{1,0:T(8,128)(2,1)S(1)}, bf16[512,256]{1,0:T(8,128)(2,1)S(1)}, u32[]{:S(2)}, u32[]{:S(2)}) %collective-permute-start.5) | collective-permute-done | bytes 262176 | tf_op jit(solution)/shard_map/ppermute | solution.py:645
  68.7 0.8 %add_convert_fusion = bf16[512,256]{1,0:T(8,128)(2,1)} fusion(f32[512,256]{1,0:T(8,128)S(1)} %get-tuple-element.43, bf16[512,256]{1,0:T(8,128)(2,1)S(1)} %collective-permute-done.5), kind=kLoop, calls=%fused_computation | loop fusion | flops 393216 | bytes 1048576 | tf_op jit(solution)/shard_map/convert_element_type | solution.py:646
  (2 shorter events, 0.0 us)
Async XLA Ops:
  1.1 13.8 %copy-start = (bf16[512,1024]{1,0:T(8,128)(2,1)S(1)}, bf16[512,1024]{1,0:T(8,128)(2,1)}, u32[]{:S(2)}) copy-start(bf16[512,1024]{1,0:T(8,128)(2,1)} %hidden_hbm.3) | copy-start | bytes 3145732
  1.3 13.7 %copy-start.2 = (bf16[512,128]{1,0:T(8,128)(2,1)S(1)}, bf16[512,128]{1,0:T(8,128)(2,1)}, u32[]{:S(2)}) copy-start(bf16[512,128]{1,0:T(8,128)(2,1)} %bc_ref.1) | copy-start | bytes 393220
  2.8 12.1 %collective-permute-start.2 = (bf16[544,256]{1,0:T(8,128)(2,1)S(1)}, bf16[544,256]{1,0:T(8,128)(2,1)S(1)}, u32[]{:S(2)}, u32[]{:S(2)}) collective-permute-start(bf16[544,256]{1,0:T(8,128)(2,1)S(1)} %get-tuple-element.29.own_ref), channel_id=1, source_target_pairs={{0,18},{18,0},{2,16},{16,2},{1,19},{19,1},{3,17},{17,3},{4,22},{22... | collective-permute-start | bytes 835592 | tf_op jit(solution)/shard_map/ppermute | solution.py:551
  6.2 8.7 %collective-permute-start = (bf16[8,512]{1,0:T(8,128)(2,1)S(1)}, bf16[8,512]{1,0:T(8,128)(2,1)S(1)}, u32[]{:S(2)}, u32[]{:S(2)}) collective-permute-start(bf16[8,512]{1,0:T(8,128)(2,1)S(1)} %get-tuple-element.25), channel_id=1, source_target_pairs={{0,4},{4,8},{8,12},{12,16},{16,20},{20,24},{24,28},{28,32},{32,36}... | collective-permute-start | bytes 24584 | tf_op jit(solution)/shard_map/ppermute | solution.py:552
  7.5 7.5 %copy-start.3 = (bf16[4,128]{1,0:T(4,128)(2,1)S(1)}, bf16[4,128]{1,0:T(4,128)(2,1)}, u32[]{:S(2)}) copy-start(bf16[4,128]{1,0:T(4,128)(2,1)} %tapbc_ref.1) | copy-start | bytes 3076
  7.5 7.4 %collective-permute-start.1 = (bf16[8,512]{1,0:T(8,128)(2,1)S(1)}, bf16[8,512]{1,0:T(8,128)(2,1)S(1)}, u32[]{:S(2)}, u32[]{:S(2)}) collective-permute-start(bf16[8,512]{1,0:T(8,128)(2,1)S(1)} %get-tuple-element.26), channel_id=1, source_target_pairs={{4,0},{8,4},{12,8},{16,12},{20,16},{24,20},{28,24},{32,28},{36,32}... | collective-permute-start | bytes 24584 | tf_op jit(solution)/shard_map/ppermute | solution.py:553
  19.8 12.8 %copy-start.1 = (bf16[256,512]{1,0:T(8,128)(2,1)S(1)}, bf16[256,512]{1,0:T(8,128)(2,1)}, u32[]{:S(2)}) copy-start(bf16[256,512]{1,0:T(8,128)(2,1)} %own_out_ref) | copy-start | bytes 786436
  19.8 21.3 %all-to-all-start = ((bf16[64,16,128]{2,1,0:T(8,128)(2,1)}), bf16[64,16,128]{2,1,0:T(8,128)(2,1)S(1)}, u32[]{:S(2)}, u32[]{:S(2)}) async-start(bf16[64,16,128]{2,1,0:T(8,128)(2,1)} %get-tuple-element.36), calls=%async_computation | async-start | bytes 524288 | tf_op jit(solution)/shard_map/all_to_all | solution.py:581
  30.4 18.2 %collective-permute-start.3 = (bf16[512,256]{1,0:T(8,128)(2,1)S(1)}, bf16[512,256]{1,0:T(8,128)(2,1)S(1)}, u32[]{:S(2)}, u32[]{:S(2)}) collective-permute-start(bf16[512,256]{1,0:T(8,128)(2,1)S(1)} %get-tuple-element.39.own_z_ref), channel_id=1, source_target_pairs={{0,18},{18,0},{2,16},{16,2},{1,19},{19,1},{3,17},{17,3},{4,22},{22... | collective-permute-start | bytes 786440 | tf_op jit(solution)/shard_map/ppermute | solution.py:569
  32.6 16.0 %collective-permute-start.4 = (bf16[256,512]{1,0:T(8,128)(2,1)S(1)}, bf16[256,512]{1,0:T(8,128)(2,1)S(1)}, u32[]{:S(2)}, u32[]{:S(2)}) collective-permute-start(bf16[256,512]{1,0:T(8,128)(2,1)S(1)} %copy-done.1), channel_id=1, source_target_pairs={{0,18},{18,0},{2,16},{16,2},{1,19},{19,1},{3,17},{17,3},{4,22},{22... | collective-permute-start | bytes 786440 | tf_op jit(solution)/shard_map/ppermute | solution.py:570
  42.4 15.8 %all-to-all-start.1 = ((bf16[64,8,128]{2,1,0:T(8,128)(2,1)}), bf16[64,8,128]{2,1,0:T(8,128)(2,1)S(1)}, u32[]{:S(2)}, u32[]{:S(2)}) async-start(bf16[64,8,128]{2,1,0:T(8,128)(2,1)} %shard_map.112.after_hbm), calls=%async_computation.1 | async-start | bytes 262144 | tf_op jit(solution)/shard_map/all_to_all | solution.py:619
  62.5 6.2 %collective-permute-start.5 = (bf16[512,256]{1,0:T(8,128)(2,1)S(1)}, bf16[512,256]{1,0:T(8,128)(2,1)S(1)}, u32[]{:S(2)}, u32[]{:S(2)}) collective-permute-start(bf16[512,256]{1,0:T(8,128)(2,1)S(1)} %get-tuple-element.44), channel_id=1, source_target_pairs={{0,1},{1,0},{2,3},{3,2},{4,5},{5,4},{6,7},{7,6},{8,9},{9,8},{10,11... | collective-permute-start | bytes 786440 | tf_op jit(solution)/shard_map/ppermute | solution.py:645

commit v3 on v2

--- a/solution.py
+++ b/solution.py
@@ -34,10 +34,6 @@
 
 def struct(shape, dtype):
     return jax.ShapeDtypeStruct(shape, dtype)
-
-
-def stored(shape, dtype):
-    return pltpu.HBM(shape, dtype)
 
 
 def lying(*arrays):
@@ -161,15 +157,9 @@
 
 def front_kernel(
     place_ref, hidden_ref, prev_ref, next_ref, own_ref, other_ref, bc_ref, tapbc_ref,
-    u_hbm, x_hbm, b_hbm, c_hbm, cols_hbm, rows_hbm, first_hbm, gains_hbm, send_hbm,
-    u_ref, x_ref, b_ref, c_ref, cols_ref, rows_ref, first_ref, gains_ref, send_ref, pad_ref, sems,
+    u_ref, y_ref, c_ref, cols_ref, first_ref, gains_ref, send_ref,
+    x_ref, b_ref, rows_ref, pad_ref,
 ):
-    copies = []
-
-    def keep(source, target):
-        copies.append(pltpu.make_async_copy(source, target, sems.at[len(copies)]))
-        copies[-1].start()
-
     row_count, width = hidden_ref.shape[0], hidden_ref.shape[1] // 2
     inner = own_ref.shape[1]
     strand, position, count = place_ref[0], place_ref[2], place_ref[3]
@@ -177,7 +167,6 @@
     turn = orient(width, strand)
     u = dot(hidden_ref[:, pl.ds(pl.multiple_of(strand * width, width), width)], turn).astype(BF16)
     u_ref[...] = u
-    keep(u_ref, u_hbm)
     before = jnp.where(position > 0, prev_ref[...].astype(F32), 0.0)
     after = jnp.where(position < count - 1, next_ref[...].astype(F32), 0.0)
     edge = dot(jnp.concatenate([before, after], axis=0).astype(BF16), turn).astype(BF16)
@@ -204,7 +193,6 @@
         ],
         axis=0,
     )
-    keep(gains_ref, gains_hbm)
     v = raw + column_of(smalls, 0)
     rate = jnp.exp2(-column_of(smalls, 4)) * LOG2E
     step = jnp.maximum(v, 0.0) + jnp.log1p(jnp.exp(-jnp.abs(v)))
@@ -229,8 +217,6 @@
     rows_ref[32:] = jnp.exp2(jnp.minimum(end - cum, 0.0)) * step
     cols_ref[...] = jnp.concatenate([cum, jnp.zeros((LANES - 16, row_count), F32)], axis=0).T
     totals = [ends[b][:, :1] for b in range(2)]
-    keep(rows_ref, rows_hbm)
-    keep(cols_ref, cols_hbm)
 
     chunk = 32
     mains = [(u, slice(HALO, HALO + row_count)), (edge, None)]
@@ -272,9 +258,6 @@
                     swapped = pltpu.roll(value.astype(F32), LANES - STATE, 1)
                     c_ref[way, r : r + chunk, :] = jnp.where(low_lane, swapped, 0.0).astype(BF16)
 
-    keep(x_ref, x_hbm)
-    keep(b_ref, b_hbm)
-    keep(c_ref, c_hbm)
 
     half = iota((STATE, LANES), 1) < HEADP
     row8 = iota((8, LANES), 0)
@@ -315,13 +298,10 @@
                 send_ref[way * 32 + n * 4 + q] = jnp.concatenate(
                     [state[n * 8 : n * 8 + 8], decay], axis=0
                 ).astype(BF16)
-        keep(send_ref.at[pl.ds(way * 32, 32)], send_hbm.at[pl.ds(way * 32, 32)])
-    keep(first_ref, first_hbm)
-    for copy in copies:
-        copy.wait()
-
-
-def scan_kernel(place_ref, got_ref, after_hbm, out_ref):
+    inside(x_ref, b_ref, c_ref, rows_ref, cols_ref, gains_ref, y_ref)
+
+
+def scan_kernel(place_ref, got_ref, out_ref):
     count = got_ref.shape[0]
     backward = place_ref[2] >= count // 2
     state = jnp.zeros((8, LANES), F32)
@@ -333,33 +313,13 @@
         state = decay * state + piece[:8]
 
 
-def inside_kernel(
-    x_hbm, b_hbm, c_hbm, rows_hbm, cols_hbm, gains_hbm, y_hbm,
-    x_ref, b_ref, c_ref, rows_ref, cols_ref, gains_ref, y_ref, sems,
-):
-    copies = start_copies(
-        (
-            (b_hbm, b_ref),
-            (c_hbm, c_ref),
-            (rows_hbm, rows_ref),
-            (cols_hbm, cols_ref),
-            (gains_hbm, gains_ref),
-            (x_hbm.at[0], x_ref.at[0]),
-            (x_hbm.at[1], x_ref.at[1]),
-        ),
-        sems,
-    )
-    for copy in copies[:-1]:
-        copy.wait()
-    results = []
+def inside(x_ref, b_ref, c_ref, rows_ref, cols_ref, gains_ref, y_ref):
     size = 128
     low = iota((size, size), 0) >= iota((size, size), 1)
     high = iota((size, size), 0) <= iota((size, size), 1)
     half = iota((size, LANES), 1) < HEADP
     skip = gains_ref[1:2]
     for way in range(2):
-        if way == 1:
-            copies[-1].wait()
         for b in range(2):
             block = slice(b * BLOCK, (b + 1) * BLOCK)
             scores = dot_nt(c_ref[way, block, :], b_ref[way, block, :])
@@ -387,24 +347,12 @@
                     y_ref[way, here, at] = (
                         jnp.where(half, outs[0], outs[1])
                         + skip[:, at] * x_ref[way, here, at].astype(F32)
-                    ).astype(BF16)
-            results.append(
-                pltpu.make_async_copy(
-                    y_ref.at[way, block, :], y_hbm.at[way, block, :], sems.at[7 + 2 * way + b]
-                )
-            )
-            results[-1].start()
-    for copy in results:
-        copy.wait()
+                    )
 
 
 def ready_kernel(
-    place_ref, u_hbm, own_z_ref, other_z_ref, own_out_ref, other_out_ref, after_hbm,
-    gate_hbm, w_hbm,
-    u_ref, gate_ref, w_ref, sems,
+    place_ref, u_ref, own_z_ref, other_z_ref, own_out_ref, other_out_ref, gate_ref, w_ref
 ):
-    loading = pltpu.make_async_copy(u_hbm, u_ref, sems.at[0])
-    loading.start()
     rows, columns = own_out_ref.shape
     part = columns // 2
     source, target = iota((columns, columns), 0), iota((columns, columns), 1)
@@ -414,43 +362,20 @@
     chosen = (source == wanted).astype(BF16)
     w_ref[:rows] = dot(own_out_ref[...], chosen).astype(BF16)
     w_ref[rows:] = dot(other_out_ref[...], chosen).astype(BF16)
-    copies = [pltpu.make_async_copy(w_ref, w_hbm, sems.at[1])]
-    copies[0].start()
-    loading.wait()
     inner = own_z_ref.shape[1]
     for g, ref in enumerate((own_z_ref, other_z_ref)):
         z = dot(u_ref[...], ref[...]).astype(BF16).astype(F32)
-        gate_ref[:, g * inner : (g + 1) * inner] = (z * sigmoid(z)).astype(BF16)
-    copies.append(pltpu.make_async_copy(gate_ref, gate_hbm, sems.at[2]))
-    copies[1].start()
-    for copy in copies:
-        copy.wait()
+        gate_ref[:, g * inner : (g + 1) * inner] = z * sigmoid(z)
 
 
 def back_kernel(
-    place_ref, y_hbm, c_hbm, came_ref, first_hbm, cols_hbm, gate_hbm, gains_hbm, w_hbm, hidden_hbm,
-    keep_ref, give_ref,
-    y_ref, c_ref, first_ref, cols_ref, gate_ref, gains_ref, w_ref, hidden_ref, state_ref, sems,
+    place_ref, y_ref, c_ref, came_ref, first_ref, cols_ref, gate_ref, gains_ref, w_ref, hidden_ref,
+    keep_ref, give_ref, state_ref,
 ):
-    part = w_hbm.shape[1] // 2
-    inner = y_hbm.shape[2] // 2
+    part = w_ref.shape[1] // 2
+    inner = y_ref.shape[2] // 2
     ours = pl.multiple_of((2 * place_ref[0] + place_ref[1]) * part, part)
     blocks = [slice(b * BLOCK, (b + 1) * BLOCK) for b in range(2)]
-    copies = start_copies(
-        (
-            (cols_hbm, cols_ref),
-            (first_hbm, first_ref),
-            (c_hbm, c_ref),
-            (gains_hbm, gains_ref),
-            (gate_hbm.at[blocks[0]], gate_ref.at[blocks[0]]),
-            (y_hbm.at[:, blocks[0]], y_ref.at[:, blocks[0]]),
-            (w_hbm, w_ref),
-            (hidden_hbm.at[:, pl.ds(ours, part)], hidden_ref),
-            (gate_hbm.at[blocks[1]], gate_ref.at[blocks[1]]),
-            (y_hbm.at[:, blocks[1]], y_ref.at[:, blocks[1]]),
-        ),
-        sems,
-    )
     same = (iota((inner, inner), 0) // HEADP == iota((inner, inner), 1) // HEADP).astype(BF16)
     for way in range(2):
         for n in range(8):
@@ -458,13 +383,9 @@
                 state_ref[way, n * 8 : n * 8 + 8, q * LANES : (q + 1) * LANES] = came_ref[
                     way * 32 + n * 4 + q
                 ].astype(F32)
-    for copy in copies[:4]:
-        copy.wait()
     for b, block in enumerate(blocks):
         decays = jnp.exp2(cols_ref[block])
-        for copy in copies[4:6] if b == 0 else copies[8:]:
-            copy.wait()
-        gate = gate_ref[block, :].astype(F32)
+        gate = gate_ref[block, :]
         total = None
         for way in range(2):
             state = state_ref[way]
@@ -477,7 +398,7 @@
                 state = factor * state + first_ref[way]
             state = jnp.concatenate([state, jnp.zeros_like(state)], axis=0).astype(BF16)
             decay = spread([decays[:, way * 8 + i : way * 8 + i + 1] for i in range(8)], BLOCK)
-            mixer = y_ref[way, block, :].astype(F32) + decay * dot(c_ref[way, block, :], state)
+            mixer = y_ref[way, block, :] + decay * dot(c_ref[way, block, :], state)
             gated = mixer * gate
             square = (gated * gated).astype(BF16)
             mean = jnp.concatenate(
@@ -486,10 +407,10 @@
             normed = gated * lax.rsqrt(mean + EPS)
             total = normed if total is None else total + normed
         mixed = (total * gains_ref[0:1]).astype(BF16)
-        for copy in copies[6:8] if b == 0 else ():
-            copy.wait()
         give_ref[block, :] = dot(mixed, w_ref[:, part:]).astype(BF16)
-        keep_ref[block, :] = dot(mixed, w_ref[:, :part]) + hidden_ref[block, :].astype(F32)
+        keep_ref[block, :] = dot(mixed, w_ref[:, :part]) + hidden_ref[
+            block, pl.ds(ours, part)
+        ].astype(F32)
 
 
 def shards(
@@ -552,96 +473,59 @@
     prev = lax.ppermute(tail, SEQ, rise)
     following = lax.ppermute(head, SEQ, fall)
 
-    kept = (
-        ((rows, width), BF16),
-        ((2, rows, 2 * inner), BF16),
-        ((2, rows, LANES), BF16),
-        ((2, rows, LANES), BF16),
-        ((rows, LANES), F32),
-        ((48, rows), F32),
-        ((2, STATE, 2 * inner), F32),
-        ((8, 2 * inner), F32),
-        ((count, 16, LANES), BF16),
-    )
     own_z, own_out, prev, following = lax.optimization_barrier(
         (zx[:, :inner], out_proj, prev, following)
     )
     other_z = lax.ppermute(own_z, *beside)
     other_out = lax.ppermute(own_out, *beside)
-    u, x, b, c, cols, turned, first, gains, send = call(
+    u, y, c, cols, first, gains, send = call(
         front_kernel,
-        tuple(stored(*k) for k in kept),
+        (
+            struct((rows, width), BF16),
+            struct((2, rows, 2 * inner), F32),
+            struct((2, rows, LANES), BF16),
+            struct((rows, LANES), F32),
+            struct((2, STATE, 2 * inner), F32),
+            struct((8, 2 * inner), F32),
+            struct((count, 16, LANES), BF16),
+        ),
         [SMEM] + [VMEM] * 7,
-        (HBM,) * 9,
-        cost(8_000_000_000, 1_000_000, 24_000_000),
-        scratch=[pltpu.VMEM(*k) for k in kept]
-        + [pltpu.VMEM((2 * inner // LANES + 1, rows + 2 * HALO, LANES), F32), dma(10)],
-    )(place, hidden_in, prev, following, pack, other_pack, proj_bc, conv_bc)
-
-    got = lax.all_to_all(send, SEQ, 0, 0, tiled=True)
-    y = call(
-        inside_kernel,
-        stored((2, rows, 2 * inner), BF16),
-        [HBM] * 6,
-        HBM,
-        cost(4_000_000_000, 2_000_000, 6_000_000),
+        (VMEM,) * 7,
+        cost(8_000_000_000, 3_000_000, 24_000_000),
         scratch=[
             pltpu.VMEM((2, rows, 2 * inner), BF16),
             pltpu.VMEM((2, rows, LANES), BF16),
-            pltpu.VMEM((2, rows, LANES), BF16),
             pltpu.VMEM((48, rows), F32),
-            pltpu.VMEM((rows, LANES), F32),
-            pltpu.VMEM((8, 2 * inner), F32),
-            pltpu.VMEM((2, rows, 2 * inner), BF16),
-            dma(11),
+            pltpu.VMEM((2 * inner // LANES + 1, rows + 2 * HALO, LANES), F32),
         ],
-    )(*lying(x, b, c, turned, cols, gains))
+    )(place, hidden_in, prev, following, pack, other_pack, proj_bc, conv_bc)
+    gate, weights = call(
+        ready_kernel,
+        (struct((rows, 2 * inner), F32), struct((2 * inner, 2 * inner), BF16)),
+        [SMEM] + [VMEM] * 5,
+        (VMEM, VMEM),
+        cost(1_000_000_000, 300_000, 3_000_000),
+    )(place, u, own_z, other_z, own_out, other_out)
+
+    send, gate, weights = lax.optimization_barrier((send, gate, weights))
+    got = lax.all_to_all(send, SEQ, 0, 0, tiled=True)
     scanned = call(
         scan_kernel,
         struct((count, 8, LANES), BF16),
-        [SMEM, VMEM, HBM],
+        [SMEM, VMEM],
         VMEM,
         cost(1_000_000, 0, 400_000),
-    )(place, got, *lying(y))
-    gate, weights = call(
-        ready_kernel,
-        (stored((rows, 2 * inner), BF16), stored((2 * inner, 2 * inner), BF16)),
-        [SMEM, HBM] + [VMEM] * 4 + [HBM],
-        (HBM, HBM),
-        cost(1_000_000_000, 300_000, 3_000_000),
-        scratch=[
-            pltpu.VMEM((rows, width), BF16),
-            pltpu.VMEM((rows, 2 * inner), BF16),
-            pltpu.VMEM((2 * inner, 2 * inner), BF16),
-            dma(3),
-        ],
-    )(place, *lying(u), own_z, other_z, own_out, other_out, *lying(scanned))
+    )(place, got)
     came = lax.all_to_all(scanned, SEQ, 0, 0, tiled=True)
 
     keep, give = call(
         back_kernel,
         (struct((rows, inner), F32), struct((rows, inner), BF16)),
-        [SMEM, HBM, HBM, VMEM] + [HBM] * 6,
+        [SMEM] + [VMEM] * 9,
         (VMEM, VMEM),
         cost(2_000_000_000, 600_000, 6_000_000),
-        scratch=[
-            pltpu.VMEM((2, rows, 2 * inner), BF16),
-            pltpu.VMEM((2, rows, LANES), BF16),
-            pltpu.VMEM((2, STATE, 2 * inner), F32),
-            pltpu.VMEM((rows, LANES), F32),
-            pltpu.VMEM((rows, 2 * inner), BF16),
-            pltpu.VMEM((8, 2 * inner), F32),
-            pltpu.VMEM((2 * inner, 2 * inner), BF16),
-            pltpu.VMEM((rows, inner), BF16),
-            pltpu.VMEM((2, STATE, 2 * inner), F32),
-            dma(10),
-        ],
-    )(
-        place,
-        *lying(y, c),
-        came,
-        *lying(first, cols, gate, gains, weights, hidden_in),
-    )
+        scratch=[pltpu.VMEM((2, STATE, 2 * inner), F32)],
+    )(place, y, c, came, first, cols, gate, gains, weights, hidden_in)
     taken = lax.ppermute(give, "core", swap)
     return (keep + taken.astype(F32)).astype(BF16)
 

time: 69.8 us -> 74 us (1.060)
  blocking collectives: 0 us -> 33.4 us
  starting transfers between devices: 35.7 us -> 19.7 us
  Pallas kernels: 19.1 us -> 11.7 us
  waiting for transfers between devices: 12.5 us -> 6.69 us
    all_to_all x0 -> x2, blocking collectives: none -> 33.4 us  [the longest x1 19.2 us: shards(): got = lax.all_to_all(send, SEQ, 0, 0, tiled=True)]
    all_to_all x2 -> x0, starting transfers between devices: 16.8 us -> none  [the longest x1 10.6 us: shards(): got = lax.all_to_all(send, SEQ, 0, 0, tiled=True)]
    all_to_all x2 -> x0, waiting for transfers between devices: 10.3 us -> none  [the longest x1 6.53 us: shards(): came = lax.all_to_all(scanned, SEQ, 0, 0, tiled=True)]
    pallas_call x4 -> x3, Pallas kernels: 13.3 us -> 7.68 us  [the longest x1 5.6 us: shards(): call(front_kernel, (struct((rows, width), BF16), struct((2, rows, 2 * inn...]
    ppermute x1, waiting for transfers between devices: 0.01 us -> 4.48 us  [shards(): other_out = lax.ppermute(own_out, *beside)]
    ppermute x1, starting transfers between devices: 2.15 us -> 0.01 us  [shards(): other_z = lax.ppermute(own_z, *beside)]
    ppermute x1, starting transfers between devices: 0.61 us -> 2.67 us  [shards(): other_out = lax.ppermute(own_out, *beside)]
    pallas_call x1, Pallas kernels: 4.3 us -> 2.51 us  [shards(): call(back_kernel, (struct((rows, inner), F32), struct((rows, inner), BF16...]
  transfers between devices with their start and end apart: 8 -> 6, of which waited for: 4 -> 3; matrix products, arithmetic and copies ran while one was open for 0% -> 0% of each run, Pallas kernels for 12% -> 8%
where the time goes in v3:
time: 74 us; the launch traced here: 73.8 us
  blocking collectives  33.4 us (45%)
  starting transfers between devices  19.7 us (27%)
  Pallas kernels  11.7 us (16%)
  waiting for transfers between devices  6.69 us (9%)
  local copies, waits for them, and re-layouts  1.28 us (2%)
  other arithmetic  0.84 us (1%)
    all_to_all x1, blocking collectives, shards(): got = lax.all_to_all(send, SEQ, 0, 0, tiled=True)  19.2 us
    all_to_all x1, blocking collectives, shards(): came = lax.all_to_all(scanned, SEQ, 0, 0, tiled=True)  14.2 us
    ppermute x1, starting transfers between devices, shards(): following = lax.ppermute(head, SEQ, fall)  6.39 us
    ppermute x1, starting transfers between devices, shards(): taken = lax.ppermute(give, 'core', swap)  5.96 us
    pallas_call x1, Pallas kernels, shards(): call(front_kernel, (struct((rows, width), BF16), struct((2, rows, 2 * inn...  5.6 us
    ppermute x1, waiting for transfers between devices, shards(): other_out = lax.ppermute(own_out, *beside)  4.48 us
    ppermute x1, starting transfers between devices, shards(): other_pack = lax.ppermute(pack, *beside)  3.39 us
    ppermute x1, starting transfers between devices, shards(): other_out = lax.ppermute(own_out, *beside)  2.67 us
  transfers between devices with their start and end apart: 6, of which 3 were waited for; matrix products, arithmetic and copies ran while one was open for 0% of the time, Pallas kernels for 8%

profile of v3, /device:TPU:1, one launch (start us, length us, event | category | flops | bytes accessed | tf_op | source)
XLA Modules:
  0.0 73.8 jit_solution(8730121915927175480)
XLA Ops:
  0.0 0.0 copy-start
  0.0 0.0 copy-start.1
  0.0 0.0 copy-start.3
  0.0 0.0 copy-start.2
  0.0 1.2 %copy.12 = bf16[64,8,2,256]{3,1,2,0:T(8,128)(2,1)S(1)} copy(bf16[64,8,2,256]{3,2,1,0:T(2,128)(2,1)} %bitcast.11) | data formatting | bytes 1048576
  1.3 0.1 pad_add_fusion.place_ref
  1.4 1.5 %shard_map.109 = (bf16[544,256]{1,0:T(8,128)(2,1)S(1)}, bf16[8,512]{1,0:T(8,128)(2,1)S(1)}, bf16[8,512]{1,0:T(8,128)(2,1)S(1)}) custom-call(s32[4]{0:T(128)S(1)} %pad_add_fusion.place_ref, bf16[512,256]{1,0:T(8,128)(2,1)S(1)} %get-tuple-element.47.x_ref, bf16[4,512]{1,0:T(4,128)(2,1)} %bitcast.12, bf16[4,256]{1,0:T(4,128)(2,1)} %taps_hbm.1, ...), custom_call_target="tpu_custom_call" | custom-call | flops 1000000 | bytes 1000000 | tf_op jit(solution)/shard_map/pallas_call | solution.py:439
  2.9 3.4 %collective-permute-start.2 = (bf16[544,256]{1,0:T(8,128)(2,1)S(1)}, bf16[544,256]{1,0:T(8,128)(2,1)S(1)}, u32[]{:S(2)}, u32[]{:S(2)}) collective-permute-start(bf16[544,256]{1,0:T(8,128)(2,1)S(1)} %get-tuple-element.30.own_ref), channel_id=1, source_target_pairs={{0,18},{18,0},{2,16},{16,2},{1,19},{19,1},{3,17},{17,3},{4,22},{22... | collective-permute-start | bytes 835592 | tf_op jit(solution)/shard_map/ppermute | solution.py:472
  6.3 1.3 %collective-permute-start = (bf16[8,512]{1,0:T(8,128)(2,1)S(1)}, bf16[8,512]{1,0:T(8,128)(2,1)S(1)}, u32[]{:S(2)}, u32[]{:S(2)}) collective-permute-start(bf16[8,512]{1,0:T(8,128)(2,1)S(1)} %get-tuple-element.26), channel_id=1, source_target_pairs={{0,4},{4,8},{8,12},{12,16},{16,20},{20,24},{24,28},{28,32},{32,36}... | collective-permute-start | bytes 24584 | tf_op jit(solution)/shard_map/ppermute | solution.py:473
  7.6 6.4 %collective-permute-start.1 = (bf16[8,512]{1,0:T(8,128)(2,1)S(1)}, bf16[8,512]{1,0:T(8,128)(2,1)S(1)}, u32[]{:S(2)}, u32[]{:S(2)}) collective-permute-start(bf16[8,512]{1,0:T(8,128)(2,1)S(1)} %get-tuple-element.27), channel_id=1, source_target_pairs={{4,0},{8,4},{12,8},{16,12},{20,16},{24,20},{28,24},{32,28},{36,32}... | collective-permute-start | bytes 24584 | tf_op jit(solution)/shard_map/ppermute | solution.py:474
  14.0 1.0 %collective-permute-done.prev_ref = bf16[8,512]{1,0:T(8,128)(2,1)S(1)} collective-permute-done((bf16[8,512]{1,0:T(8,128)(2,1)S(1)}, bf16[8,512]{1,0:T(8,128)(2,1)S(1)}, u32[]{:S(2)}, u32[]{:S(2)}) %collective-permute-start) | collective-permute-done | bytes 8224 | tf_op jit(solution)/shard_map/ppermute | solution.py:473
  15.0 0.0 collective-permute-done.1.next_ref
  15.1 0.0 collective-permute-start.3
  15.1 0.0 copy-done.1
  15.1 2.7 %collective-permute-start.4 = (bf16[256,512]{1,0:T(8,128)(2,1)S(1)}, bf16[256,512]{1,0:T(8,128)(2,1)S(1)}, u32[]{:S(2)}, u32[]{:S(2)}) collective-permute-start(bf16[256,512]{1,0:T(8,128)(2,1)S(1)} %copy-done.1), channel_id=1, source_target_pairs={{0,18},{18,0},{2,16},{16,2},{1,19},{19,1},{3,17},{17,3},{4,22},{22... | collective-permute-start | bytes 786440 | tf_op jit(solution)/shard_map/ppermute | solution.py:480
  17.7 0.0 collective-permute-done.2.other_ref
  17.7 0.0 copy-done
  17.7 0.0 copy-done.3
  17.7 0.0 copy-done.2
  17.8 5.6 %shard_map.110 = (bf16[512,512]{1,0:T(8,128)(2,1)S(1)}, f32[2,512,512]{2,1,0:T(8,128)S(1)}, bf16[2,512,128]{2,1,0:T(8,128)(2,1)S(1)}, f32[512,128]{1,0:T(8,128)S...) custom-call(s32[4]{0:T(128)S(1)} %pad_add_fusion.place_ref, ...), custom_call_target="tpu_custom_call" | custom-call | flops 8000000000 | bytes 24000000 | tf_op jit(solution)/shard_map/pallas_call | solution.py:481
  23.4 0.0 collective-permute-done.3.other_z_ref
  23.4 4.5 %collective-permute-done.4.other_out_ref = bf16[256,512]{1,0:T(8,128)(2,1)S(1)} collective-permute-done((bf16[256,512]{1,0:T(8,128)(2,1)S(1)}, bf16[256,512]{1,0:T(8,128)(2,1)S(1)}, u32[]{:S(2)}, u32[]{:S(2)}) %collective-permute-start.4) | collective-permute-done | bytes 262176 | tf_op jit(solution)/shard_map/ppermute | solution.py:480
  27.9 1.4 %shard_map.111 = (f32[512,512]{1,0:T(8,128)S(1)}, bf16[512,512]{1,0:T(8,128)(2,1)S(1)}) custom-call(s32[4]{0:T(128)S(1)} %pad_add_fusion.place_ref, bf16[512,512]{1,0:T(8,128)(2,1)S(1)} %get-tuple-element.34.u_ref, bf16[512,256]{1,0:T(8,128)(2,1)S(1)} %get-tuple-element.35.own_z_ref, bf16[512,256]{1,0:T(8,128)(2,1)S(1)} %collective-permute-done.3.other_z_ref, ...), custom_call_target="tpu_custom_call" | custom-call | flops 1000000000 | bytes 3000000 | tf_op jit(solution)/shard_map/pallas_call | solution.py:502
  29.3 19.2 %all_to_all.10.got_ref = bf16[64,16,128]{2,1,0:T(8,128)(2,1)S(1)} all-to-all(bf16[64,16,128]{2,1,0:T(8,128)(2,1)S(1)} %get-tuple-element.39), channel_id=1, replica_groups=mesh['seq_0'=8,'seq_1'=2,'seq_2'=4,'x_hi'=2,'core'=2] {'seq_0','seq_1','..., dimensions={0} | all-to-all | bytes 524288 | tf_op jit(solution)/shard_map/all_to_all | solution.py:511
  48.5 0.7 shard_map.112
  49.2 14.2 %all_to_all.11.came_ref = bf16[64,8,128]{2,1,0:T(8,128)(2,1)S(1)} all-to-all(bf16[64,8,128]{2,1,0:T(8,128)(2,1)S(1)} %shard_map.112), channel_id=1, replica_groups=mesh['seq_0'=8,'seq_1'=2,'seq_2'=4,'x_hi'=2,'core'=2] {'seq_0','seq_1','..., dimensions={0} | all-to-all | bytes 262144 | tf_op jit(solution)/shard_map/all_to_all | solution.py:519
  63.4 2.5 %shard_map.113 = (f32[512,256]{1,0:T(8,128)S(1)}, bf16[512,256]{1,0:T(8,128)(2,1)S(1)}) custom-call(s32[4]{0:T(128)S(1)} %pad_add_fusion.place_ref, f32[2,512,512]{2,1,0:T(8,128)S(1)} %get-tuple-element.31.y_ref, bf16[2,512,128]{2,1,0:T(8,128)(2,1)S(1)} %get-tuple-element.32.c_ref, bf16[64,8,128]{2,1,0:T(8,128)(2,1)S(1)} %all_to_all.11.came_ref, ...), custom_call_target="tpu_custom_call" | custom-call | flops 2000000000 | bytes 6000000 | tf_op jit(solution)/shard_map/pallas_call | solution.py:521
  65.9 6.0 %collective-permute-start.5 = (bf16[512,256]{1,0:T(8,128)(2,1)S(1)}, bf16[512,256]{1,0:T(8,128)(2,1)S(1)}, u32[]{:S(2)}, u32[]{:S(2)}) collective-permute-start(bf16[512,256]{1,0:T(8,128)(2,1)S(1)} %get-tuple-element.46), channel_id=1, source_target_pairs={{0,1},{1,0},{2,3},{3,2},{4,5},{5,4},{6,7},{7,6},{8,9},{9,8},{10,11... | collective-permute-start | bytes 786440 | tf_op jit(solution)/shard_map/ppermute | solution.py:529
  71.9 1.2 %collective-permute-done.5 = bf16[512,256]{1,0:T(8,128)(2,1)S(1)} collective-permute-done((bf16[512,256]{1,0:T(8,128)(2,1)S(1)}, bf16[512,256]{1,0:T(8,128)(2,1)S(1)}, u32[]{:S(2)}, u32[]{:S(2)}) %collective-permute-start.5) | collective-permute-done | bytes 262176 | tf_op jit(solution)/shard_map/ppermute | solution.py:529
  73.0 0.8 %add_convert_fusion = bf16[512,256]{1,0:T(8,128)(2,1)} fusion(f32[512,256]{1,0:T(8,128)S(1)} %get-tuple-element.45, bf16[512,256]{1,0:T(8,128)(2,1)S(1)} %collective-permute-done.5), kind=kLoop, calls=%fused_computation | loop fusion | flops 393216 | bytes 1048576 | tf_op jit(solution)/shard_map/convert_element_type | solution.py:530
  (1 shorter events, 0.0 us)
Async XLA Ops:
  0.0 17.7 %copy-start = (bf16[512,1024]{1,0:T(8,128)(2,1)S(1)}, bf16[512,1024]{1,0:T(8,128)(2,1)}, u32[]{:S(2)}) copy-start(bf16[512,1024]{1,0:T(8,128)(2,1)} %hidden_ref.3) | copy-start | bytes 3145732
  0.0 15.1 %copy-start.1 = (bf16[256,512]{1,0:T(8,128)(2,1)S(1)}, bf16[256,512]{1,0:T(8,128)(2,1)}, u32[]{:S(2)}) copy-start(bf16[256,512]{1,0:T(8,128)(2,1)} %own_out_ref) | copy-start | bytes 786436
  0.0 17.7 %copy-start.3 = (bf16[4,128]{1,0:T(4,128)(2,1)S(1)}, bf16[4,128]{1,0:T(4,128)(2,1)}, u32[]{:S(2)}) copy-start(bf16[4,128]{1,0:T(4,128)(2,1)} %tapbc_ref.1) | copy-start | bytes 3076
  0.0 17.7 %copy-start.2 = (bf16[512,128]{1,0:T(8,128)(2,1)S(1)}, bf16[512,128]{1,0:T(8,128)(2,1)}, u32[]{:S(2)}) copy-start(bf16[512,128]{1,0:T(8,128)(2,1)} %bc_ref.1) | copy-start | bytes 393220
  2.9 14.8 %collective-permute-start.2 = (bf16[544,256]{1,0:T(8,128)(2,1)S(1)}, bf16[544,256]{1,0:T(8,128)(2,1)S(1)}, u32[]{:S(2)}, u32[]{:S(2)}) collective-permute-start(bf16[544,256]{1,0:T(8,128)(2,1)S(1)} %get-tuple-element.30.own_ref), channel_id=1, source_target_pairs={{0,18},{18,0},{2,16},{16,2},{1,19},{19,1},{3,17},{17,3},{4,22},{22... | collective-permute-start | bytes 835592 | tf_op jit(solution)/shard_map/ppermute | solution.py:472
  6.3 8.7 %collective-permute-start = (bf16[8,512]{1,0:T(8,128)(2,1)S(1)}, bf16[8,512]{1,0:T(8,128)(2,1)S(1)}, u32[]{:S(2)}, u32[]{:S(2)}) collective-permute-start(bf16[8,512]{1,0:T(8,128)(2,1)S(1)} %get-tuple-element.26), channel_id=1, source_target_pairs={{0,4},{4,8},{8,12},{12,16},{16,20},{20,24},{24,28},{28,32},{32,36}... | collective-permute-start | bytes 24584 | tf_op jit(solution)/shard_map/ppermute | solution.py:473
  7.6 7.4 %collective-permute-start.1 = (bf16[8,512]{1,0:T(8,128)(2,1)S(1)}, bf16[8,512]{1,0:T(8,128)(2,1)S(1)}, u32[]{:S(2)}, u32[]{:S(2)}) collective-permute-start(bf16[8,512]{1,0:T(8,128)(2,1)S(1)} %get-tuple-element.27), channel_id=1, source_target_pairs={{4,0},{8,4},{12,8},{16,12},{20,16},{24,20},{28,24},{32,28},{36,32}... | collective-permute-start | bytes 24584 | tf_op jit(solution)/shard_map/ppermute | solution.py:474
  15.1 8.3 %collective-permute-start.3 = (bf16[512,256]{1,0:T(8,128)(2,1)S(1)}, bf16[512,256]{1,0:T(8,128)(2,1)S(1)}, u32[]{:S(2)}, u32[]{:S(2)}) collective-permute-start(bf16[512,256]{1,0:T(8,128)(2,1)S(1)} %get-tuple-element.35.own_z_ref), channel_id=1, source_target_pairs={{0,18},{18,0},{2,16},{16,2},{1,19},{19,1},{3,17},{17,3},{4,22},{22... | collective-permute-start | bytes 786440 | tf_op jit(solution)/shard_map/ppermute | solution.py:479
  15.1 12.8 %collective-permute-start.4 = (bf16[256,512]{1,0:T(8,128)(2,1)S(1)}, bf16[256,512]{1,0:T(8,128)(2,1)S(1)}, u32[]{:S(2)}, u32[]{:S(2)}) collective-permute-start(bf16[256,512]{1,0:T(8,128)(2,1)S(1)} %copy-done.1), channel_id=1, source_target_pairs={{0,18},{18,0},{2,16},{16,2},{1,19},{19,1},{3,17},{17,3},{4,22},{22... | collective-permute-start | bytes 786440 | tf_op jit(solution)/shard_map/ppermute | solution.py:480
  65.9 7.1 %collective-permute-start.5 = (bf16[512,256]{1,0:T(8,128)(2,1)S(1)}, bf16[512,256]{1,0:T(8,128)(2,1)S(1)}, u32[]{:S(2)}, u32[]{:S(2)}) collective-permute-start(bf16[512,256]{1,0:T(8,128)(2,1)S(1)} %get-tuple-element.46), channel_id=1, source_target_pairs={{0,1},{1,0},{2,3},{3,2},{4,5},{5,4},{6,7},{7,6},{8,9},{9,8},{10,11... | collective-permute-start | bytes 786440 | tf_op jit(solution)/shard_map/ppermute | solution.py:529

commit v4 on v3

--- a/solution.py
+++ b/solution.py
@@ -93,15 +93,15 @@
     return (source == jnp.where(strand == 0, target, n - 1 - target)).astype(BF16)
 
 
-DT_AT, TAP_AT, SMALL_AT, PACKED = 512, 520, 528, 544
+DT_AT, TAP_AT, SMALL_AT, PACKED = 0, 8, 16, 32
 
 
 def pack_kernel(
-    place_ref, x_ref, dt_hbm, taps_hbm, bias_hbm, exp_hbm, skip_hbm, gain_hbm, hidden_hbm,
+    place_ref, dt_hbm, taps_hbm, bias_hbm, exp_hbm, skip_hbm, gain_hbm, hidden_hbm,
     pack_ref, head_ref, tail_ref,
     dt_ref, taps_ref, bias_ref, exp_ref, skip_ref, gain_ref, sems,
 ):
-    inner, heads = x_ref.shape[1], dt_ref.shape[0]
+    inner, heads = pack_ref.shape[1], dt_ref.shape[0]
     rows, width = hidden_hbm.shape[0], hidden_hbm.shape[1] // 2
     columns = pl.ds(pl.multiple_of(place_ref[0] * width, width), width)
     copies = start_copies(
@@ -117,7 +117,6 @@
         ),
         sems,
     )
-    pack_ref[:DT_AT] = x_ref[...]
     for copy in copies:
         copy.wait()
     lane = iota((1, inner), 1)
@@ -130,7 +129,7 @@
     packed.append(jnp.zeros((SMALL_AT - TAP_AT - taps_ref.shape[0], inner), F32))
     packed += parts_of(small) + parts_of(gain_ref[...])
     packed.append(jnp.zeros((PACKED - SMALL_AT - 6, inner), F32))
-    pack_ref[DT_AT:] = jnp.concatenate(packed, axis=0).astype(BF16)
+    pack_ref[...] = jnp.concatenate(packed, axis=0).astype(BF16)
 
 
 def unpack(ref):
@@ -156,17 +155,17 @@
 
 
 def front_kernel(
-    place_ref, hidden_ref, prev_ref, next_ref, own_ref, other_ref, bc_ref, tapbc_ref,
-    u_ref, y_ref, c_ref, cols_ref, first_ref, gains_ref, send_ref,
+    place_ref, hidden_ref, prev_ref, next_ref, own_zx_ref, other_zx_ref, own_ref, other_ref, bc_ref,
+    tapbc_ref, gate_ref, y_ref, c_ref, cols_ref, first_ref, gains_ref, send_ref,
     x_ref, b_ref, rows_ref, pad_ref,
 ):
     row_count, width = hidden_ref.shape[0], hidden_ref.shape[1] // 2
     inner = own_ref.shape[1]
     strand, position, count = place_ref[0], place_ref[2], place_ref[3]
     packs = (own_ref, other_ref)
+    projections = (own_zx_ref, other_zx_ref)
     turn = orient(width, strand)
     u = dot(hidden_ref[:, pl.ds(pl.multiple_of(strand * width, width), width)], turn).astype(BF16)
-    u_ref[...] = u
     before = jnp.where(position > 0, prev_ref[...].astype(F32), 0.0)
     after = jnp.where(position < count - 1, next_ref[...].astype(F32), 0.0)
     edge = dot(jnp.concatenate([before, after], axis=0).astype(BF16), turn).astype(BF16)
@@ -222,7 +221,7 @@
     mains = [(u, slice(HALO, HALO + row_count)), (edge, None)]
     for piece, where in mains:
         for g in range(3):
-            w = packs[g][:DT_AT] if g < 2 else bc_ref[...]
+            w = projections[g][:, inner:] if g < 2 else bc_ref[...]
             full = dot(piece, w).astype(BF16).astype(F32)
             for k in range(w.shape[1] // LANES):
                 value, at = full[:, k * LANES : (k + 1) * LANES], g * inner // LANES + k
@@ -298,6 +297,9 @@
                 send_ref[way * 32 + n * 4 + q] = jnp.concatenate(
                     [state[n * 8 : n * 8 + 8], decay], axis=0
                 ).astype(BF16)
+    for g, ref in enumerate(projections):
+        z = dot(u, ref[:, :inner]).astype(BF16).astype(F32)
+        gate_ref[:, g * inner : (g + 1) * inner] = z * sigmoid(z)
     inside(x_ref, b_ref, c_ref, rows_ref, cols_ref, gains_ref, y_ref)
 
 
@@ -350,29 +352,18 @@
                     )
 
 
-def ready_kernel(
-    place_ref, u_ref, own_z_ref, other_z_ref, own_out_ref, other_out_ref, gate_ref, w_ref
+def back_kernel(
+    place_ref, y_ref, c_ref, came_ref, first_ref, cols_ref, gate_ref, gains_ref, own_out_ref,
+    other_out_ref, hidden_ref, keep_ref, give_ref, state_ref, w_ref,
 ):
     rows, columns = own_out_ref.shape
     part = columns // 2
     source, target = iota((columns, columns), 0), iota((columns, columns), 1)
-    core = place_ref[1]
-    column = jnp.where(target < part, target + core * part, target - core * part)
+    column = jnp.where(target < part, target + place_ref[1] * part, target - place_ref[1] * part)
     wanted = jnp.where(place_ref[0] == 0, column, columns - 1 - column)
     chosen = (source == wanted).astype(BF16)
     w_ref[:rows] = dot(own_out_ref[...], chosen).astype(BF16)
     w_ref[rows:] = dot(other_out_ref[...], chosen).astype(BF16)
-    inner = own_z_ref.shape[1]
-    for g, ref in enumerate((own_z_ref, other_z_ref)):
-        z = dot(u_ref[...], ref[...]).astype(BF16).astype(F32)
-        gate_ref[:, g * inner : (g + 1) * inner] = z * sigmoid(z)
-
-
-def back_kernel(
-    place_ref, y_ref, c_ref, came_ref, first_ref, cols_ref, gate_ref, gains_ref, w_ref, hidden_ref,
-    keep_ref, give_ref, state_ref,
-):
-    part = w_ref.shape[1] // 2
     inner = y_ref.shape[2] // 2
     ours = pl.multiple_of((2 * place_ref[0] + place_ref[1]) * part, part)
     blocks = [slice(b * BLOCK, (b + 1) * BLOCK) for b in range(2)]
@@ -443,7 +434,7 @@
             struct((HALO, width), BF16),
             struct((HALO, width), BF16),
         ),
-        [SMEM, VMEM] + [HBM] * 7,
+        [SMEM] + [HBM] * 7,
         (VMEM,) * 3,
         cost(1_000_000, 0, 1_000_000),
         scratch=[
@@ -457,7 +448,6 @@
         ],
     )(
         place,
-        zx[:, inner:],
         *lying(
             proj_dt.T,
             conv_x,
@@ -469,19 +459,17 @@
         ),
     )
     beside = (("seq_1", "x_hi"), [(0, 3), (3, 0), (1, 2), (2, 1)])
+    other_zx = lax.ppermute(zx, *beside)
     other_pack = lax.ppermute(pack, *beside)
     prev = lax.ppermute(tail, SEQ, rise)
     following = lax.ppermute(head, SEQ, fall)
 
-    own_z, own_out, prev, following = lax.optimization_barrier(
-        (zx[:, :inner], out_proj, prev, following)
-    )
-    other_z = lax.ppermute(own_z, *beside)
+    own_out, prev, following = lax.optimization_barrier((out_proj, prev, following))
     other_out = lax.ppermute(own_out, *beside)
-    u, y, c, cols, first, gains, send = call(
+    gate, y, c, cols, first, gains, send = call(
         front_kernel,
         (
-            struct((rows, width), BF16),
+            struct((rows, 2 * inner), F32),
             struct((2, rows, 2 * inner), F32),
             struct((2, rows, LANES), BF16),
             struct((rows, LANES), F32),
@@ -489,7 +477,7 @@
             struct((8, 2 * inner), F32),
             struct((count, 16, LANES), BF16),
         ),
-        [SMEM] + [VMEM] * 7,
+        [SMEM] + [VMEM] * 9,
         (VMEM,) * 7,
         cost(8_000_000_000, 3_000_000, 24_000_000),
         scratch=[
@@ -498,16 +486,8 @@
             pltpu.VMEM((48, rows), F32),
             pltpu.VMEM((2 * inner // LANES + 1, rows + 2 * HALO, LANES), F32),
         ],
-    )(place, hidden_in, prev, following, pack, other_pack, proj_bc, conv_bc)
-    gate, weights = call(
-        ready_kernel,
-        (struct((rows, 2 * inner), F32), struct((2 * inner, 2 * inner), BF16)),
-        [SMEM] + [VMEM] * 5,
-        (VMEM, VMEM),
-        cost(1_000_000_000, 300_000, 3_000_000),
-    )(place, u, own_z, other_z, own_out, other_out)
-
-    send, gate, weights = lax.optimization_barrier((send, gate, weights))
+    )(place, hidden_in, prev, following, zx, other_zx, pack, other_pack, proj_bc, conv_bc)
+    send, other_out = lax.optimization_barrier((send, other_out))
     got = lax.all_to_all(send, SEQ, 0, 0, tiled=True)
     scanned = call(
         scan_kernel,
@@ -521,11 +501,14 @@
     keep, give = call(
         back_kernel,
         (struct((rows, inner), F32), struct((rows, inner), BF16)),
-        [SMEM] + [VMEM] * 9,
+        [SMEM] + [VMEM] * 10,
         (VMEM, VMEM),
         cost(2_000_000_000, 600_000, 6_000_000),
-        scratch=[pltpu.VMEM((2, STATE, 2 * inner), F32)],
-    )(place, y, c, came, first, cols, gate, gains, weights, hidden_in)
+        scratch=[
+            pltpu.VMEM((2, STATE, 2 * inner), F32),
+            pltpu.VMEM((2 * inner, 2 * inner), BF16),
+        ],
+    )(place, y, c, came, first, cols, gate, gains, out_proj, other_out, hidden_in)
     taken = lax.ppermute(give, "core", swap)
     return (keep + taken.astype(F32)).astype(BF16)
 

time: 74 us -> 69.9 us (0.945)
  waiting for transfers between devices: 6.69 us -> 3.23 us
  blocking collectives: 33.4 us -> 36.8 us
  starting transfers between devices: 19.7 us -> 16.7 us
  Pallas kernels: 11.7 us -> 10.8 us
    ppermute x1, waiting for transfers between devices: 4.48 us -> 0.77 us  [shards(): other_out = lax.ppermute(own_out, *beside)]
    ppermute x1, starting transfers between devices: 0.01 us -> 3.39 us  [shards(): other_zx = lax.ppermute(zx, *beside)]
    ppermute x1, starting transfers between devices: 3.39 us -> 0.11 us  [shards(): other_pack = lax.ppermute(pack, *beside)]
    all_to_all x1, blocking collectives: 19.2 us -> 22.5 us  [shards(): got = lax.all_to_all(send, SEQ, 0, 0, tiled=True)]
    ppermute x1, starting transfers between devices: 2.67 us -> 0.01 us  [shards(): other_out = lax.ppermute(own_out, *beside)]
    pallas_call x2 -> x1, Pallas kernels: 6.99 us -> 5.85 us  [shards(): call(front_kernel, (struct((rows, 2 * inner), F32), struct((2, rows, 2 *...]
  transfers between devices with their start and end apart: 6 -> 6, of which waited for: 3 -> 4; matrix products, arithmetic and copies ran while one was open for 0% -> 0% of each run, Pallas kernels for 8% -> 11%
where the time goes in v4:
time: 69.9 us; the launch traced here: 69.7 us
  blocking collectives  36.8 us (53%)
  starting transfers between devices  16.7 us (24%)
  Pallas kernels  10.8 us (15%)
  waiting for transfers between devices  3.23 us (5%)
  local copies, waits for them, and re-layouts  1.25 us (2%)
  other arithmetic  0.84 us (1%)
    all_to_all x1, blocking collectives, shards(): got = lax.all_to_all(send, SEQ, 0, 0, tiled=True)  22.5 us
    all_to_all x1, blocking collectives, shards(): came = lax.all_to_all(scanned, SEQ, 0, 0, tiled=True)  14.3 us
    ppermute x1, starting transfers between devices, shards(): following = lax.ppermute(head, SEQ, fall)  6.45 us
    pallas_call x1, Pallas kernels, shards(): call(front_kernel, (struct((rows, 2 * inner), F32), struct((2, rows, 2 *...  5.85 us
    ppermute x1, starting transfers between devices, shards(): taken = lax.ppermute(give, 'core', swap)  5.3 us
    ppermute x1, starting transfers between devices, shards(): other_zx = lax.ppermute(zx, *beside)  3.39 us
    pallas_call x1, Pallas kernels, shards(): call(back_kernel, (struct((rows, inner), F32), struct((rows, inner), BF16...  2.74 us
    pallas_call x1, Pallas kernels, shards(): call(pack_kernel, (struct((PACKED, inner), BF16), struct((HALO, width), B...  1.51 us
  transfers between devices with their start and end apart: 6, of which 4 were waited for; matrix products, arithmetic and copies ran while one was open for 0% of the time, Pallas kernels for 11%

profile of v4, /device:TPU:1, one launch (start us, length us, event | category | flops | bytes accessed | tf_op | source)
XLA Modules:
  0.0 69.7 jit_solution(12029201893258278607)
XLA Ops:
  0.0 0.0 copy-start
  0.0 0.0 copy-start.1
  0.0 0.0 copy-start.2
  0.0 0.0 copy-start.3
  0.0 1.2 %copy.12 = bf16[64,8,2,256]{3,1,2,0:T(8,128)(2,1)S(1)} copy(bf16[64,8,2,256]{3,2,1,0:T(2,128)(2,1)} %bitcast.12) | data formatting | bytes 1048576
  1.3 3.4 %collective-permute-start.2 = (bf16[512,512]{1,0:T(8,128)(2,1)S(1)}, bf16[512,512]{1,0:T(8,128)(2,1)S(1)}, u32[]{:S(2)}, u32[]{:S(2)}) collective-permute-start(bf16[512,512]{1,0:T(8,128)(2,1)S(1)} %bitcast.10), channel_id=1, source_target_pairs={{0,18},{18,0},{2,16},{16,2},{1,19},{19,1},{3,17},{17,3},{4,22},{22... | collective-permute-start | bytes 1572872 | tf_op jit(solution)/shard_map/ppermute | solution.py:462
  4.7 0.1 pad_add_fusion.place_ref
  4.7 1.5 %shard_map.109 = (bf16[32,256]{1,0:T(8,128)(2,1)S(1)}, bf16[8,512]{1,0:T(8,128)(2,1)S(1)}, bf16[8,512]{1,0:T(8,128)(2,1)S(1)}) custom-call(s32[4]{0:T(128)S(1)} %pad_add_fusion.place_ref, bf16[4,512]{1,0:T(4,128)(2,1)} %bitcast.13, bf16[4,256]{1,0:T(4,128)(2,1)} %taps_hbm.1, f32[1,4]{1,0:T(1,128)} %bitcast.15, s32[1,4]{1,0:T(1,128)} %bitcast.16, ...), custom_call_target="tpu_custom_call" | custom-call | flops 1000000 | bytes 1000000 | tf_op jit(solution)/shard_map/pallas_call | solution.py:430
  6.3 0.1 collective-permute-start.3
  6.4 1.5 %collective-permute-start = (bf16[8,512]{1,0:T(8,128)(2,1)S(1)}, bf16[8,512]{1,0:T(8,128)(2,1)S(1)}, u32[]{:S(2)}, u32[]{:S(2)}) collective-permute-start(bf16[8,512]{1,0:T(8,128)(2,1)S(1)} %get-tuple-element.22), channel_id=1, source_target_pairs={{0,4},{4,8},{8,12},{12,16},{16,20},{20,24},{24,28},{28,32},{32,36}... | collective-permute-start | bytes 24584 | tf_op jit(solution)/shard_map/ppermute | solution.py:464
  7.8 6.4 %collective-permute-start.1 = (bf16[8,512]{1,0:T(8,128)(2,1)S(1)}, bf16[8,512]{1,0:T(8,128)(2,1)S(1)}, u32[]{:S(2)}, u32[]{:S(2)}) collective-permute-start(bf16[8,512]{1,0:T(8,128)(2,1)S(1)} %get-tuple-element.23), channel_id=1, source_target_pairs={{4,0},{8,4},{12,8},{16,12},{20,16},{24,20},{28,24},{32,28},{36,32}... | collective-permute-start | bytes 24584 | tf_op jit(solution)/shard_map/ppermute | solution.py:465
  14.3 1.0 %collective-permute-done.prev_ref = bf16[8,512]{1,0:T(8,128)(2,1)S(1)} collective-permute-done((bf16[8,512]{1,0:T(8,128)(2,1)S(1)}, bf16[8,512]{1,0:T(8,128)(2,1)S(1)}, u32[]{:S(2)}, u32[]{:S(2)}) %collective-permute-start) | collective-permute-done | bytes 8224 | tf_op jit(solution)/shard_map/ppermute | solution.py:464
  15.3 0.0 collective-permute-done.1.next_ref
  15.3 0.0 copy-done.1
  15.3 0.0 collective-permute-start.4
  15.3 0.3 collective-permute-done.3.other_ref
  15.6 0.0 collective-permute-done.2.other_zx_ref
  15.6 0.0 copy-done
  15.6 0.0 copy-done.2
  15.6 0.0 copy-done.3
  15.6 5.8 %shard_map.110 = (f32[512,512]{1,0:T(8,128)S(1)}, f32[2,512,512]{2,1,0:T(8,128)S(1)}, bf16[2,512,128]{2,1,0:T(8,128)(2,1)S(1)}, f32[512,128]{1,0:T(8,128)S(1)}, ...) custom-call(s32[4]{0:T(128)S(1)} %pad_add_fusion.place_ref, ...), custom_call_target="tpu_custom_call" | custom-call | flops 8000000000 | bytes 24000000 | tf_op jit(solution)/shard_map/pallas_call | solution.py:469
  21.5 0.8 %collective-permute-done.4.other_out_ref = bf16[256,512]{1,0:T(8,128)(2,1)S(1)} collective-permute-done((bf16[256,512]{1,0:T(8,128)(2,1)S(1)}, bf16[256,512]{1,0:T(8,128)(2,1)S(1)}, u32[]{:S(2)}, u32[]{:S(2)}) %collective-permute-start.4) | collective-permute-done | bytes 262176 | tf_op jit(solution)/shard_map/ppermute | solution.py:468
  22.2 22.5 %all_to_all.10.got_ref = bf16[64,16,128]{2,1,0:T(8,128)(2,1)S(1)} all-to-all(bf16[64,16,128]{2,1,0:T(8,128)(2,1)S(1)} %get-tuple-element.31), channel_id=1, replica_groups=mesh['seq_0'=8,'seq_1'=2,'seq_2'=4,'x_hi'=2,'core'=2] {'seq_0','seq_1','..., dimensions={0} | all-to-all | bytes 524288 | tf_op jit(solution)/shard_map/all_to_all | solution.py:491
  44.7 0.7 shard_map.111
  45.4 14.3 %all_to_all.11.came_ref = bf16[64,8,128]{2,1,0:T(8,128)(2,1)S(1)} all-to-all(bf16[64,8,128]{2,1,0:T(8,128)(2,1)S(1)} %shard_map.111), channel_id=1, replica_groups=mesh['seq_0'=8,'seq_1'=2,'seq_2'=4,'x_hi'=2,'core'=2] {'seq_0','seq_1','..., dimensions={0} | all-to-all | bytes 262144 | tf_op jit(solution)/shard_map/all_to_all | solution.py:499
  59.7 2.7 %shard_map.112 = (f32[512,256]{1,0:T(8,128)S(1)}, bf16[512,256]{1,0:T(8,128)(2,1)S(1)}) custom-call(s32[4]{0:T(128)S(1)} %pad_add_fusion.place_ref, f32[2,512,512]{2,1,0:T(8,128)S(1)} %get-tuple-element.27.y_ref, bf16[2,512,128]{2,1,0:T(8,128)(2,1)S(1)} %get-tuple-element.28.c_ref, bf16[64,8,128]{2,1,0:T(8,128)(2,1)S(1)} %all_to_all.11.came_ref, ...), custom_call_target="tpu_custom_call" | custom-call | flops 2000000000 | bytes 6000000 | tf_op jit(solution)/shard_map/pallas_call | solution.py:501
  62.4 5.3 %collective-permute-start.5 = (bf16[512,256]{1,0:T(8,128)(2,1)S(1)}, bf16[512,256]{1,0:T(8,128)(2,1)S(1)}, u32[]{:S(2)}, u32[]{:S(2)}) collective-permute-start(bf16[512,256]{1,0:T(8,128)(2,1)S(1)} %get-tuple-element.38), channel_id=1, source_target_pairs={{0,1},{1,0},{2,3},{3,2},{4,5},{5,4},{6,7},{7,6},{8,9},{9,8},{10,11... | collective-permute-start | bytes 786440 | tf_op jit(solution)/shard_map/ppermute | solution.py:512
  67.7 1.2 %collective-permute-done.5 = bf16[512,256]{1,0:T(8,128)(2,1)S(1)} collective-permute-done((bf16[512,256]{1,0:T(8,128)(2,1)S(1)}, bf16[512,256]{1,0:T(8,128)(2,1)S(1)}, u32[]{:S(2)}, u32[]{:S(2)}) %collective-permute-start.5) | collective-permute-done | bytes 262176 | tf_op jit(solution)/shard_map/ppermute | solution.py:512
  68.9 0.8 %add_convert_fusion = bf16[512,256]{1,0:T(8,128)(2,1)} fusion(f32[512,256]{1,0:T(8,128)S(1)} %get-tuple-element.37, bf16[512,256]{1,0:T(8,128)(2,1)S(1)} %collective-permute-done.5), kind=kLoop, calls=%fused_computation | loop fusion | flops 393216 | bytes 1048576 | tf_op jit(solution)/shard_map/convert_element_type | solution.py:513
Async XLA Ops:
  0.0 15.6 %copy-start = (bf16[512,1024]{1,0:T(8,128)(2,1)S(1)}, bf16[512,1024]{1,0:T(8,128)(2,1)}, u32[]{:S(2)}) copy-start(bf16[512,1024]{1,0:T(8,128)(2,1)} %hidden_ref.3) | copy-start | bytes 3145732
  0.0 15.3 %copy-start.1 = (bf16[256,512]{1,0:T(8,128)(2,1)S(1)}, bf16[256,512]{1,0:T(8,128)(2,1)}, u32[]{:S(2)}) copy-start(bf16[256,512]{1,0:T(8,128)(2,1)} %own_out_ref.1) | copy-start | bytes 786436
  0.0 15.6 %copy-start.2 = (bf16[512,128]{1,0:T(8,128)(2,1)S(1)}, bf16[512,128]{1,0:T(8,128)(2,1)}, u32[]{:S(2)}) copy-start(bf16[512,128]{1,0:T(8,128)(2,1)} %bc_ref.1) | copy-start | bytes 393220
  0.0 15.6 %copy-start.3 = (bf16[4,128]{1,0:T(4,128)(2,1)S(1)}, bf16[4,128]{1,0:T(4,128)(2,1)}, u32[]{:S(2)}) copy-start(bf16[4,128]{1,0:T(4,128)(2,1)} %tapbc_ref.1) | copy-start | bytes 3076
  1.3 14.3 %collective-permute-start.2 = (bf16[512,512]{1,0:T(8,128)(2,1)S(1)}, bf16[512,512]{1,0:T(8,128)(2,1)S(1)}, u32[]{:S(2)}, u32[]{:S(2)}) collective-permute-start(bf16[512,512]{1,0:T(8,128)(2,1)S(1)} %bitcast.10), channel_id=1, source_target_pairs={{0,18},{18,0},{2,16},{16,2},{1,19},{19,1},{3,17},{17,3},{4,22},{22... | collective-permute-start | bytes 1572872 | tf_op jit(solution)/shard_map/ppermute | solution.py:462
  6.3 9.3 %collective-permute-start.3 = (bf16[32,256]{1,0:T(8,128)(2,1)S(1)}, bf16[32,256]{1,0:T(8,128)(2,1)S(1)}, u32[]{:S(2)}, u32[]{:S(2)}) collective-permute-start(bf16[32,256]{1,0:T(8,128)(2,1)S(1)} %get-tuple-element.26.own_ref), channel_id=1, source_target_pairs={{0,18},{18,0},{2,16},{16,2},{1,19},{19,1},{3,17},{17,3},{4,22},{22... | collective-permute-start | bytes 49160 | tf_op jit(solution)/shard_map/ppermute | solution.py:463
  6.4 9.0 %collective-permute-start = (bf16[8,512]{1,0:T(8,128)(2,1)S(1)}, bf16[8,512]{1,0:T(8,128)(2,1)S(1)}, u32[]{:S(2)}, u32[]{:S(2)}) collective-permute-start(bf16[8,512]{1,0:T(8,128)(2,1)S(1)} %get-tuple-element.22), channel_id=1, source_target_pairs={{0,4},{4,8},{8,12},{12,16},{16,20},{20,24},{24,28},{28,32},{32,36}... | collective-permute-start | bytes 24584 | tf_op jit(solution)/shard_map/ppermute | solution.py:464
  7.8 7.5 %collective-permute-start.1 = (bf16[8,512]{1,0:T(8,128)(2,1)S(1)}, bf16[8,512]{1,0:T(8,128)(2,1)S(1)}, u32[]{:S(2)}, u32[]{:S(2)}) collective-permute-start(bf16[8,512]{1,0:T(8,128)(2,1)S(1)} %get-tuple-element.23), channel_id=1, source_target_pairs={{4,0},{8,4},{12,8},{16,12},{20,16},{24,20},{28,24},{32,28},{36,32}... | collective-permute-start | bytes 24584 | tf_op jit(solution)/shard_map/ppermute | solution.py:465
  15.3 6.9 %collective-permute-start.4 = (bf16[256,512]{1,0:T(8,128)(2,1)S(1)}, bf16[256,512]{1,0:T(8,128)(2,1)S(1)}, u32[]{:S(2)}, u32[]{:S(2)}) collective-permute-start(bf16[256,512]{1,0:T(8,128)(2,1)S(1)} %copy-done.1), channel_id=1, source_target_pairs={{0,18},{18,0},{2,16},{16,2},{1,19},{19,1},{3,17},{17,3},{4,22},{22... | collective-permute-start | bytes 786440 | tf_op jit(solution)/shard_map/ppermute | solution.py:468
  62.4 6.5 %collective-permute-start.5 = (bf16[512,256]{1,0:T(8,128)(2,1)S(1)}, bf16[512,256]{1,0:T(8,128)(2,1)S(1)}, u32[]{:S(2)}, u32[]{:S(2)}) collective-permute-start(bf16[512,256]{1,0:T(8,128)(2,1)S(1)} %get-tuple-element.38), channel_id=1, source_target_pairs={{0,1},{1,0},{2,3},{3,2},{4,5},{5,4},{6,7},{7,6},{8,9},{9,8},{10,11... | collective-permute-start | bytes 786440 | tf_op jit(solution)/shard_map/ppermute | solution.py:512

commit v5 on v4

--- a/solution.py
+++ b/solution.py
@@ -93,11 +93,11 @@
     return (source == jnp.where(strand == 0, target, n - 1 - target)).astype(BF16)
 
 
-DT_AT, TAP_AT, SMALL_AT, PACKED = 0, 8, 16, 32
+DT_AT, TAP_AT, SMALL_AT, PACKED = 512, 520, 528, 544
 
 
 def pack_kernel(
-    place_ref, dt_hbm, taps_hbm, bias_hbm, exp_hbm, skip_hbm, gain_hbm, hidden_hbm,
+    place_ref, x_ref, dt_hbm, taps_hbm, bias_hbm, exp_hbm, skip_hbm, gain_hbm, hidden_hbm,
     pack_ref, head_ref, tail_ref,
     dt_ref, taps_ref, bias_ref, exp_ref, skip_ref, gain_ref, sems,
 ):
@@ -117,6 +117,7 @@
         ),
         sems,
     )
+    pack_ref[:DT_AT] = x_ref[...]
     for copy in copies:
         copy.wait()
     lane = iota((1, inner), 1)
@@ -129,7 +130,7 @@
     packed.append(jnp.zeros((SMALL_AT - TAP_AT - taps_ref.shape[0], inner), F32))
     packed += parts_of(small) + parts_of(gain_ref[...])
     packed.append(jnp.zeros((PACKED - SMALL_AT - 6, inner), F32))
-    pack_ref[...] = jnp.concatenate(packed, axis=0).astype(BF16)
+    pack_ref[DT_AT:] = jnp.concatenate(packed, axis=0).astype(BF16)
 
 
 def unpack(ref):
@@ -154,21 +155,48 @@
     )
 
 
+def turned_out(place_ref, out_ref):
+    columns = out_ref.shape[1]
+    part = columns // 2
+    source, target = iota((columns, columns), 0), iota((columns, columns), 1)
+    column = jnp.where(target < part, target + place_ref[1] * part, target - place_ref[1] * part)
+    wanted = jnp.where(place_ref[0] == 0, column, columns - 1 - column)
+    return dot(out_ref[...], (source == wanted).astype(BF16)).astype(BF16)
+
+
+def gated_by(u, w):
+    z = dot(u, w).astype(BF16).astype(F32)
+    return z * sigmoid(z)
+
+
+def early_kernel(
+    place_ref, hidden_ref, zx_ref, bc_ref, out_ref, u_ref, main_ref, gate_ref, w_ref
+):
+    width, inner = zx_ref.shape[0], zx_ref.shape[1] // 2
+    strand = place_ref[0]
+    u = hidden_ref[:, pl.ds(pl.multiple_of(strand * width, width), width)]
+    u = dot(u, orient(width, strand)).astype(BF16)
+    u_ref[...] = u
+    main_ref[:, :inner] = dot(u, zx_ref[:, inner:]).astype(BF16)
+    main_ref[:, inner:] = dot(u, bc_ref[...]).astype(BF16)
+    gate_ref[...] = gated_by(u, zx_ref[:, :inner])
+    w_ref[...] = turned_out(place_ref, out_ref)
+
+
 def front_kernel(
-    place_ref, hidden_ref, prev_ref, next_ref, own_zx_ref, other_zx_ref, own_ref, other_ref, bc_ref,
-    tapbc_ref, gate_ref, y_ref, c_ref, cols_ref, first_ref, gains_ref, send_ref,
+    place_ref, u_ref, main_ref, prev_ref, next_ref, own_ref, other_ref, bc_ref, tapbc_ref,
+    y_ref, c_ref, cols_ref, first_ref, gains_ref, send_ref,
     x_ref, b_ref, rows_ref, pad_ref,
 ):
-    row_count, width = hidden_ref.shape[0], hidden_ref.shape[1] // 2
+    row_count, width = u_ref.shape
     inner = own_ref.shape[1]
     strand, position, count = place_ref[0], place_ref[2], place_ref[3]
     packs = (own_ref, other_ref)
-    projections = (own_zx_ref, other_zx_ref)
-    turn = orient(width, strand)
-    u = dot(hidden_ref[:, pl.ds(pl.multiple_of(strand * width, width), width)], turn).astype(BF16)
+    u = u_ref[...]
     before = jnp.where(position > 0, prev_ref[...].astype(F32), 0.0)
     after = jnp.where(position < count - 1, next_ref[...].astype(F32), 0.0)
-    edge = dot(jnp.concatenate([before, after], axis=0).astype(BF16), turn).astype(BF16)
+    edge = dot(jnp.concatenate([before, after], axis=0).astype(BF16), orient(width, strand))
+    edge = edge.astype(BF16)
 
     raw = jnp.concatenate(
         [
@@ -218,18 +246,20 @@
     totals = [ends[b][:, :1] for b in range(2)]
 
     chunk = 32
-    mains = [(u, slice(HALO, HALO + row_count)), (edge, None)]
-    for piece, where in mains:
-        for g in range(3):
-            w = projections[g][:, inner:] if g < 2 else bc_ref[...]
-            full = dot(piece, w).astype(BF16).astype(F32)
-            for k in range(w.shape[1] // LANES):
-                value, at = full[:, k * LANES : (k + 1) * LANES], g * inner // LANES + k
-                if where is not None:
-                    pad_ref[at, where] = value
-                else:
-                    pad_ref[at, :HALO] = value[:HALO]
-                    pad_ref[at, HALO + row_count :] = value[HALO:]
+    tiles = inner // LANES
+    for g in range(3):
+        w = packs[g][:DT_AT] if g < 2 else bc_ref[...]
+        if g == 1:
+            middle = dot(u, w).astype(BF16)
+        else:
+            middle = main_ref[:, :inner] if g == 0 else main_ref[:, inner:]
+        middle = middle.astype(F32)
+        outer = dot(edge, w).astype(BF16).astype(F32)
+        for k in range(w.shape[1] // LANES):
+            at, lanes = g * tiles + k, slice(k * LANES, (k + 1) * LANES)
+            pad_ref[at, :HALO] = outer[:HALO, lanes]
+            pad_ref[at, HALO : HALO + row_count] = middle[:, lanes]
+            pad_ref[at, HALO + row_count :] = outer[HALO:, lanes]
     taps = jnp.concatenate(
         [ref[TAP_AT : TAP_AT + REACH + 1].astype(F32) for ref in packs]
         + [tapbc_ref[...].astype(F32)],
@@ -297,9 +327,6 @@
                 send_ref[way * 32 + n * 4 + q] = jnp.concatenate(
                     [state[n * 8 : n * 8 + 8], decay], axis=0
                 ).astype(BF16)
-    for g, ref in enumerate(projections):
-        z = dot(u, ref[:, :inner]).astype(BF16).astype(F32)
-        gate_ref[:, g * inner : (g + 1) * inner] = z * sigmoid(z)
     inside(x_ref, b_ref, c_ref, rows_ref, cols_ref, gains_ref, y_ref)
 
 
@@ -353,20 +380,15 @@
 
 
 def back_kernel(
-    place_ref, y_ref, c_ref, came_ref, first_ref, cols_ref, gate_ref, gains_ref, own_out_ref,
-    other_out_ref, hidden_ref, keep_ref, give_ref, state_ref, w_ref,
+    place_ref, y_ref, c_ref, came_ref, first_ref, cols_ref, gains_ref, own_gate_ref, own_w_ref,
+    u_ref, other_z_ref, other_out_ref, hidden_ref, keep_ref, give_ref, state_ref, w_ref,
 ):
-    rows, columns = own_out_ref.shape
-    part = columns // 2
-    source, target = iota((columns, columns), 0), iota((columns, columns), 1)
-    column = jnp.where(target < part, target + place_ref[1] * part, target - place_ref[1] * part)
-    wanted = jnp.where(place_ref[0] == 0, column, columns - 1 - column)
-    chosen = (source == wanted).astype(BF16)
-    w_ref[:rows] = dot(own_out_ref[...], chosen).astype(BF16)
-    w_ref[rows:] = dot(other_out_ref[...], chosen).astype(BF16)
+    part = own_w_ref.shape[1] // 2
     inner = y_ref.shape[2] // 2
     ours = pl.multiple_of((2 * place_ref[0] + place_ref[1]) * part, part)
     blocks = [slice(b * BLOCK, (b + 1) * BLOCK) for b in range(2)]
+    w_ref[:inner] = own_w_ref[...]
+    w_ref[inner:] = turned_out(place_ref, other_out_ref)
     same = (iota((inner, inner), 0) // HEADP == iota((inner, inner), 1) // HEADP).astype(BF16)
     for way in range(2):
         for n in range(8):
@@ -376,7 +398,9 @@
                 ].astype(F32)
     for b, block in enumerate(blocks):
         decays = jnp.exp2(cols_ref[block])
-        gate = gate_ref[block, :]
+        gate = jnp.concatenate(
+            [own_gate_ref[block, :], gated_by(u_ref[block, :], other_z_ref[...])], axis=1
+        )
         total = None
         for way in range(2):
             state = state_ref[way]
@@ -434,7 +458,7 @@
             struct((HALO, width), BF16),
             struct((HALO, width), BF16),
         ),
-        [SMEM] + [HBM] * 7,
+        [SMEM, VMEM] + [HBM] * 7,
         (VMEM,) * 3,
         cost(1_000_000, 0, 1_000_000),
         scratch=[
@@ -448,6 +472,7 @@
         ],
     )(
         place,
+        zx[:, inner:],
         *lying(
             proj_dt.T,
             conv_x,
@@ -459,17 +484,28 @@
         ),
     )
     beside = (("seq_1", "x_hi"), [(0, 3), (3, 0), (1, 2), (2, 1)])
-    other_zx = lax.ppermute(zx, *beside)
     other_pack = lax.ppermute(pack, *beside)
     prev = lax.ppermute(tail, SEQ, rise)
     following = lax.ppermute(head, SEQ, fall)
 
-    own_out, prev, following = lax.optimization_barrier((out_proj, prev, following))
+    own_z, own_out, pack = lax.optimization_barrier((zx[:, :inner], out_proj, pack))
+    other_z = lax.ppermute(own_z, *beside)
     other_out = lax.ppermute(own_out, *beside)
-    gate, y, c, cols, first, gains, send = call(
+    u, main, own_gate, own_w = call(
+        early_kernel,
+        (
+            struct((rows, width), BF16),
+            struct((rows, inner + LANES), BF16),
+            struct((rows, inner), F32),
+            struct((inner, 2 * inner), BF16),
+        ),
+        [SMEM] + [VMEM] * 4,
+        (VMEM,) * 4,
+        cost(2_000_000_000, 130_000, 4_000_000),
+    )(place, hidden_in, zx, proj_bc, out_proj)
+    y, c, cols, first, gains, send = call(
         front_kernel,
         (
-            struct((rows, 2 * inner), F32),
             struct((2, rows, 2 * inner), F32),
             struct((2, rows, LANES), BF16),
             struct((rows, LANES), F32),
@@ -477,8 +513,8 @@
             struct((8, 2 * inner), F32),
             struct((count, 16, LANES), BF16),
         ),
-        [SMEM] + [VMEM] * 9,
-        (VMEM,) * 7,
+        [SMEM] + [VMEM] * 8,
+        (VMEM,) * 6,
         cost(8_000_000_000, 3_000_000, 24_000_000),
         scratch=[
             pltpu.VMEM((2, rows, 2 * inner), BF16),
@@ -486,8 +522,8 @@
             pltpu.VMEM((48, rows), F32),
             pltpu.VMEM((2 * inner // LANES + 1, rows + 2 * HALO, LANES), F32),
         ],
-    )(place, hidden_in, prev, following, zx, other_zx, pack, other_pack, proj_bc, conv_bc)
-    send, other_out = lax.optimization_barrier((send, other_out))
+    )(place, u, main, prev, following, pack, other_pack, proj_bc, conv_bc)
+    send, other_z, other_out = lax.optimization_barrier((send, other_z, other_out))
     got = lax.all_to_all(send, SEQ, 0, 0, tiled=True)
     scanned = call(
         scan_kernel,
@@ -501,14 +537,16 @@
     keep, give = call(
         back_kernel,
         (struct((rows, inner), F32), struct((rows, inner), BF16)),
-        [SMEM] + [VMEM] * 10,
+        [SMEM] + [VMEM] * 12,
         (VMEM, VMEM),
         cost(2_000_000_000, 600_000, 6_000_000),
         scratch=[
             pltpu.VMEM((2, STATE, 2 * inner), F32),
             pltpu.VMEM((2 * inner, 2 * inner), BF16),
         ],
-    )(place, y, c, came, first, cols, gate, gains, out_proj, other_out, hidden_in)
+    )(
+        place, y, c, came, first, cols, gains, own_gate, own_w, u, other_z, other_out, hidden_in
+    )
     taken = lax.ppermute(give, "core", swap)
     return (keep + taken.astype(F32)).astype(BF16)
 

time: 69.9 us -> 70.5 us (level)
  blocking collectives: 36.8 us -> 34.3 us
  waiting for transfers between devices: 3.23 us -> 5.13 us
    all_to_all x1, blocking collectives: 22.5 us -> 18.6 us  [shards(): got = lax.all_to_all(send, SEQ, 0, 0, tiled=True)]
    ppermute x1, starting transfers between devices: 3.39 us -> 0.01 us  [shards(): other_z = lax.ppermute(own_z, *beside)]
    ppermute x1, starting transfers between devices: 0.11 us -> 3.39 us  [shards(): other_pack = lax.ppermute(pack, *beside)]
    ppermute x1, waiting for transfers between devices: 0.77 us -> 3.95 us  [shards(): other_out = lax.ppermute(own_out, *beside)]
    ppermute x1, starting transfers between devices: 0.01 us -> 2.67 us  [shards(): other_out = lax.ppermute(own_out, *beside)]
    ppermute x1, starting transfers between devices: 5.3 us -> 3.38 us  [shards(): taken = lax.ppermute(give, 'core', swap)]
    all_to_all x1, blocking collectives: 14.3 us -> 15.7 us  [shards(): came = lax.all_to_all(scanned, SEQ, 0, 0, tiled=True)]
    ppermute x1, waiting for transfers between devices: 1.03 us -> 0.01 us  [shards(): prev = lax.ppermute(tail, SEQ, rise)]
  transfers between devices with their start and end apart: 6 -> 6, of which waited for: 4 -> 2; matrix products, arithmetic and copies ran while one was open for 0% -> 0% of each run, Pallas kernels for 11% -> 10%
where the time goes in v5:
time: 70.5 us; the launch traced here: 70.3 us
  blocking collectives  34.3 us (49%)
  starting transfers between devices  17.1 us (24%)
  Pallas kernels  11.4 us (16%)
  waiting for transfers between devices  5.13 us (7%)
  local copies, waits for them, and re-layouts  1.28 us (2%)
  other arithmetic  0.84 us (1%)
    all_to_all x1, blocking collectives, shards(): got = lax.all_to_all(send, SEQ, 0, 0, tiled=True)  18.6 us
    all_to_all x1, blocking collectives, shards(): came = lax.all_to_all(scanned, SEQ, 0, 0, tiled=True)  15.7 us
    ppermute x1, starting transfers between devices, shards(): following = lax.ppermute(head, SEQ, fall)  6.39 us
    pallas_call x1, Pallas kernels, shards(): call(front_kernel, (struct((2, rows, 2 * inner), F32), struct((2, rows, L...  5.14 us
    ppermute x1, waiting for transfers between devices, shards(): other_out = lax.ppermute(own_out, *beside)  3.95 us
    ppermute x1, starting transfers between devices, shards(): other_pack = lax.ppermute(pack, *beside)  3.39 us
    ppermute x1, starting transfers between devices, shards(): taken = lax.ppermute(give, 'core', swap)  3.38 us
    ppermute x1, starting transfers between devices, shards(): other_out = lax.ppermute(own_out, *beside)  2.67 us
  transfers between devices with their start and end apart: 6, of which 2 were waited for; matrix products, arithmetic and copies ran while one was open for 0% of the time, Pallas kernels for 10%

profile of v5, /device:TPU:1, one launch (start us, length us, event | category | flops | bytes accessed | tf_op | source)
XLA Modules:
  0.0 70.3 jit_solution(5984476615782222304)
XLA Ops:
  0.0 0.0 copy-start
  0.0 0.0 copy-start.1
  0.0 0.0 copy-start.2
  0.0 1.2 %copy.12 = bf16[64,8,2,256]{3,1,2,0:T(8,128)(2,1)S(1)} copy(bf16[64,8,2,256]{3,2,1,0:T(2,128)(2,1)} %bitcast.12) | data formatting | bytes 1048576
  1.3 0.1 pad_add_fusion.place_ref
  1.4 1.5 %shard_map.110 = (bf16[544,256]{1,0:T(8,128)(2,1)S(1)}, bf16[8,512]{1,0:T(8,128)(2,1)S(1)}, bf16[8,512]{1,0:T(8,128)(2,1)S(1)}) custom-call(s32[4]{0:T(128)S(1)} %pad_add_fusion.place_ref, bf16[512,256]{1,0:T(8,128)(2,1)S(1)} %get-tuple-element.48.x_ref, bf16[4,512]{1,0:T(4,128)(2,1)} %bitcast.13, bf16[4,256]{1,0:T(4,128)(2,1)} %taps_hbm.1, ...), custom_call_target="tpu_custom_call" | custom-call | flops 1000000 | bytes 1000000 | tf_op jit(solution)/shard_map/pallas_call | solution.py:454
  2.9 3.4 %collective-permute-start.2 = (bf16[544,256]{1,0:T(8,128)(2,1)S(1)}, bf16[544,256]{1,0:T(8,128)(2,1)S(1)}, u32[]{:S(2)}, u32[]{:S(2)}) collective-permute-start(bf16[544,256]{1,0:T(8,128)(2,1)S(1)} %get-tuple-element.31.own_ref), channel_id=1, source_target_pairs={{0,18},{18,0},{2,16},{16,2},{1,19},{19,1},{3,17},{17,3},{4,22},{22... | collective-permute-start | bytes 835592 | tf_op jit(solution)/shard_map/ppermute | solution.py:487
  6.3 1.3 %collective-permute-start = (bf16[8,512]{1,0:T(8,128)(2,1)S(1)}, bf16[8,512]{1,0:T(8,128)(2,1)S(1)}, u32[]{:S(2)}, u32[]{:S(2)}) collective-permute-start(bf16[8,512]{1,0:T(8,128)(2,1)S(1)} %get-tuple-element.28), channel_id=1, source_target_pairs={{0,4},{4,8},{8,12},{12,16},{16,20},{20,24},{24,28},{28,32},{32,36}... | collective-permute-start | bytes 24584 | tf_op jit(solution)/shard_map/ppermute | solution.py:488
  7.6 6.4 %collective-permute-start.1 = (bf16[8,512]{1,0:T(8,128)(2,1)S(1)}, bf16[8,512]{1,0:T(8,128)(2,1)S(1)}, u32[]{:S(2)}, u32[]{:S(2)}) collective-permute-start(bf16[8,512]{1,0:T(8,128)(2,1)S(1)} %get-tuple-element.29), channel_id=1, source_target_pairs={{4,0},{8,4},{12,8},{16,12},{20,16},{24,20},{28,24},{32,28},{36,32}... | collective-permute-start | bytes 24584 | tf_op jit(solution)/shard_map/ppermute | solution.py:489
  14.0 0.0 copy-start.3
  14.0 0.0 collective-permute-start.3
  14.0 0.0 copy-done.1
  14.0 2.7 %collective-permute-start.4 = (bf16[256,512]{1,0:T(8,128)(2,1)S(1)}, bf16[256,512]{1,0:T(8,128)(2,1)S(1)}, u32[]{:S(2)}, u32[]{:S(2)}) collective-permute-start(bf16[256,512]{1,0:T(8,128)(2,1)S(1)} %copy-done.1), channel_id=1, source_target_pairs={{0,18},{18,0},{2,16},{16,2},{1,19},{19,1},{3,17},{17,3},{4,22},{22... | collective-permute-start | bytes 786440 | tf_op jit(solution)/shard_map/ppermute | solution.py:493
  16.7 0.0 copy-done
  16.7 0.0 copy-done.2
  16.7 1.5 %shard_map.109 = (bf16[512,512]{1,0:T(8,128)(2,1)S(1)}, bf16[512,384]{1,0:T(8,128)(2,1)S(1)}, f32[512,256]{1,0:T(8,128)S(1)}, bf16[256,512]{1,0:T(8,128)(2,1)S(1)}) custom-call(s32[4]{0:T(128)S(1)} %pad_add_fusion.place_ref, bf16[512,1024]{1,0:T(8,128)(2,1)S(1)} %copy-done, bf16[512,512]{1,0:T(8,128)(2,1)S(1)} %bitcast.11, bf16[512,128]{1,0:T(8,128)(2,1)S(1)} %copy-done.2, ...), custom_call_target="tpu_custom_call" | custom-call | flops 2000000000 | bytes 4000000 | tf_op jit(solution)/shard_map/pallas_call | solution.py:494
  18.2 0.0 collective-permute-done.prev_ref
  18.3 0.0 collective-permute-done.1.next_ref
  18.3 0.0 collective-permute-done.2.other_ref
  18.3 0.0 copy-done.3
  18.3 5.1 %shard_map.111 = (f32[2,512,512]{2,1,0:T(8,128)S(1)}, bf16[2,512,128]{2,1,0:T(8,128)(2,1)S(1)}, f32[512,128]{1,0:T(8,128)S(1)}, f32[2,64,512]{2,1,0:T(8,128)S(1)...) custom-call(s32[4]{0:T(128)S(1)} %pad_add_fusion.place_ref, bf16[512,512]{1,0:T(8,128)(2,1)S(1)} %get-tuple-element.26.u_ref, ...), custom_call_target="tpu_custom_call" | custom-call | flops 8000000000 | bytes 24000000 | tf_op jit(solution)/shard_map/pallas_call | solution.py:506
  23.4 0.0 collective-permute-done.3.other_z_ref
  23.4 4.0 %collective-permute-done.4.other_out_ref = bf16[256,512]{1,0:T(8,128)(2,1)S(1)} collective-permute-done((bf16[256,512]{1,0:T(8,128)(2,1)S(1)}, bf16[256,512]{1,0:T(8,128)(2,1)S(1)}, u32[]{:S(2)}, u32[]{:S(2)}) %collective-permute-start.4) | collective-permute-done | bytes 262176 | tf_op jit(solution)/shard_map/ppermute | solution.py:493
  27.4 18.6 %all_to_all.10.got_ref = bf16[64,16,128]{2,1,0:T(8,128)(2,1)S(1)} all-to-all(bf16[64,16,128]{2,1,0:T(8,128)(2,1)S(1)} %get-tuple-element.37), channel_id=1, replica_groups=mesh['seq_0'=8,'seq_1'=2,'seq_2'=4,'x_hi'=2,'core'=2] {'seq_0','seq_1','..., dimensions={0} | all-to-all | bytes 524288 | tf_op jit(solution)/shard_map/all_to_all | solution.py:527
  46.0 0.7 shard_map.112
  46.7 15.7 %all_to_all.11.came_ref = bf16[64,8,128]{2,1,0:T(8,128)(2,1)S(1)} all-to-all(bf16[64,8,128]{2,1,0:T(8,128)(2,1)S(1)} %shard_map.112), channel_id=1, replica_groups=mesh['seq_0'=8,'seq_1'=2,'seq_2'=4,'x_hi'=2,'core'=2] {'seq_0','seq_1','..., dimensions={0} | all-to-all | bytes 262144 | tf_op jit(solution)/shard_map/all_to_all | solution.py:535
  62.4 2.5 %shard_map.113 = (f32[512,256]{1,0:T(8,128)S(1)}, bf16[512,256]{1,0:T(8,128)(2,1)S(1)}) custom-call(s32[4]{0:T(128)S(1)} %pad_add_fusion.place_ref, f32[2,512,512]{2,1,0:T(8,128)S(1)} %get-tuple-element.32.y_ref, bf16[2,512,128]{2,1,0:T(8,128)(2,1)S(1)} %get-tuple-element.33.c_ref, bf16[64,8,128]{2,1,0:T(8,128)(2,1)S(1)} %all_to_all.11.came_ref, ...), custom_call_target="tpu_custom_call" | custom-call | flops 2000000000 | bytes 6000000 | tf_op jit(solution)/shard_map/pallas_call | solution.py:537
  65.0 3.4 %collective-permute-start.5 = (bf16[512,256]{1,0:T(8,128)(2,1)S(1)}, bf16[512,256]{1,0:T(8,128)(2,1)S(1)}, u32[]{:S(2)}, u32[]{:S(2)}) collective-permute-start(bf16[512,256]{1,0:T(8,128)(2,1)S(1)} %get-tuple-element.46), channel_id=1, source_target_pairs={{0,1},{1,0},{2,3},{3,2},{4,5},{5,4},{6,7},{7,6},{8,9},{9,8},{10,11... | collective-permute-start | bytes 786440 | tf_op jit(solution)/shard_map/ppermute | solution.py:550
  68.3 1.2 %collective-permute-done.5 = bf16[512,256]{1,0:T(8,128)(2,1)S(1)} collective-permute-done((bf16[512,256]{1,0:T(8,128)(2,1)S(1)}, bf16[512,256]{1,0:T(8,128)(2,1)S(1)}, u32[]{:S(2)}, u32[]{:S(2)}) %collective-permute-start.5) | collective-permute-done | bytes 262176 | tf_op jit(solution)/shard_map/ppermute | solution.py:550
  69.5 0.8 %add_convert_fusion = bf16[512,256]{1,0:T(8,128)(2,1)} fusion(f32[512,256]{1,0:T(8,128)S(1)} %get-tuple-element.45, bf16[512,256]{1,0:T(8,128)(2,1)S(1)} %collective-permute-done.5), kind=kLoop, calls=%fused_computation | loop fusion | flops 393216 | bytes 1048576 | tf_op jit(solution)/shard_map/convert_element_type | solution.py:551
  (1 shorter events, 0.0 us)
Async XLA Ops:
  0.0 16.7 %copy-start = (bf16[512,1024]{1,0:T(8,128)(2,1)S(1)}, bf16[512,1024]{1,0:T(8,128)(2,1)}, u32[]{:S(2)}) copy-start(bf16[512,1024]{1,0:T(8,128)(2,1)} %hidden_ref.3) | copy-start | bytes 3145732
  0.0 14.0 %copy-start.1 = (bf16[256,512]{1,0:T(8,128)(2,1)S(1)}, bf16[256,512]{1,0:T(8,128)(2,1)}, u32[]{:S(2)}) copy-start(bf16[256,512]{1,0:T(8,128)(2,1)} %out_ref.1) | copy-start | bytes 786436
  0.0 16.7 %copy-start.2 = (bf16[512,128]{1,0:T(8,128)(2,1)S(1)}, bf16[512,128]{1,0:T(8,128)(2,1)}, u32[]{:S(2)}) copy-start(bf16[512,128]{1,0:T(8,128)(2,1)} %bc_ref.3) | copy-start | bytes 393220
  2.9 15.3 %collective-permute-start.2 = (bf16[544,256]{1,0:T(8,128)(2,1)S(1)}, bf16[544,256]{1,0:T(8,128)(2,1)S(1)}, u32[]{:S(2)}, u32[]{:S(2)}) collective-permute-start(bf16[544,256]{1,0:T(8,128)(2,1)S(1)} %get-tuple-element.31.own_ref), channel_id=1, source_target_pairs={{0,18},{18,0},{2,16},{16,2},{1,19},{19,1},{3,17},{17,3},{4,22},{22... | collective-permute-start | bytes 835592 | tf_op jit(solution)/shard_map/ppermute | solution.py:487
  6.3 11.9 %collective-permute-start = (bf16[8,512]{1,0:T(8,128)(2,1)S(1)}, bf16[8,512]{1,0:T(8,128)(2,1)S(1)}, u32[]{:S(2)}, u32[]{:S(2)}) collective-permute-start(bf16[8,512]{1,0:T(8,128)(2,1)S(1)} %get-tuple-element.28), channel_id=1, source_target_pairs={{0,4},{4,8},{8,12},{12,16},{16,20},{20,24},{24,28},{28,32},{32,36}... | collective-permute-start | bytes 24584 | tf_op jit(solution)/shard_map/ppermute | solution.py:488
  7.6 10.6 %collective-permute-start.1 = (bf16[8,512]{1,0:T(8,128)(2,1)S(1)}, bf16[8,512]{1,0:T(8,128)(2,1)S(1)}, u32[]{:S(2)}, u32[]{:S(2)}) collective-permute-start(bf16[8,512]{1,0:T(8,128)(2,1)S(1)} %get-tuple-element.29), channel_id=1, source_target_pairs={{4,0},{8,4},{12,8},{16,12},{20,16},{24,20},{28,24},{32,28},{36,32}... | collective-permute-start | bytes 24584 | tf_op jit(solution)/shard_map/ppermute | solution.py:489
  14.0 4.3 %copy-start.3 = (bf16[4,128]{1,0:T(4,128)(2,1)S(1)}, bf16[4,128]{1,0:T(4,128)(2,1)}, u32[]{:S(2)}) copy-start(bf16[4,128]{1,0:T(4,128)(2,1)} %tapbc_ref.1) | copy-start | bytes 3076
  14.0 9.4 %collective-permute-start.3 = (bf16[512,256]{1,0:T(8,128)(2,1)S(1)}, bf16[512,256]{1,0:T(8,128)(2,1)S(1)}, u32[]{:S(2)}, u32[]{:S(2)}) collective-permute-start(bf16[512,256]{1,0:T(8,128)(2,1)S(1)} %get-tuple-element.35), channel_id=1, source_target_pairs={{0,18},{18,0},{2,16},{16,2},{1,19},{19,1},{3,17},{17,3},{4,22},{22... | collective-permute-start | bytes 786440 | tf_op jit(solution)/shard_map/ppermute | solution.py:492
  14.0 13.4 %collective-permute-start.4 = (bf16[256,512]{1,0:T(8,128)(2,1)S(1)}, bf16[256,512]{1,0:T(8,128)(2,1)S(1)}, u32[]{:S(2)}, u32[]{:S(2)}) collective-permute-start(bf16[256,512]{1,0:T(8,128)(2,1)S(1)} %copy-done.1), channel_id=1, source_target_pairs={{0,18},{18,0},{2,16},{16,2},{1,19},{19,1},{3,17},{17,3},{4,22},{22... | collective-permute-start | bytes 786440 | tf_op jit(solution)/shard_map/ppermute | solution.py:493
  65.0 4.5 %collective-permute-start.5 = (bf16[512,256]{1,0:T(8,128)(2,1)S(1)}, bf16[512,256]{1,0:T(8,128)(2,1)S(1)}, u32[]{:S(2)}, u32[]{:S(2)}) collective-permute-start(bf16[512,256]{1,0:T(8,128)(2,1)S(1)} %get-tuple-element.46), channel_id=1, source_target_pairs={{0,1},{1,0},{2,3},{3,2},{4,5},{5,4},{6,7},{7,6},{8,9},{9,8},{10,11... | collective-permute-start | bytes 786440 | tf_op jit(solution)/shard_map/ppermute | solution.py:550

commit v6 on v5

--- a/solution.py
+++ b/solution.py
@@ -523,16 +523,23 @@
             pltpu.VMEM((2 * inner // LANES + 1, rows + 2 * HALO, LANES), F32),
         ],
     )(place, u, main, prev, following, pack, other_pack, proj_bc, conv_bc)
-    send, other_z, other_out = lax.optimization_barrier((send, other_z, other_out))
-    got = lax.all_to_all(send, SEQ, 0, 0, tiled=True)
-    scanned = call(
-        scan_kernel,
-        struct((count, 8, LANES), BF16),
-        [SMEM, VMEM],
-        VMEM,
-        cost(1_000_000, 0, 400_000),
-    )(place, got)
-    came = lax.all_to_all(scanned, SEQ, 0, 0, tiled=True)
+    def passed_on(place, send, *others):
+        got = lax.all_to_all(send, SEQ, 0, 0, tiled=True)
+        scanned = call(
+            scan_kernel,
+            struct((count, 8, LANES), BF16),
+            [SMEM, VMEM],
+            VMEM,
+            cost(1_000_000, 0, 400_000),
+        )(place, got)
+        return lax.all_to_all(scanned, SEQ, 0, 0, tiled=True), *others
+
+    came, y, c, cols, first, gains, own_gate, own_w, u = lax.cond(
+        core < 2,
+        passed_on,
+        lambda place, send, *others: (send[:, :8], *[-other for other in others]),
+        place, send, y, c, cols, first, gains, own_gate, own_w, u,
+    )
 
     keep, give = call(
         back_kernel,

time: 70.5 us -> 67.6 us (0.959)
  waiting for transfers between devices: 5.13 us -> 1.18 us
  blocking collectives: 34.3 us -> 31.9 us
  Pallas kernels: 11.4 us -> 12.9 us
  starting transfers between devices: 17.1 us -> 18.4 us
  local copies, waits for them, and re-layouts: 1.28 us -> 2.02 us
    ppermute x1, waiting for transfers between devices: 3.95 us -> 0.01 us  [shards(): other_out = lax.ppermute(own_out, *beside)]
    all_to_all x2, blocking collectives: 34.3 us -> 31.9 us  [the longest x1 17.6 us: passed_on(): got = lax.all_to_all(send, SEQ, 0, 0, tiled=True)]
    ppermute x1, starting transfers between devices: 3.38 us -> 4.65 us  [shards(): taken = lax.ppermute(give, 'core', swap)]
    pallas_call x1, Pallas kernels: 1.54 us -> 2.46 us  [shards(): call(early_kernel, (struct((rows, width), BF16), struct((rows, inner + LA...]
    slice x1, local copies, waits for them, and re-layouts: 0.04 us -> 0.75 us  [shards(): zx[:, :inner]]
  transfers between devices with their start and end apart: 6 -> 6, of which waited for: 2 -> 1; matrix products, arithmetic and copies ran while one was open for 0% -> 0% of each run, Pallas kernels for 10% -> 13%
where the time goes in v6:
time: 67.6 us; the launch traced here: 67.4 us
  blocking collectives  31.9 us (47%)
  starting transfers between devices  18.4 us (27%)
  Pallas kernels  12.9 us (19%)
  local copies, waits for them, and re-layouts  2.02 us (3%)
  waiting for transfers between devices  1.18 us (2%)
  other arithmetic  0.83 us (1%)
    all_to_all x1, blocking collectives, passed_on(): got = lax.all_to_all(send, SEQ, 0, 0, tiled=True)  17.6 us
    all_to_all x1, blocking collectives, passed_on(): return (lax.all_to_all(scanned, SEQ, 0, 0, tiled=True), *others)  14.3 us
    ppermute x1, starting transfers between devices, shards(): following = lax.ppermute(head, SEQ, fall)  6.39 us
    pallas_call x1, Pallas kernels, shards(): call(front_kernel, (struct((2, rows, 2 * inner), F32), struct((2, rows, L...  5.74 us
    ppermute x1, starting transfers between devices, shards(): taken = lax.ppermute(give, 'core', swap)  4.65 us
    ppermute x1, starting transfers between devices, shards(): other_pack = lax.ppermute(pack, *beside)  3.39 us
    ppermute x1, starting transfers between devices, shards(): other_out = lax.ppermute(own_out, *beside)  2.67 us
    pallas_call x1, Pallas kernels, shards(): call(back_kernel, (struct((rows, inner), F32), struct((rows, inner), BF16...  2.48 us
  transfers between devices with their start and end apart: 6, of which 1 were waited for; matrix products, arithmetic and copies ran while one was open for 0% of the time, Pallas kernels for 13%

profile of v6, /device:TPU:1, one launch (start us, length us, event | category | flops | bytes accessed | tf_op | source)
XLA Modules:
  0.0 67.4 jit_solution(14331629180661522855)
XLA Ops:
  0.0 1.2 %copy.12 = bf16[64,8,2,256]{3,1,2,0:T(8,128)(2,1)S(1)} copy(bf16[64,8,2,256]{3,2,1,0:T(2,128)(2,1)} %bitcast.12) | data formatting | bytes 1048576
  1.3 0.8 %fusion = (bf16[512,256]{1,0:T(8,128)(2,1)}, bf16[512,256]{1,0:T(8,128)(2,1)S(1)}) fusion(bf16[512,512]{1,0:T(8,128)(2,1)S(1)} %bitcast.10), kind=kLoop, calls=%fused_computation.2 | loop fusion | bytes 1048576 | tf_op jit(solution)/shard_map/slice | solution.py:491
  2.0 0.1 pad_add_fusion.place_ref
  2.1 1.5 %shard_map.110 = (bf16[544,256]{1,0:T(8,128)(2,1)S(1)}, bf16[8,512]{1,0:T(8,128)(2,1)S(1)}, bf16[8,512]{1,0:T(8,128)(2,1)S(1)}) custom-call(s32[4]{0:T(128)S(1)} %pad_add_fusion.place_ref, bf16[512,256]{1,0:T(8,128)(2,1)S(1)} %get-tuple-element.117.x_ref, bf16[4,512]{1,0:T(4,128)(2,1)} %bitcast.13, bf16[4,256]{1,0:T(4,128)(2,1)} %taps_hbm.1, ...), custom_call_target="tpu_custom_call" | custom-call | flops 1000000 | bytes 1000000 | tf_op jit(solution)/shard_map/pallas_call | solution.py:454
  3.6 3.4 %collective-permute-start.2 = (bf16[544,256]{1,0:T(8,128)(2,1)S(1)}, bf16[544,256]{1,0:T(8,128)(2,1)S(1)}, u32[]{:S(2)}, u32[]{:S(2)}) collective-permute-start(bf16[544,256]{1,0:T(8,128)(2,1)S(1)} %get-tuple-element.94.own_ref), channel_id=1, source_target_pairs={{0,18},{18,0},{2,16},{16,2},{1,19},{19,1},{3,17},{17,3},{4,22},{22... | collective-permute-start | bytes 835592 | tf_op jit(solution)/shard_map/ppermute | solution.py:487
  7.0 1.3 %collective-permute-start = (bf16[8,512]{1,0:T(8,128)(2,1)S(1)}, bf16[8,512]{1,0:T(8,128)(2,1)S(1)}, u32[]{:S(2)}, u32[]{:S(2)}) collective-permute-start(bf16[8,512]{1,0:T(8,128)(2,1)S(1)} %get-tuple-element.91), channel_id=1, source_target_pairs={{0,4},{4,8},{8,12},{12,16},{16,20},{20,24},{24,28},{28,32},{32,36}... | collective-permute-start | bytes 24584 | tf_op jit(solution)/shard_map/ppermute | solution.py:488
  8.3 6.4 %collective-permute-start.1 = (bf16[8,512]{1,0:T(8,128)(2,1)S(1)}, bf16[8,512]{1,0:T(8,128)(2,1)S(1)}, u32[]{:S(2)}, u32[]{:S(2)}) collective-permute-start(bf16[8,512]{1,0:T(8,128)(2,1)S(1)} %get-tuple-element.92), channel_id=1, source_target_pairs={{4,0},{8,4},{12,8},{16,12},{20,16},{24,20},{28,24},{32,28},{36,32}... | collective-permute-start | bytes 24584 | tf_op jit(solution)/shard_map/ppermute | solution.py:489
  14.7 0.0 collective-permute-start.3
  14.7 0.0 copy-done.1
  14.7 2.7 %collective-permute-start.4 = (bf16[256,512]{1,0:T(8,128)(2,1)S(1)}, bf16[256,512]{1,0:T(8,128)(2,1)S(1)}, u32[]{:S(2)}, u32[]{:S(2)}) collective-permute-start(bf16[256,512]{1,0:T(8,128)(2,1)S(1)} %copy-done.1), channel_id=1, source_target_pairs={{0,18},{18,0},{2,16},{16,2},{1,19},{19,1},{3,17},{17,3},{4,22},{22... | collective-permute-start | bytes 786440 | tf_op jit(solution)/shard_map/ppermute | solution.py:493
  17.4 0.0 copy-done
  17.4 0.0 copy-done.2
  17.4 2.5 %shard_map.109 = (bf16[512,512]{1,0:T(8,128)(2,1)}, bf16[512,384]{1,0:T(8,128)(2,1)S(1)}, f32[512,256]{1,0:T(8,128)}, bf16[256,512]{1,0:T(8,128)(2,1)}) custom-call(s32[4]{0:T(128)S(1)} %pad_add_fusion.place_ref, bf16[512,1024]{1,0:T(8,128)(2,1)S(1)} %copy-done, bf16[512,512]{1,0:T(8,128)(2,1)S(1)} %bitcast.11, bf16[512,128]{1,0:T(8,128)(2,1)S(1)} %copy-done.2, ...), custom_call_target="tpu_custom_call" | custom-call | flops 2000000000 | bytes 4000000 | tf_op jit(solution)/shard_map/pallas_call | solution.py:494
  19.8 0.0 collective-permute-done.prev_ref
  19.9 0.0 collective-permute-done.1.next_ref
  19.9 0.0 collective-permute-done.2.other_ref
  19.9 0.0 copy-done.3
  19.9 0.0 copy-start.4
  19.9 0.0 copy-start.5
  19.9 0.0 copy-start.6
  19.9 5.7 %shard_map.111 = (f32[2,512,512]{2,1,0:T(8,128)S(1)}, bf16[2,512,128]{2,1,0:T(8,128)(2,1)S(1)}, f32[512,128]{1,0:T(8,128)S(1)}, f32[2,64,512]{2,1,0:T(8,128)S(1)...) custom-call(s32[4]{0:T(128)S(1)} %pad_add_fusion.place_ref, bf16[512,512]{1,0:T(8,128)(2,1)} %get-tuple-element.89.u_ref, ...), custom_call_target="tpu_custom_call" | custom-call | flops 8000000000 | bytes 24000000 | tf_op jit(solution)/shard_map/pallas_call | solution.py:506
  25.7 0.0 copy-done.4
  25.7 32.6 %conditional.1 = (bf16[64,8,128]{2,1,0:T(8,128)(2,1)S(1)}, f32[2,512,512]{2,1,0:T(8,128)S(1)}, bf16[2,512,128]{2,1,0:T(8,128)(2,1)S(1)}, f32[512,128]{1,0:T(8,12...) conditional(s32[]{:T(128)} %convert_element_type.9, ...), branch_computations={%region_0.0_spmd, %region_1.0_spmd} | conditional | flops 1000000 | bytes 8683592 | solution.py:537
  25.7 17.6 %all_to_all.8.got_ref = bf16[64,16,128]{2,1,0:T(8,128)(2,1)S(1)} all-to-all(bf16[64,16,128]{2,1,0:T(8,128)(2,1)S(1)} %get-tuple-element.53), channel_id=1, replica_groups=mesh['seq_0'=8,'seq_1'=2,'seq_2'=4,'x_hi'=2,'core'=2] {'seq_0','seq_1','..., dimensions={0} | all-to-all | bytes 524288 | tf_op jit(solution)/shard_map/cond/branch_1_fun/all_to_all | solution.py:527
  43.3 0.7 %branch_1_fun.1 = bf16[64,8,128]{2,1,0:T(8,128)(2,1)S(1)} custom-call(s32[4]{0:T(128)S(1)} %get-tuple-element.52.place_ref, bf16[64,16,128]{2,1,0:T(8,128)(2,1)S(1)} %all_to_all.8.got_ref), custom_call_target="tpu_custom_call" | custom-call | flops 1000000 | bytes 400000 | tf_op jit(solution)/shard_map/cond/branch_1_fun/pallas_call | solution.py:528
  44.0 14.3 %all_to_all.9 = bf16[64,8,128]{2,1,0:T(8,128)(2,1)S(1)} all-to-all(bf16[64,8,128]{2,1,0:T(8,128)(2,1)S(1)} %branch_1_fun.1), channel_id=1, replica_groups=mesh['seq_0'=8,'seq_1'=2,'seq_2'=4,'x_hi'=2,'core'=2] {'seq_0','seq_1','..., dimensions={0} | all-to-all | bytes 262144 | tf_op jit(solution)/shard_map/cond/branch_1_fun/all_to_all | solution.py:535
  58.3 0.0 collective-permute-done.3.other_z_ref
  58.3 0.0 collective-permute-done.4.other_out_ref
  58.3 2.5 %shard_map.112 = (f32[512,256]{1,0:T(8,128)S(1)}, bf16[512,256]{1,0:T(8,128)(2,1)S(1)}) custom-call(s32[4]{0:T(128)S(1)} %pad_add_fusion.place_ref, f32[2,512,512]{2,1,0:T(8,128)S(1)} %get-tuple-element.103.y_ref, bf16[2,512,128]{2,1,0:T(8,128)(2,1)S(1)} %get-tuple-element.104.c_ref, bf16[64,8,128]{2,1,0:T(8,128)(2,1)S(1)} %get-tuple-element.105.came_ref, ...), custom_call_target="tpu_custom_call" | custom-call | flops 2000000000 | bytes 6000000 | tf_op jit(solution)/shard_map/pallas_call | solution.py:544
  60.8 4.6 %collective-permute-start.5 = (bf16[512,256]{1,0:T(8,128)(2,1)S(1)}, bf16[512,256]{1,0:T(8,128)(2,1)S(1)}, u32[]{:S(2)}, u32[]{:S(2)}) collective-permute-start(bf16[512,256]{1,0:T(8,128)(2,1)S(1)} %get-tuple-element.115), channel_id=1, source_target_pairs={{0,1},{1,0},{2,3},{3,2},{4,5},{5,4},{6,7},{7,6},{8,9},{9,8},{10,11... | collective-permute-start | bytes 786440 | tf_op jit(solution)/shard_map/ppermute | solution.py:557
  65.5 1.2 %collective-permute-done.5 = bf16[512,256]{1,0:T(8,128)(2,1)S(1)} collective-permute-done((bf16[512,256]{1,0:T(8,128)(2,1)S(1)}, bf16[512,256]{1,0:T(8,128)(2,1)S(1)}, u32[]{:S(2)}, u32[]{:S(2)}) %collective-permute-start.5) | collective-permute-done | bytes 262176 | tf_op jit(solution)/shard_map/ppermute | solution.py:557
  66.6 0.8 %add_convert_fusion = bf16[512,256]{1,0:T(8,128)(2,1)} fusion(f32[512,256]{1,0:T(8,128)S(1)} %get-tuple-element.114, bf16[512,256]{1,0:T(8,128)(2,1)S(1)} %collective-permute-done.5), kind=kLoop, calls=%fused_computation | loop fusion | flops 393216 | bytes 1048576 | tf_op jit(solution)/shard_map/convert_element_type | solution.py:558
  (6 shorter events, 0.0 us)
Async XLA Ops:
  0.0 17.4 %copy-start = (bf16[512,1024]{1,0:T(8,128)(2,1)S(1)}, bf16[512,1024]{1,0:T(8,128)(2,1)}, u32[]{:S(2)}) copy-start(bf16[512,1024]{1,0:T(8,128)(2,1)} %hidden_ref.3) | copy-start | bytes 3145732
  0.0 14.7 %copy-start.1 = (bf16[256,512]{1,0:T(8,128)(2,1)S(1)}, bf16[256,512]{1,0:T(8,128)(2,1)}, u32[]{:S(2)}) copy-start(bf16[256,512]{1,0:T(8,128)(2,1)} %out_ref.1) | copy-start | bytes 786436
  0.0 17.4 %copy-start.2 = (bf16[512,128]{1,0:T(8,128)(2,1)S(1)}, bf16[512,128]{1,0:T(8,128)(2,1)}, u32[]{:S(2)}) copy-start(bf16[512,128]{1,0:T(8,128)(2,1)} %bc_ref.3) | copy-start | bytes 393220
  3.6 16.2 %collective-permute-start.2 = (bf16[544,256]{1,0:T(8,128)(2,1)S(1)}, bf16[544,256]{1,0:T(8,128)(2,1)S(1)}, u32[]{:S(2)}, u32[]{:S(2)}) collective-permute-start(bf16[544,256]{1,0:T(8,128)(2,1)S(1)} %get-tuple-element.94.own_ref), channel_id=1, source_target_pairs={{0,18},{18,0},{2,16},{16,2},{1,19},{19,1},{3,17},{17,3},{4,22},{22... | collective-permute-start | bytes 835592 | tf_op jit(solution)/shard_map/ppermute | solution.py:487
  7.0 12.8 %collective-permute-start = (bf16[8,512]{1,0:T(8,128)(2,1)S(1)}, bf16[8,512]{1,0:T(8,128)(2,1)S(1)}, u32[]{:S(2)}, u32[]{:S(2)}) collective-permute-start(bf16[8,512]{1,0:T(8,128)(2,1)S(1)} %get-tuple-element.91), channel_id=1, source_target_pairs={{0,4},{4,8},{8,12},{12,16},{16,20},{20,24},{24,28},{28,32},{32,36}... | collective-permute-start | bytes 24584 | tf_op jit(solution)/shard_map/ppermute | solution.py:488
  8.3 11.5 %collective-permute-start.1 = (bf16[8,512]{1,0:T(8,128)(2,1)S(1)}, bf16[8,512]{1,0:T(8,128)(2,1)S(1)}, u32[]{:S(2)}, u32[]{:S(2)}) collective-permute-start(bf16[8,512]{1,0:T(8,128)(2,1)S(1)} %get-tuple-element.92), channel_id=1, source_target_pairs={{4,0},{8,4},{12,8},{16,12},{20,16},{24,20},{28,24},{32,28},{36,32}... | collective-permute-start | bytes 24584 | tf_op jit(solution)/shard_map/ppermute | solution.py:489
  14.7 5.2 %copy-start.3 = (bf16[4,128]{1,0:T(4,128)(2,1)S(1)}, bf16[4,128]{1,0:T(4,128)(2,1)}, u32[]{:S(2)}) copy-start(bf16[4,128]{1,0:T(4,128)(2,1)} %tapbc_ref.1) | copy-start | bytes 3076
  14.7 43.6 %collective-permute-start.3 = (bf16[512,256]{1,0:T(8,128)(2,1)}, bf16[512,256]{1,0:T(8,128)(2,1)S(1)}, u32[]{:S(2)}, u32[]{:S(2)}) collective-permute-start(bf16[512,256]{1,0:T(8,128)(2,1)} %get-tuple-element.112), channel_id=1, source_target_pairs={{0,18},{18,0},{2,16},{16,2},{1,19},{19,1},{3,17},{17,3},{4,22},{22... | collective-permute-start | bytes 786440 | tf_op jit(solution)/shard_map/ppermute | solution.py:492
  14.7 43.6 %collective-permute-start.4 = (bf16[256,512]{1,0:T(8,128)(2,1)S(1)}, bf16[256,512]{1,0:T(8,128)(2,1)S(1)}, u32[]{:S(2)}, u32[]{:S(2)}) collective-permute-start(bf16[256,512]{1,0:T(8,128)(2,1)S(1)} %copy-done.1), channel_id=1, source_target_pairs={{0,18},{18,0},{2,16},{16,2},{1,19},{19,1},{3,17},{17,3},{4,22},{22... | collective-permute-start | bytes 786440 | tf_op jit(solution)/shard_map/ppermute | solution.py:493
  19.9 5.8 %copy-start.4 = (bf16[512,512]{1,0:T(8,128)(2,1)S(1)}, bf16[512,512]{1,0:T(8,128)(2,1)}, u32[]{:S(2)}) copy-start(bf16[512,512]{1,0:T(8,128)(2,1)} %get-tuple-element.89.u_ref) | copy-start | bytes 1572868
  19.9 5.8 %copy-start.5 = (f32[512,256]{1,0:T(8,128)S(1)}, f32[512,256]{1,0:T(8,128)}, u32[]{:S(2)}) copy-start(f32[512,256]{1,0:T(8,128)} %get-tuple-element.101) | copy-start | bytes 1572868
  19.9 5.8 %copy-start.6 = (bf16[256,512]{1,0:T(8,128)(2,1)S(1)}, bf16[256,512]{1,0:T(8,128)(2,1)}, u32[]{:S(2)}) copy-start(bf16[256,512]{1,0:T(8,128)(2,1)} %get-tuple-element.102) | copy-start | bytes 786436
  60.8 5.8 %collective-permute-start.5 = (bf16[512,256]{1,0:T(8,128)(2,1)S(1)}, bf16[512,256]{1,0:T(8,128)(2,1)S(1)}, u32[]{:S(2)}, u32[]{:S(2)}) collective-permute-start(bf16[512,256]{1,0:T(8,128)(2,1)S(1)} %get-tuple-element.115), channel_id=1, source_target_pairs={{0,1},{1,0},{2,3},{3,2},{4,5},{5,4},{6,7},{7,6},{8,9},{9,8},{10,11... | collective-permute-start | bytes 786440 | tf_op jit(solution)/shard_map/ppermute | solution.py:557

commit v7 on v6

--- a/solution.py
+++ b/solution.py
@@ -97,8 +97,8 @@
 
 
 def pack_kernel(
-    place_ref, x_ref, dt_hbm, taps_hbm, bias_hbm, exp_hbm, skip_hbm, gain_hbm, hidden_hbm,
-    pack_ref, head_ref, tail_ref,
+    place_ref, zx_ref, dt_hbm, taps_hbm, bias_hbm, exp_hbm, skip_hbm, gain_hbm, hidden_hbm, out_hbm,
+    pack_ref, late_ref, head_ref, tail_ref,
     dt_ref, taps_ref, bias_ref, exp_ref, skip_ref, gain_ref, sems,
 ):
     inner, heads = pack_ref.shape[1], dt_ref.shape[0]
@@ -114,10 +114,13 @@
             (gain_hbm, gain_ref),
             (hidden_hbm.at[pl.ds(0, HALO), columns], head_ref),
             (hidden_hbm.at[pl.ds(rows - HALO, HALO), columns], tail_ref),
+            (out_hbm.at[:, :inner], late_ref.at[:inner, inner:]),
+            (out_hbm.at[:, inner:], late_ref.at[inner:, inner:]),
         ),
         sems,
     )
-    pack_ref[:DT_AT] = x_ref[...]
+    pack_ref[:DT_AT] = zx_ref[:, inner:]
+    late_ref[:, :inner] = zx_ref[:, :inner]
     for copy in copies:
         copy.wait()
     lane = iota((1, inner), 1)
@@ -155,13 +158,13 @@
     )
 
 
-def turned_out(place_ref, out_ref):
-    columns = out_ref.shape[1]
+def turned_out(place_ref, out):
+    columns = out.shape[1]
     part = columns // 2
     source, target = iota((columns, columns), 0), iota((columns, columns), 1)
     column = jnp.where(target < part, target + place_ref[1] * part, target - place_ref[1] * part)
     wanted = jnp.where(place_ref[0] == 0, column, columns - 1 - column)
-    return dot(out_ref[...], (source == wanted).astype(BF16)).astype(BF16)
+    return dot(out, (source == wanted).astype(BF16)).astype(BF16)
 
 
 def gated_by(u, w):
@@ -169,33 +172,23 @@
     return z * sigmoid(z)
 
 
-def early_kernel(
-    place_ref, hidden_ref, zx_ref, bc_ref, out_ref, u_ref, main_ref, gate_ref, w_ref
-):
-    width, inner = zx_ref.shape[0], zx_ref.shape[1] // 2
-    strand = place_ref[0]
-    u = hidden_ref[:, pl.ds(pl.multiple_of(strand * width, width), width)]
-    u = dot(u, orient(width, strand)).astype(BF16)
-    u_ref[...] = u
-    main_ref[:, :inner] = dot(u, zx_ref[:, inner:]).astype(BF16)
-    main_ref[:, inner:] = dot(u, bc_ref[...]).astype(BF16)
-    gate_ref[...] = gated_by(u, zx_ref[:, :inner])
-    w_ref[...] = turned_out(place_ref, out_ref)
-
-
 def front_kernel(
-    place_ref, u_ref, main_ref, prev_ref, next_ref, own_ref, other_ref, bc_ref, tapbc_ref,
-    y_ref, c_ref, cols_ref, first_ref, gains_ref, send_ref,
+    place_ref, hidden_ref, zx_ref, prev_ref, next_ref, own_ref, other_ref, bc_ref, tapbc_ref,
+    u_ref, gate_ref, y_ref, c_ref, cols_ref, first_ref, gains_ref, send_ref,
     x_ref, b_ref, rows_ref, pad_ref,
 ):
-    row_count, width = u_ref.shape
+    row_count, width = hidden_ref.shape[0], hidden_ref.shape[1] // 2
     inner = own_ref.shape[1]
     strand, position, count = place_ref[0], place_ref[2], place_ref[3]
     packs = (own_ref, other_ref)
-    u = u_ref[...]
+    turn = orient(width, strand)
+    u = hidden_ref[:, pl.ds(pl.multiple_of(strand * width, width), width)]
+    u = dot(u, turn).astype(BF16)
+    u_ref[...] = u
+    gate_ref[...] = gated_by(u, zx_ref[:, :inner])
     before = jnp.where(position > 0, prev_ref[...].astype(F32), 0.0)
     after = jnp.where(position < count - 1, next_ref[...].astype(F32), 0.0)
-    edge = dot(jnp.concatenate([before, after], axis=0).astype(BF16), orient(width, strand))
+    edge = dot(jnp.concatenate([before, after], axis=0).astype(BF16), turn)
     edge = edge.astype(BF16)
 
     raw = jnp.concatenate(
@@ -249,11 +242,7 @@
     tiles = inner // LANES
     for g in range(3):
         w = packs[g][:DT_AT] if g < 2 else bc_ref[...]
-        if g == 1:
-            middle = dot(u, w).astype(BF16)
-        else:
-            middle = main_ref[:, :inner] if g == 0 else main_ref[:, inner:]
-        middle = middle.astype(F32)
+        middle = dot(u, w).astype(BF16).astype(F32)
         outer = dot(edge, w).astype(BF16).astype(F32)
         for k in range(w.shape[1] // LANES):
             at, lanes = g * tiles + k, slice(k * LANES, (k + 1) * LANES)
@@ -380,15 +369,17 @@
 
 
 def back_kernel(
-    place_ref, y_ref, c_ref, came_ref, first_ref, cols_ref, gains_ref, own_gate_ref, own_w_ref,
-    u_ref, other_z_ref, other_out_ref, hidden_ref, keep_ref, give_ref, state_ref, w_ref,
+    place_ref, y_ref, c_ref, came_ref, first_ref, cols_ref, gains_ref, own_gate_ref, u_ref,
+    own_out_ref, late_ref, hidden_ref, keep_ref, give_ref, state_ref, w_ref,
 ):
-    part = own_w_ref.shape[1] // 2
+    part = own_out_ref.shape[1] // 2
     inner = y_ref.shape[2] // 2
     ours = pl.multiple_of((2 * place_ref[0] + place_ref[1]) * part, part)
     blocks = [slice(b * BLOCK, (b + 1) * BLOCK) for b in range(2)]
-    w_ref[:inner] = own_w_ref[...]
-    w_ref[inner:] = turned_out(place_ref, other_out_ref)
+    w_ref[:inner] = turned_out(place_ref, own_out_ref[...])
+    w_ref[inner:] = turned_out(
+        place_ref, jnp.concatenate([late_ref[:inner, inner:], late_ref[inner:, inner:]], axis=1)
+    )
     same = (iota((inner, inner), 0) // HEADP == iota((inner, inner), 1) // HEADP).astype(BF16)
     for way in range(2):
         for n in range(8):
@@ -399,7 +390,7 @@
     for b, block in enumerate(blocks):
         decays = jnp.exp2(cols_ref[block])
         gate = jnp.concatenate(
-            [own_gate_ref[block, :], gated_by(u_ref[block, :], other_z_ref[...])], axis=1
+            [own_gate_ref[block, :], gated_by(u_ref[block, :], late_ref[:, :inner])], axis=1
         )
         total = None
         for way in range(2):
@@ -451,15 +442,16 @@
     place = jnp.stack([x_hi, core, lax.axis_index(SEQ), jnp.int32(count)]).astype(jnp.int32)
     zx = proj_zx.reshape(width, 2 * inner)
 
-    pack, head, tail = call(
+    pack, late, head, tail = call(
         pack_kernel,
         (
             struct((PACKED, inner), BF16),
+            struct((width, 2 * inner), BF16),
             struct((HALO, width), BF16),
             struct((HALO, width), BF16),
         ),
-        [SMEM, VMEM] + [HBM] * 7,
-        (VMEM,) * 3,
+        [SMEM, VMEM] + [HBM] * 8,
+        (VMEM,) * 4,
         cost(1_000_000, 0, 1_000_000),
         scratch=[
             pltpu.VMEM((4, width), BF16),
@@ -468,11 +460,11 @@
             pltpu.VMEM((1, 4), jnp.int32),
             pltpu.VMEM((1, 4), F32),
             pltpu.VMEM((1, inner), F32),
-            dma(8),
+            dma(10),
         ],
     )(
         place,
-        zx[:, inner:],
+        zx,
         *lying(
             proj_dt.T,
             conv_x,
@@ -481,6 +473,7 @@
             skip_gain.reshape(1, 4),
             norm_gain.reshape(1, inner),
             hidden_in,
+            out_proj,
         ),
     )
     beside = (("seq_1", "x_hi"), [(0, 3), (3, 0), (1, 2), (2, 1)])
@@ -488,24 +481,12 @@
     prev = lax.ppermute(tail, SEQ, rise)
     following = lax.ppermute(head, SEQ, fall)
 
-    own_z, own_out, pack = lax.optimization_barrier((zx[:, :inner], out_proj, pack))
-    other_z = lax.ppermute(own_z, *beside)
-    other_out = lax.ppermute(own_out, *beside)
-    u, main, own_gate, own_w = call(
-        early_kernel,
+    other_late = lax.ppermute(late, *beside)
+    u, own_gate, y, c, cols, first, gains, send = call(
+        front_kernel,
         (
             struct((rows, width), BF16),
-            struct((rows, inner + LANES), BF16),
             struct((rows, inner), F32),
-            struct((inner, 2 * inner), BF16),
-        ),
-        [SMEM] + [VMEM] * 4,
-        (VMEM,) * 4,
-        cost(2_000_000_000, 130_000, 4_000_000),
-    )(place, hidden_in, zx, proj_bc, out_proj)
-    y, c, cols, first, gains, send = call(
-        front_kernel,
-        (
             struct((2, rows, 2 * inner), F32),
             struct((2, rows, LANES), BF16),
             struct((rows, LANES), F32),
@@ -514,7 +495,7 @@
             struct((count, 16, LANES), BF16),
         ),
         [SMEM] + [VMEM] * 8,
-        (VMEM,) * 6,
+        (VMEM,) * 8,
         cost(8_000_000_000, 3_000_000, 24_000_000),
         scratch=[
             pltpu.VMEM((2, rows, 2 * inner), BF16),
@@ -522,7 +503,7 @@
             pltpu.VMEM((48, rows), F32),
             pltpu.VMEM((2 * inner // LANES + 1, rows + 2 * HALO, LANES), F32),
         ],
-    )(place, u, main, prev, following, pack, other_pack, proj_bc, conv_bc)
+    )(place, hidden_in, zx, prev, following, pack, other_pack, proj_bc, conv_bc)
     def passed_on(place, send, *others):
         got = lax.all_to_all(send, SEQ, 0, 0, tiled=True)
         scanned = call(
@@ -534,17 +515,17 @@
         )(place, got)
         return lax.all_to_all(scanned, SEQ, 0, 0, tiled=True), *others
 
-    came, y, c, cols, first, gains, own_gate, own_w, u = lax.cond(
+    came, y, c, cols, first, gains, own_gate, u = lax.cond(
         core < 2,
         passed_on,
         lambda place, send, *others: (send[:, :8], *[-other for other in others]),
-        place, send, y, c, cols, first, gains, own_gate, own_w, u,
+        place, send, y, c, cols, first, gains, own_gate, u,
     )
 
     keep, give = call(
         back_kernel,
         (struct((rows, inner), F32), struct((rows, inner), BF16)),
-        [SMEM] + [VMEM] * 12,
+        [SMEM] + [VMEM] * 11,
         (VMEM, VMEM),
         cost(2_000_000_000, 600_000, 6_000_000),
         scratch=[
@@ -552,7 +533,7 @@
             pltpu.VMEM((2 * inner, 2 * inner), BF16),
         ],
     )(
-        place, y, c, came, first, cols, gains, own_gate, own_w, u, other_z, other_out, hidden_in
+        place, y, c, came, first, cols, gains, own_gate, u, out_proj, other_late, hidden_in
     )
     taken = lax.ppermute(give, "core", swap)
     return (keep + taken.astype(F32)).astype(BF16)

time: 67.6 us -> 66.8 us (0.988)
  blocking collectives: 31.9 us -> 35.4 us
  starting transfers between devices: 18.4 us -> 16.1 us
  Pallas kernels: 12.9 us -> 10.8 us
  waiting for transfers between devices: 1.18 us -> 2.2 us
  local copies, waits for them, and re-layouts: 2.02 us -> 1.24 us
    all_to_all x1, blocking collectives: 17.6 us -> 21.1 us  [passed_on(): got = lax.all_to_all(send, SEQ, 0, 0, tiled=True)]
    ppermute x2 -> x1, starting transfers between devices: 2.68 us -> 0.01 us  [shards(): other_late = lax.ppermute(late, *beside)]
    pallas_call x3 -> x2, Pallas kernels: 9.72 us -> 7.56 us  [the longest x1 5.74 us: shards(): call(front_kernel, (struct((rows, width), BF16), struct((rows, inner), F3...]
    ppermute x1, waiting for transfers between devices: 0.01 us -> 1.03 us  [shards(): prev = lax.ppermute(tail, SEQ, rise)]
    slice x1 -> x0, local copies, waits for them, and re-layouts: 0.75 us -> none  [shards(): zx[:, :inner]]
  transfers between devices with their start and end apart: 6 -> 5, of which waited for: 1 -> 2; matrix products, arithmetic and copies ran while one was open for 0% -> 0% of each run, Pallas kernels for 13% -> 10%
where the time goes in v7:
time: 66.8 us; the launch traced here: 66.6 us
  blocking collectives  35.4 us (53%)
  starting transfers between devices  16.1 us (24%)
  Pallas kernels  10.8 us (16%)
  waiting for transfers between devices  2.2 us (3%)
  local copies, waits for them, and re-layouts  1.24 us (2%)
  other arithmetic  0.84 us (1%)
    all_to_all x1, blocking collectives, passed_on(): got = lax.all_to_all(send, SEQ, 0, 0, tiled=True)  21.1 us
    all_to_all x1, blocking collectives, passed_on(): return (lax.all_to_all(scanned, SEQ, 0, 0, tiled=True), *others)  14.3 us
    ppermute x1, starting transfers between devices, shards(): following = lax.ppermute(head, SEQ, fall)  6.39 us
    pallas_call x1, Pallas kernels, shards(): call(front_kernel, (struct((rows, width), BF16), struct((rows, inner), F3...  5.74 us
    ppermute x1, starting transfers between devices, shards(): taken = lax.ppermute(give, 'core', swap)  5 us
    ppermute x1, starting transfers between devices, shards(): other_pack = lax.ppermute(pack, *beside)  3.39 us
    pallas_call x1, Pallas kernels, shards(): call(back_kernel, (struct((rows, inner), F32), struct((rows, inner), BF16...  2.55 us
    pallas_call x1, Pallas kernels, shards(): call(pack_kernel, (struct((PACKED, inner), BF16), struct((width, 2 * inne...  1.82 us
  transfers between devices with their start and end apart: 5, of which 2 were waited for; matrix products, arithmetic and copies ran while one was open for 0% of the time, Pallas kernels for 10%

profile of v7, /device:TPU:1, one launch (start us, length us, event | category | flops | bytes accessed | tf_op | source)
XLA Modules:
  0.0 66.6 jit_solution(10920523269031605592)
XLA Ops:
  0.0 0.0 copy-start
  0.0 0.0 copy-start.3
  0.0 0.0 copy-start.2
  0.0 1.2 %copy.12 = bf16[64,8,2,256]{3,1,2,0:T(8,128)(2,1)S(1)} copy(bf16[64,8,2,256]{3,2,1,0:T(2,128)(2,1)} %bitcast.12) | data formatting | bytes 1048576
  1.3 0.1 pad_add_fusion.place_ref
  1.3 1.8 %shard_map.109 = (bf16[544,256]{1,0:T(8,128)(2,1)S(1)}, bf16[512,512]{1,0:T(8,128)(2,1)S(1)}, bf16[8,512]{1,0:T(8,128)(2,1)S(1)}, bf16[8,512]{1,0:T(8,128)(2,1)S(1)}) custom-call(s32[4]{0:T(128)S(1)} %pad_add_fusion.place_ref, bf16[512,512]{1,0:T(8,128)(2,1)S(1)} %bitcast.10, bf16[4,512]{1,0:T(4,128)(2,1)} %bitcast.13, bf16[4,256]{1,0:T(4,128)(2,1)} %taps_hbm.1, ...), custom_call_target="tpu_custom_call" | custom-call | flops 1000000 | bytes 1000000 | tf_op jit(solution)/shard_map/pallas_call | solution.py:445
  3.2 3.4 %collective-permute-start.2 = (bf16[544,256]{1,0:T(8,128)(2,1)S(1)}, bf16[544,256]{1,0:T(8,128)(2,1)S(1)}, u32[]{:S(2)}, u32[]{:S(2)}) collective-permute-start(bf16[544,256]{1,0:T(8,128)(2,1)S(1)} %get-tuple-element.80.own_ref), channel_id=1, source_target_pairs={{0,18},{18,0},{2,16},{16,2},{1,19},{19,1},{3,17},{17,3},{4,22},{22... | collective-permute-start | bytes 835592 | tf_op jit(solution)/shard_map/ppermute | solution.py:480
  6.6 1.3 %collective-permute-start = (bf16[8,512]{1,0:T(8,128)(2,1)S(1)}, bf16[8,512]{1,0:T(8,128)(2,1)S(1)}, u32[]{:S(2)}, u32[]{:S(2)}) collective-permute-start(bf16[8,512]{1,0:T(8,128)(2,1)S(1)} %get-tuple-element.78), channel_id=1, source_target_pairs={{0,4},{4,8},{8,12},{12,16},{16,20},{20,24},{24,28},{28,32},{32,36}... | collective-permute-start | bytes 24584 | tf_op jit(solution)/shard_map/ppermute | solution.py:481
  7.9 6.4 %collective-permute-start.1 = (bf16[8,512]{1,0:T(8,128)(2,1)S(1)}, bf16[8,512]{1,0:T(8,128)(2,1)S(1)}, u32[]{:S(2)}, u32[]{:S(2)}) collective-permute-start(bf16[8,512]{1,0:T(8,128)(2,1)S(1)} %get-tuple-element.79), channel_id=1, source_target_pairs={{4,0},{8,4},{12,8},{16,12},{20,16},{24,20},{28,24},{32,28},{36,32}... | collective-permute-start | bytes 24584 | tf_op jit(solution)/shard_map/ppermute | solution.py:482
  14.2 0.0 collective-permute-start.3
  14.3 1.0 %collective-permute-done.prev_ref = bf16[8,512]{1,0:T(8,128)(2,1)S(1)} collective-permute-done((bf16[8,512]{1,0:T(8,128)(2,1)S(1)}, bf16[8,512]{1,0:T(8,128)(2,1)S(1)}, u32[]{:S(2)}, u32[]{:S(2)}) %collective-permute-start) | collective-permute-done | bytes 8224 | tf_op jit(solution)/shard_map/ppermute | solution.py:481
  15.3 0.0 collective-permute-done.1.next_ref
  15.3 0.0 collective-permute-done.2.other_ref
  15.3 0.0 copy-done
  15.3 0.0 copy-done.3
  15.3 0.0 copy-done.2
  15.3 5.7 %shard_map.110 = (bf16[512,512]{1,0:T(8,128)(2,1)S(1)}, f32[512,256]{1,0:T(8,128)S(1)}, f32[2,512,512]{2,1,0:T(8,128)S(1)}, bf16[2,512,128]{2,1,0:T(8,128)(2,1)S...) custom-call(s32[4]{0:T(128)S(1)} %pad_add_fusion.place_ref, ...), custom_call_target="tpu_custom_call" | custom-call | flops 8000000000 | bytes 24000000 | tf_op jit(solution)/shard_map/pallas_call | solution.py:485
  21.1 0.0 copy-start.1
  21.1 36.1 %conditional.1 = (bf16[64,8,128]{2,1,0:T(8,128)(2,1)S(1)}, f32[2,512,512]{2,1,0:T(8,128)S(1)}, bf16[2,512,128]{2,1,0:T(8,128)(2,1)S(1)}, f32[512,128]{1,0:T(8,12...) conditional(s32[]{:T(128)} %convert_element_type.9, ...), branch_computations={%region_0.0_spmd, %region_1.0_spmd} | conditional | flops 1000000 | bytes 8159296 | solution.py:518
  21.1 21.1 %all_to_all.8.got_ref = bf16[64,16,128]{2,1,0:T(8,128)(2,1)S(1)} all-to-all(bf16[64,16,128]{2,1,0:T(8,128)(2,1)S(1)} %get-tuple-element.48), channel_id=1, replica_groups=mesh['seq_0'=8,'seq_1'=2,'seq_2'=4,'x_hi'=2,'core'=2] {'seq_0','seq_1','..., dimensions={0} | all-to-all | bytes 524288 | tf_op jit(solution)/shard_map/cond/branch_1_fun/all_to_all | solution.py:508
  42.2 0.7 %branch_1_fun.1 = bf16[64,8,128]{2,1,0:T(8,128)(2,1)S(1)} custom-call(s32[4]{0:T(128)S(1)} %get-tuple-element.47.place_ref, bf16[64,16,128]{2,1,0:T(8,128)(2,1)S(1)} %all_to_all.8.got_ref), custom_call_target="tpu_custom_call" | custom-call | flops 1000000 | bytes 400000 | tf_op jit(solution)/shard_map/cond/branch_1_fun/pallas_call | solution.py:509
  42.9 14.3 %all_to_all.9 = bf16[64,8,128]{2,1,0:T(8,128)(2,1)S(1)} all-to-all(bf16[64,8,128]{2,1,0:T(8,128)(2,1)S(1)} %branch_1_fun.1), channel_id=1, replica_groups=mesh['seq_0'=8,'seq_1'=2,'seq_2'=4,'x_hi'=2,'core'=2] {'seq_0','seq_1','..., dimensions={0} | all-to-all | bytes 262144 | tf_op jit(solution)/shard_map/cond/branch_1_fun/all_to_all | solution.py:516
  57.2 0.0 collective-permute-done.3.late_ref
  57.2 0.0 copy-done.1
  57.2 2.5 %shard_map.111 = (f32[512,256]{1,0:T(8,128)S(1)}, bf16[512,256]{1,0:T(8,128)(2,1)S(1)}) custom-call(s32[4]{0:T(128)S(1)} %pad_add_fusion.place_ref, f32[2,512,512]{2,1,0:T(8,128)S(1)} %get-tuple-element.89.y_ref, bf16[2,512,128]{2,1,0:T(8,128)(2,1)S(1)} %get-tuple-element.90.c_ref, bf16[64,8,128]{2,1,0:T(8,128)(2,1)S(1)} %get-tuple-element.91.came_ref, ...), custom_call_target="tpu_custom_call" | custom-call | flops 2000000000 | bytes 6000000 | tf_op jit(solution)/shard_map/pallas_call | solution.py:525
  59.7 5.0 %collective-permute-start.4 = (bf16[512,256]{1,0:T(8,128)(2,1)S(1)}, bf16[512,256]{1,0:T(8,128)(2,1)S(1)}, u32[]{:S(2)}, u32[]{:S(2)}) collective-permute-start(bf16[512,256]{1,0:T(8,128)(2,1)S(1)} %get-tuple-element.99), channel_id=1, source_target_pairs={{0,1},{1,0},{2,3},{3,2},{4,5},{5,4},{6,7},{7,6},{8,9},{9,8},{10,11... | collective-permute-start | bytes 786440 | tf_op jit(solution)/shard_map/ppermute | solution.py:538
  64.7 1.2 %collective-permute-done.4 = bf16[512,256]{1,0:T(8,128)(2,1)S(1)} collective-permute-done((bf16[512,256]{1,0:T(8,128)(2,1)S(1)}, bf16[512,256]{1,0:T(8,128)(2,1)S(1)}, u32[]{:S(2)}, u32[]{:S(2)}) %collective-permute-start.4) | collective-permute-done | bytes 262176 | tf_op jit(solution)/shard_map/ppermute | solution.py:538
  65.9 0.8 %add_convert_fusion = bf16[512,256]{1,0:T(8,128)(2,1)} fusion(f32[512,256]{1,0:T(8,128)S(1)} %get-tuple-element.98, bf16[512,256]{1,0:T(8,128)(2,1)S(1)} %collective-permute-done.4), kind=kLoop, calls=%fused_computation | loop fusion | flops 393216 | bytes 1048576 | tf_op jit(solution)/shard_map/convert_element_type | solution.py:539
Async XLA Ops:
  0.0 15.3 %copy-start = (bf16[512,1024]{1,0:T(8,128)(2,1)S(1)}, bf16[512,1024]{1,0:T(8,128)(2,1)}, u32[]{:S(2)}) copy-start(bf16[512,1024]{1,0:T(8,128)(2,1)} %hidden_ref.3) | copy-start | bytes 3145732
  0.0 15.3 %copy-start.3 = (bf16[4,128]{1,0:T(4,128)(2,1)S(1)}, bf16[4,128]{1,0:T(4,128)(2,1)}, u32[]{:S(2)}) copy-start(bf16[4,128]{1,0:T(4,128)(2,1)} %tapbc_ref.1) | copy-start | bytes 3076
  0.0 15.3 %copy-start.2 = (bf16[512,128]{1,0:T(8,128)(2,1)S(1)}, bf16[512,128]{1,0:T(8,128)(2,1)}, u32[]{:S(2)}) copy-start(bf16[512,128]{1,0:T(8,128)(2,1)} %bc_ref.1) | copy-start | bytes 393220
  3.2 12.1 %collective-permute-start.2 = (bf16[544,256]{1,0:T(8,128)(2,1)S(1)}, bf16[544,256]{1,0:T(8,128)(2,1)S(1)}, u32[]{:S(2)}, u32[]{:S(2)}) collective-permute-start(bf16[544,256]{1,0:T(8,128)(2,1)S(1)} %get-tuple-element.80.own_ref), channel_id=1, source_target_pairs={{0,18},{18,0},{2,16},{16,2},{1,19},{19,1},{3,17},{17,3},{4,22},{22... | collective-permute-start | bytes 835592 | tf_op jit(solution)/shard_map/ppermute | solution.py:480
  6.6 8.7 %collective-permute-start = (bf16[8,512]{1,0:T(8,128)(2,1)S(1)}, bf16[8,512]{1,0:T(8,128)(2,1)S(1)}, u32[]{:S(2)}, u32[]{:S(2)}) collective-permute-start(bf16[8,512]{1,0:T(8,128)(2,1)S(1)} %get-tuple-element.78), channel_id=1, source_target_pairs={{0,4},{4,8},{8,12},{12,16},{16,20},{20,24},{24,28},{28,32},{32,36}... | collective-permute-start | bytes 24584 | tf_op jit(solution)/shard_map/ppermute | solution.py:481
  7.9 7.4 %collective-permute-start.1 = (bf16[8,512]{1,0:T(8,128)(2,1)S(1)}, bf16[8,512]{1,0:T(8,128)(2,1)S(1)}, u32[]{:S(2)}, u32[]{:S(2)}) collective-permute-start(bf16[8,512]{1,0:T(8,128)(2,1)S(1)} %get-tuple-element.79), channel_id=1, source_target_pairs={{4,0},{8,4},{12,8},{16,12},{20,16},{24,20},{28,24},{32,28},{36,32}... | collective-permute-start | bytes 24584 | tf_op jit(solution)/shard_map/ppermute | solution.py:482
  14.2 42.9 %collective-permute-start.3 = (bf16[512,512]{1,0:T(8,128)(2,1)S(1)}, bf16[512,512]{1,0:T(8,128)(2,1)S(1)}, u32[]{:S(2)}, u32[]{:S(2)}) collective-permute-start(bf16[512,512]{1,0:T(8,128)(2,1)S(1)} %get-tuple-element.97), channel_id=1, source_target_pairs={{0,18},{18,0},{2,16},{16,2},{1,19},{19,1},{3,17},{17,3},{4,22},{22... | collective-permute-start | bytes 1572872 | tf_op jit(solution)/shard_map/ppermute | solution.py:484
  21.1 36.1 %copy-start.1 = (bf16[256,512]{1,0:T(8,128)(2,1)S(1)}, bf16[256,512]{1,0:T(8,128)(2,1)}, u32[]{:S(2)}) copy-start(bf16[256,512]{1,0:T(8,128)(2,1)} %own_out_ref.1) | copy-start | bytes 786436
  59.7 6.2 %collective-permute-start.4 = (bf16[512,256]{1,0:T(8,128)(2,1)S(1)}, bf16[512,256]{1,0:T(8,128)(2,1)S(1)}, u32[]{:S(2)}, u32[]{:S(2)}) collective-permute-start(bf16[512,256]{1,0:T(8,128)(2,1)S(1)} %get-tuple-element.99), channel_id=1, source_target_pairs={{0,1},{1,0},{2,3},{3,2},{4,5},{5,4},{6,7},{7,6},{8,9},{9,8},{10,11... | collective-permute-start | bytes 786440 | tf_op jit(solution)/shard_map/ppermute | solution.py:538

commit v8 on v7

--- a/solution.py
+++ b/solution.py
@@ -93,7 +93,11 @@
     return (source == jnp.where(strand == 0, target, n - 1 - target)).astype(BF16)
 
 
-DT_AT, TAP_AT, SMALL_AT, PACKED = 512, 520, 528, 544
+DT_AT, TAP_AT, SMALL_AT, PACKED = 0, 8, 16, 32
+
+
+def half_kernel(zx_ref, x_ref):
+    x_ref[...] = zx_ref[:, x_ref.shape[1] :]
 
 
 def pack_kernel(
@@ -119,7 +123,6 @@
         ),
         sems,
     )
-    pack_ref[:DT_AT] = zx_ref[:, inner:]
     late_ref[:, :inner] = zx_ref[:, :inner]
     for copy in copies:
         copy.wait()
@@ -133,7 +136,7 @@
     packed.append(jnp.zeros((SMALL_AT - TAP_AT - taps_ref.shape[0], inner), F32))
     packed += parts_of(small) + parts_of(gain_ref[...])
     packed.append(jnp.zeros((PACKED - SMALL_AT - 6, inner), F32))
-    pack_ref[DT_AT:] = jnp.concatenate(packed, axis=0).astype(BF16)
+    pack_ref[...] = jnp.concatenate(packed, axis=0).astype(BF16)
 
 
 def unpack(ref):
@@ -173,7 +176,8 @@
 
 
 def front_kernel(
-    place_ref, hidden_ref, zx_ref, prev_ref, next_ref, own_ref, other_ref, bc_ref, tapbc_ref,
+    place_ref, hidden_ref, zx_ref, other_x_ref, prev_ref, next_ref, own_ref, other_ref, bc_ref,
+    tapbc_ref,
     u_ref, gate_ref, y_ref, c_ref, cols_ref, first_ref, gains_ref, send_ref,
     x_ref, b_ref, rows_ref, pad_ref,
 ):
@@ -241,7 +245,7 @@
     chunk = 32
     tiles = inner // LANES
     for g in range(3):
-        w = packs[g][:DT_AT] if g < 2 else bc_ref[...]
+        w = (zx_ref[:, inner:], other_x_ref[...], bc_ref[...])[g]
         middle = dot(u, w).astype(BF16).astype(F32)
         outer = dot(edge, w).astype(BF16).astype(F32)
         for k in range(w.shape[1] // LANES):
@@ -440,7 +444,12 @@
     swap = [(0, 1), (1, 0)]
     x_hi, core = lax.axis_index("x_hi"), lax.axis_index("core")
     place = jnp.stack([x_hi, core, lax.axis_index(SEQ), jnp.int32(count)]).astype(jnp.int32)
+    beside = (("seq_1", "x_hi"), [(0, 3), (3, 0), (1, 2), (2, 1)])
     zx = proj_zx.reshape(width, 2 * inner)
+    own_x = call(
+        half_kernel, struct((width, inner), BF16), [VMEM], VMEM, cost(1_000, 0, 500_000), mib=2
+    )(zx)
+    other_x = lax.ppermute(own_x, *beside)
 
     pack, late, head, tail = call(
         pack_kernel,
@@ -476,7 +485,6 @@
             out_proj,
         ),
     )
-    beside = (("seq_1", "x_hi"), [(0, 3), (3, 0), (1, 2), (2, 1)])
     other_pack = lax.ppermute(pack, *beside)
     prev = lax.ppermute(tail, SEQ, rise)
     following = lax.ppermute(head, SEQ, fall)
@@ -494,7 +502,7 @@
             struct((8, 2 * inner), F32),
             struct((count, 16, LANES), BF16),
         ),
-        [SMEM] + [VMEM] * 8,
+        [SMEM] + [VMEM] * 9,
         (VMEM,) * 8,
         cost(8_000_000_000, 3_000_000, 24_000_000),
         scratch=[
@@ -503,7 +511,9 @@
             pltpu.VMEM((48, rows), F32),
             pltpu.VMEM((2 * inner // LANES + 1, rows + 2 * HALO, LANES), F32),
         ],
-    )(place, hidden_in, zx, prev, following, pack, other_pack, proj_bc, conv_bc)
+    )(
+        place, hidden_in, zx, other_x, prev, following, pack, other_pack, proj_bc, conv_bc
+    )
     def passed_on(place, send, *others):
         got = lax.all_to_all(send, SEQ, 0, 0, tiled=True)
         scanned = call(

time: 66.8 us -> 67.4 us (level)
    ppermute x0 -> x1, starting transfers between devices: none -> 3.39 us  [shards(): other_x = lax.ppermute(own_x, *beside)]
    ppermute x1, starting transfers between devices: 3.39 us -> 0.11 us  [shards(): other_pack = lax.ppermute(pack, *beside)]
  transfers between devices with their start and end apart: 5 -> 6, of which waited for: 2 -> 2; matrix products, arithmetic and copies ran while one was open for 0% -> 0% of each run, Pallas kernels for 10% -> 12%
where the time goes in v8:
time: 67.4 us; the launch traced here: 67.2 us
  blocking collectives  35.3 us (52%)
  starting transfers between devices  16.7 us (25%)
  Pallas kernels  10.8 us (16%)
  waiting for transfers between devices  2.2 us (3%)
  local copies, waits for them, and re-layouts  1.24 us (2%)
  other arithmetic  0.83 us (1%)
    all_to_all x1, blocking collectives, passed_on(): got = lax.all_to_all(send, SEQ, 0, 0, tiled=True)  21 us
    all_to_all x1, blocking collectives, passed_on(): return (lax.all_to_all(scanned, SEQ, 0, 0, tiled=True), *others)  14.3 us
    ppermute x1, starting transfers between devices, shards(): following = lax.ppermute(head, SEQ, fall)  6.45 us
    pallas_call x1, Pallas kernels, shards(): call(front_kernel, (struct((rows, width), BF16), struct((rows, inner), F3...  5.75 us
    ppermute x1, starting transfers between devices, shards(): taken = lax.ppermute(give, 'core', swap)  5.29 us
    ppermute x1, starting transfers between devices, shards(): other_x = lax.ppermute(own_x, *beside)  3.39 us
    pallas_call x1, Pallas kernels, shards(): call(back_kernel, (struct((rows, inner), F32), struct((rows, inner), BF16...  2.55 us
    pallas_call x1, Pallas kernels, shards(): call(pack_kernel, (struct((PACKED, inner), BF16), struct((width, 2 * inne...  1.82 us
  transfers between devices with their start and end apart: 6, of which 2 were waited for; matrix products, arithmetic and copies ran while one was open for 0% of the time, Pallas kernels for 12%

profile of v8, /device:TPU:1, one launch (start us, length us, event | category | flops | bytes accessed | tf_op | source)
XLA Modules:
  0.0 67.2 jit_solution(3091054148730239566)
XLA Ops:
  0.0 0.0 copy-start
  0.0 0.0 copy-start.3
  0.0 0.0 copy-start.2
  0.0 1.2 %copy.12 = bf16[64,8,2,256]{3,1,2,0:T(8,128)(2,1)S(1)} copy(bf16[64,8,2,256]{3,2,1,0:T(2,128)(2,1)} %bitcast.13) | data formatting | bytes 1048576
  1.3 3.4 %collective-permute-start = (bf16[512,256]{1,0:T(8,128)(2,1)S(1)}, bf16[512,256]{1,0:T(8,128)(2,1)S(1)}, u32[]{:S(2)}, u32[]{:S(2)}) collective-permute-start(bf16[512,256]{1,0:T(8,128)(2,1)S(1)} %shard_map.109), channel_id=1, source_target_pairs={{0,18},{18,0},{2,16},{16,2},{1,19},{19,1},{3,17},{17,3},{4,22},{22... | collective-permute-start | bytes 786440 | tf_op jit(solution)/shard_map/ppermute | solution.py:452
  4.7 0.1 pad_add_fusion.place_ref
  4.7 1.8 %shard_map.110 = (bf16[32,256]{1,0:T(8,128)(2,1)S(1)}, bf16[512,512]{1,0:T(8,128)(2,1)S(1)}, bf16[8,512]{1,0:T(8,128)(2,1)S(1)}, bf16[8,512]{1,0:T(8,128)(2,1)S(1)}) custom-call(s32[4]{0:T(128)S(1)} %pad_add_fusion.place_ref, bf16[512,512]{1,0:T(8,128)(2,1)S(1)} %bitcast.11, bf16[4,512]{1,0:T(4,128)(2,1)} %bitcast.14, bf16[4,256]{1,0:T(4,128)(2,1)} %taps_hbm.1, ...), custom_call_target="tpu_custom_call" | custom-call | flops 1000000 | bytes 1000000 | tf_op jit(solution)/shard_map/pallas_call | solution.py:454
  6.6 0.1 collective-permute-start.3
  6.7 1.5 %collective-permute-start.1 = (bf16[8,512]{1,0:T(8,128)(2,1)S(1)}, bf16[8,512]{1,0:T(8,128)(2,1)S(1)}, u32[]{:S(2)}, u32[]{:S(2)}) collective-permute-start(bf16[8,512]{1,0:T(8,128)(2,1)S(1)} %get-tuple-element.78), channel_id=1, source_target_pairs={{0,4},{4,8},{8,12},{12,16},{16,20},{20,24},{24,28},{28,32},{32,36}... | collective-permute-start | bytes 24584 | tf_op jit(solution)/shard_map/ppermute | solution.py:489
  8.1 6.4 %collective-permute-start.2 = (bf16[8,512]{1,0:T(8,128)(2,1)S(1)}, bf16[8,512]{1,0:T(8,128)(2,1)S(1)}, u32[]{:S(2)}, u32[]{:S(2)}) collective-permute-start(bf16[8,512]{1,0:T(8,128)(2,1)S(1)} %get-tuple-element.79), channel_id=1, source_target_pairs={{4,0},{8,4},{12,8},{16,12},{20,16},{24,20},{28,24},{32,28},{36,32}... | collective-permute-start | bytes 24584 | tf_op jit(solution)/shard_map/ppermute | solution.py:490
  14.6 0.0 collective-permute-start.4
  14.6 1.0 %collective-permute-done.1.prev_ref = bf16[8,512]{1,0:T(8,128)(2,1)S(1)} collective-permute-done((bf16[8,512]{1,0:T(8,128)(2,1)S(1)}, bf16[8,512]{1,0:T(8,128)(2,1)S(1)}, u32[]{:S(2)}, u32[]{:S(2)}) %collective-permute-start.1) | collective-permute-done | bytes 8224 | tf_op jit(solution)/shard_map/ppermute | solution.py:489
  15.6 0.0 collective-permute-done.2.next_ref
  15.6 0.0 collective-permute-done.3.other_ref
  15.6 0.0 collective-permute-done.other_x_ref
  15.6 0.0 copy-done
  15.7 0.0 copy-done.3
  15.7 0.0 copy-done.2
  15.7 5.8 %shard_map.111 = (bf16[512,512]{1,0:T(8,128)(2,1)S(1)}, f32[512,256]{1,0:T(8,128)S(1)}, f32[2,512,512]{2,1,0:T(8,128)S(1)}, bf16[2,512,128]{2,1,0:T(8,128)(2,1)S...) custom-call(s32[4]{0:T(128)S(1)} %pad_add_fusion.place_ref, ...), custom_call_target="tpu_custom_call" | custom-call | flops 8000000000 | bytes 24000000 | tf_op jit(solution)/shard_map/pallas_call | solution.py:493
  21.4 0.0 copy-start.1
  21.4 36.0 %conditional.1 = (bf16[64,8,128]{2,1,0:T(8,128)(2,1)S(1)}, f32[2,512,512]{2,1,0:T(8,128)S(1)}, bf16[2,512,128]{2,1,0:T(8,128)(2,1)S(1)}, f32[512,128]{1,0:T(8,12...) conditional(s32[]{:T(128)} %convert_element_type.9, ...), branch_computations={%region_0.0_spmd, %region_1.0_spmd} | conditional | flops 1000000 | bytes 8159296 | solution.py:528
  21.5 21.0 %all_to_all.8.got_ref = bf16[64,16,128]{2,1,0:T(8,128)(2,1)S(1)} all-to-all(bf16[64,16,128]{2,1,0:T(8,128)(2,1)S(1)} %get-tuple-element.48), channel_id=1, replica_groups=mesh['seq_0'=8,'seq_1'=2,'seq_2'=4,'x_hi'=2,'core'=2] {'seq_0','seq_1','..., dimensions={0} | all-to-all | bytes 524288 | tf_op jit(solution)/shard_map/cond/branch_1_fun/all_to_all | solution.py:518
  42.4 0.7 %branch_1_fun.1 = bf16[64,8,128]{2,1,0:T(8,128)(2,1)S(1)} custom-call(s32[4]{0:T(128)S(1)} %get-tuple-element.47.place_ref, bf16[64,16,128]{2,1,0:T(8,128)(2,1)S(1)} %all_to_all.8.got_ref), custom_call_target="tpu_custom_call" | custom-call | flops 1000000 | bytes 400000 | tf_op jit(solution)/shard_map/cond/branch_1_fun/pallas_call | solution.py:519
  43.1 14.3 %all_to_all.9 = bf16[64,8,128]{2,1,0:T(8,128)(2,1)S(1)} all-to-all(bf16[64,8,128]{2,1,0:T(8,128)(2,1)S(1)} %branch_1_fun.1), channel_id=1, replica_groups=mesh['seq_0'=8,'seq_1'=2,'seq_2'=4,'x_hi'=2,'core'=2] {'seq_0','seq_1','..., dimensions={0} | all-to-all | bytes 262144 | tf_op jit(solution)/shard_map/cond/branch_1_fun/all_to_all | solution.py:526
  57.4 0.0 collective-permute-done.4.late_ref
  57.5 0.0 copy-done.1
  57.5 2.5 %shard_map.112 = (f32[512,256]{1,0:T(8,128)S(1)}, bf16[512,256]{1,0:T(8,128)(2,1)S(1)}) custom-call(s32[4]{0:T(128)S(1)} %pad_add_fusion.place_ref, f32[2,512,512]{2,1,0:T(8,128)S(1)} %get-tuple-element.89.y_ref, bf16[2,512,128]{2,1,0:T(8,128)(2,1)S(1)} %get-tuple-element.90.c_ref, bf16[64,8,128]{2,1,0:T(8,128)(2,1)S(1)} %get-tuple-element.91.came_ref, ...), custom_call_target="tpu_custom_call" | custom-call | flops 2000000000 | bytes 6000000 | tf_op jit(solution)/shard_map/pallas_call | solution.py:535
  60.0 5.3 %collective-permute-start.5 = (bf16[512,256]{1,0:T(8,128)(2,1)S(1)}, bf16[512,256]{1,0:T(8,128)(2,1)S(1)}, u32[]{:S(2)}, u32[]{:S(2)}) collective-permute-start(bf16[512,256]{1,0:T(8,128)(2,1)S(1)} %get-tuple-element.99), channel_id=1, source_target_pairs={{0,1},{1,0},{2,3},{3,2},{4,5},{5,4},{6,7},{7,6},{8,9},{9,8},{10,11... | collective-permute-start | bytes 786440 | tf_op jit(solution)/shard_map/ppermute | solution.py:548
  65.3 1.2 %collective-permute-done.5 = bf16[512,256]{1,0:T(8,128)(2,1)S(1)} collective-permute-done((bf16[512,256]{1,0:T(8,128)(2,1)S(1)}, bf16[512,256]{1,0:T(8,128)(2,1)S(1)}, u32[]{:S(2)}, u32[]{:S(2)}) %collective-permute-start.5) | collective-permute-done | bytes 262176 | tf_op jit(solution)/shard_map/ppermute | solution.py:548
  66.5 0.8 %add_convert_fusion = bf16[512,256]{1,0:T(8,128)(2,1)} fusion(f32[512,256]{1,0:T(8,128)S(1)} %get-tuple-element.98, bf16[512,256]{1,0:T(8,128)(2,1)S(1)} %collective-permute-done.5), kind=kLoop, calls=%fused_computation | loop fusion | flops 393216 | bytes 1048576 | tf_op jit(solution)/shard_map/convert_element_type | solution.py:549
  (1 shorter events, 0.0 us)
Async XLA Ops:
  0.0 15.6 %copy-start = (bf16[512,1024]{1,0:T(8,128)(2,1)S(1)}, bf16[512,1024]{1,0:T(8,128)(2,1)}, u32[]{:S(2)}) copy-start(bf16[512,1024]{1,0:T(8,128)(2,1)} %hidden_ref.3) | copy-start | bytes 3145732
  0.0 15.7 %copy-start.3 = (bf16[4,128]{1,0:T(4,128)(2,1)S(1)}, bf16[4,128]{1,0:T(4,128)(2,1)}, u32[]{:S(2)}) copy-start(bf16[4,128]{1,0:T(4,128)(2,1)} %tapbc_ref.1) | copy-start | bytes 3076
  0.0 15.7 %copy-start.2 = (bf16[512,128]{1,0:T(8,128)(2,1)S(1)}, bf16[512,128]{1,0:T(8,128)(2,1)}, u32[]{:S(2)}) copy-start(bf16[512,128]{1,0:T(8,128)(2,1)} %bc_ref.1) | copy-start | bytes 393220
  1.3 14.4 %collective-permute-start = (bf16[512,256]{1,0:T(8,128)(2,1)S(1)}, bf16[512,256]{1,0:T(8,128)(2,1)S(1)}, u32[]{:S(2)}, u32[]{:S(2)}) collective-permute-start(bf16[512,256]{1,0:T(8,128)(2,1)S(1)} %shard_map.109), channel_id=1, source_target_pairs={{0,18},{18,0},{2,16},{16,2},{1,19},{19,1},{3,17},{17,3},{4,22},{22... | collective-permute-start | bytes 786440 | tf_op jit(solution)/shard_map/ppermute | solution.py:452
  6.6 9.1 %collective-permute-start.3 = (bf16[32,256]{1,0:T(8,128)(2,1)S(1)}, bf16[32,256]{1,0:T(8,128)(2,1)S(1)}, u32[]{:S(2)}, u32[]{:S(2)}) collective-permute-start(bf16[32,256]{1,0:T(8,128)(2,1)S(1)} %get-tuple-element.80.own_ref), channel_id=1, source_target_pairs={{0,18},{18,0},{2,16},{16,2},{1,19},{19,1},{3,17},{17,3},{4,22},{22... | collective-permute-start | bytes 49160 | tf_op jit(solution)/shard_map/ppermute | solution.py:488
  6.7 9.0 %collective-permute-start.1 = (bf16[8,512]{1,0:T(8,128)(2,1)S(1)}, bf16[8,512]{1,0:T(8,128)(2,1)S(1)}, u32[]{:S(2)}, u32[]{:S(2)}) collective-permute-start(bf16[8,512]{1,0:T(8,128)(2,1)S(1)} %get-tuple-element.78), channel_id=1, source_target_pairs={{0,4},{4,8},{8,12},{12,16},{16,20},{20,24},{24,28},{28,32},{32,36}... | collective-permute-start | bytes 24584 | tf_op jit(solution)/shard_map/ppermute | solution.py:489
  8.1 7.5 %collective-permute-start.2 = (bf16[8,512]{1,0:T(8,128)(2,1)S(1)}, bf16[8,512]{1,0:T(8,128)(2,1)S(1)}, u32[]{:S(2)}, u32[]{:S(2)}) collective-permute-start(bf16[8,512]{1,0:T(8,128)(2,1)S(1)} %get-tuple-element.79), channel_id=1, source_target_pairs={{4,0},{8,4},{12,8},{16,12},{20,16},{24,20},{28,24},{32,28},{36,32}... | collective-permute-start | bytes 24584 | tf_op jit(solution)/shard_map/ppermute | solution.py:490
  14.6 42.9 %collective-permute-start.4 = (bf16[512,512]{1,0:T(8,128)(2,1)S(1)}, bf16[512,512]{1,0:T(8,128)(2,1)S(1)}, u32[]{:S(2)}, u32[]{:S(2)}) collective-permute-start(bf16[512,512]{1,0:T(8,128)(2,1)S(1)} %get-tuple-element.97), channel_id=1, source_target_pairs={{0,18},{18,0},{2,16},{16,2},{1,19},{19,1},{3,17},{17,3},{4,22},{22... | collective-permute-start | bytes 1572872 | tf_op jit(solution)/shard_map/ppermute | solution.py:492
  21.4 36.0 %copy-start.1 = (bf16[256,512]{1,0:T(8,128)(2,1)S(1)}, bf16[256,512]{1,0:T(8,128)(2,1)}, u32[]{:S(2)}) copy-start(bf16[256,512]{1,0:T(8,128)(2,1)} %own_out_ref.1) | copy-start | bytes 786436
  60.0 6.5 %collective-permute-start.5 = (bf16[512,256]{1,0:T(8,128)(2,1)S(1)}, bf16[512,256]{1,0:T(8,128)(2,1)S(1)}, u32[]{:S(2)}, u32[]{:S(2)}) collective-permute-start(bf16[512,256]{1,0:T(8,128)(2,1)S(1)} %get-tuple-element.99), channel_id=1, source_target_pairs={{0,1},{1,0},{2,3},{3,2},{4,5},{5,4},{6,7},{7,6},{8,9},{9,8},{10,11... | collective-permute-start | bytes 786440 | tf_op jit(solution)/shard_map/ppermute | solution.py:548

commit v9 on v8

--- a/solution.py
+++ b/solution.py
@@ -102,12 +102,13 @@
 
 def pack_kernel(
     place_ref, zx_ref, dt_hbm, taps_hbm, bias_hbm, exp_hbm, skip_hbm, gain_hbm, hidden_hbm, out_hbm,
-    pack_ref, late_ref, head_ref, tail_ref,
+    pack_ref, late_ref, far_ref, near_ref,
     dt_ref, taps_ref, bias_ref, exp_ref, skip_ref, gain_ref, sems,
 ):
     inner, heads = pack_ref.shape[1], dt_ref.shape[0]
     rows, width = hidden_hbm.shape[0], hidden_hbm.shape[1] // 2
     columns = pl.ds(pl.multiple_of(place_ref[0] * width, width), width)
+    odd, last = lax.rem(place_ref[2], 2), rows - HALO
     copies = start_copies(
         (
             (dt_hbm, dt_ref),
@@ -116,8 +117,8 @@
             (exp_hbm, exp_ref),
             (skip_hbm, skip_ref),
             (gain_hbm, gain_ref),
-            (hidden_hbm.at[pl.ds(0, HALO), columns], head_ref),
-            (hidden_hbm.at[pl.ds(rows - HALO, HALO), columns], tail_ref),
+            (hidden_hbm.at[pl.ds(pl.multiple_of(odd * last, HALO), HALO), columns], far_ref),
+            (hidden_hbm.at[pl.ds(pl.multiple_of((1 - odd) * last, HALO), HALO), columns], near_ref),
             (out_hbm.at[:, :inner], late_ref.at[:inner, inner:]),
             (out_hbm.at[:, inner:], late_ref.at[inner:, inner:]),
         ),
@@ -176,7 +177,7 @@
 
 
 def front_kernel(
-    place_ref, hidden_ref, zx_ref, other_x_ref, prev_ref, next_ref, own_ref, other_ref, bc_ref,
+    place_ref, hidden_ref, zx_ref, other_x_ref, far_ref, near_ref, own_ref, other_ref, bc_ref,
     tapbc_ref,
     u_ref, gate_ref, y_ref, c_ref, cols_ref, first_ref, gains_ref, send_ref,
     x_ref, b_ref, rows_ref, pad_ref,
@@ -190,8 +191,10 @@
     u = dot(u, turn).astype(BF16)
     u_ref[...] = u
     gate_ref[...] = gated_by(u, zx_ref[:, :inner])
-    before = jnp.where(position > 0, prev_ref[...].astype(F32), 0.0)
-    after = jnp.where(position < count - 1, next_ref[...].astype(F32), 0.0)
+    odd = lax.rem(position, 2) == 1
+    far, near = far_ref[...].astype(F32), near_ref[...].astype(F32)
+    before = jnp.where(position > 0, jnp.where(odd, near, far), 0.0)
+    after = jnp.where(position < count - 1, jnp.where(odd, far, near), 0.0)
     edge = dot(jnp.concatenate([before, after], axis=0).astype(BF16), turn)
     edge = edge.astype(BF16)
 
@@ -439,8 +442,8 @@
     rows, width = hidden_in.shape[0], hidden_in.shape[1] // 2
     inner = proj_zx.shape[2]
     count = math.prod(lax.axis_size(axis) for axis in SEQ)
-    rise = [(i, (i + 1) % count) for i in range(count)]
-    fall = [((i + 1) % count, i) for i in range(count)]
+    outer = [(i, i + 1 if i % 2 else i - 1) for i in range(1, count - 1)]
+    inside_pairs = [(i, i - 1 if i % 2 else i + 1) for i in range(count)]
     swap = [(0, 1), (1, 0)]
     x_hi, core = lax.axis_index("x_hi"), lax.axis_index("core")
     place = jnp.stack([x_hi, core, lax.axis_index(SEQ), jnp.int32(count)]).astype(jnp.int32)
@@ -451,7 +454,7 @@
     )(zx)
     other_x = lax.ppermute(own_x, *beside)
 
-    pack, late, head, tail = call(
+    pack, late, far, near = call(
         pack_kernel,
         (
             struct((PACKED, inner), BF16),
@@ -486,8 +489,8 @@
         ),
     )
     other_pack = lax.ppermute(pack, *beside)
-    prev = lax.ppermute(tail, SEQ, rise)
-    following = lax.ppermute(head, SEQ, fall)
+    got_far = lax.ppermute(far, SEQ, outer)
+    got_near = lax.ppermute(near, SEQ, inside_pairs)
 
     other_late = lax.ppermute(late, *beside)
     u, own_gate, y, c, cols, first, gains, send = call(
@@ -512,7 +515,7 @@
             pltpu.VMEM((2 * inner // LANES + 1, rows + 2 * HALO, LANES), F32),
         ],
     )(
-        place, hidden_in, zx, other_x, prev, following, pack, other_pack, proj_bc, conv_bc
+        place, hidden_in, zx, other_x, got_far, got_near, pack, other_pack, proj_bc, conv_bc
     )
     def passed_on(place, send, *others):
         got = lax.all_to_all(send, SEQ, 0, 0, tiled=True)

time: 67.4 us -> 66.8 us (level)
  blocking collectives: 35.3 us -> 36.6 us
  waiting for transfers between devices: 2.2 us -> 1.18 us
  starting transfers between devices: 16.7 us -> 15.7 us
    ppermute x2, starting transfers between devices: 7.92 us -> 4.75 us  [the longest x1 4.1 us: shards(): got_near = lax.ppermute(near, SEQ, inside_pairs)]
    ppermute x1, starting transfers between devices: 0.01 us -> 2.48 us  [shards(): other_late = lax.ppermute(late, *beside)]
    all_to_all x1, blocking collectives: 21 us -> 22.3 us  [passed_on(): got = lax.all_to_all(send, SEQ, 0, 0, tiled=True)]
    ppermute x2, waiting for transfers between devices: 1.03 us -> 0.01 us  [the longest x1 0.01 us: shards(): got_far = lax.ppermute(far, SEQ, outer)]
  transfers between devices with their start and end apart: 6 -> 6, of which waited for: 2 -> 1; matrix products, arithmetic and copies ran while one was open for 0% -> 0% of each run, Pallas kernels for 12% -> 12%
where the time goes in v9:
time: 66.8 us; the launch traced here: 66.5 us
  blocking collectives  36.6 us (55%)
  starting transfers between devices  15.7 us (24%)
  Pallas kernels  10.8 us (16%)
  local copies, waits for them, and re-layouts  1.24 us (2%)
  waiting for transfers between devices  1.18 us (2%)
  other arithmetic  0.83 us (1%)
    all_to_all x1, blocking collectives, passed_on(): got = lax.all_to_all(send, SEQ, 0, 0, tiled=True)  22.3 us
    all_to_all x1, blocking collectives, passed_on(): return (lax.all_to_all(scanned, SEQ, 0, 0, tiled=True), *others)  14.3 us
    pallas_call x1, Pallas kernels, shards(): call(front_kernel, (struct((rows, width), BF16), struct((rows, inner), F3...  5.76 us
    ppermute x1, starting transfers between devices, shards(): taken = lax.ppermute(give, 'core', swap)  5 us
    ppermute x1, starting transfers between devices, shards(): got_near = lax.ppermute(near, SEQ, inside_pairs)  4.1 us
    ppermute x1, starting transfers between devices, shards(): other_x = lax.ppermute(own_x, *beside)  3.39 us
    pallas_call x1, Pallas kernels, shards(): call(back_kernel, (struct((rows, inner), F32), struct((rows, inner), BF16...  2.54 us
    ppermute x1, starting transfers between devices, shards(): other_late = lax.ppermute(late, *beside)  2.48 us
  transfers between devices with their start and end apart: 6, of which 1 were waited for; matrix products, arithmetic and copies ran while one was open for 0% of the time, Pallas kernels for 12%

profile of v9, /device:TPU:1, one launch (start us, length us, event | category | flops | bytes accessed | tf_op | source)
XLA Modules:
  0.0 66.5 jit_solution(10199004930548626800)
XLA Ops:
  0.0 0.0 copy-start
  0.0 0.0 copy-start.3
  0.0 0.0 copy-start.2
  0.0 1.2 %copy.12 = bf16[64,8,2,256]{3,1,2,0:T(8,128)(2,1)S(1)} copy(bf16[64,8,2,256]{3,2,1,0:T(2,128)(2,1)} %bitcast.13) | data formatting | bytes 1048576
  1.3 3.4 %collective-permute-start = (bf16[512,256]{1,0:T(8,128)(2,1)S(1)}, bf16[512,256]{1,0:T(8,128)(2,1)S(1)}, u32[]{:S(2)}, u32[]{:S(2)}) collective-permute-start(bf16[512,256]{1,0:T(8,128)(2,1)S(1)} %shard_map.109), channel_id=1, source_target_pairs={{0,18},{18,0},{2,16},{16,2},{1,19},{19,1},{3,17},{17,3},{4,22},{22... | collective-permute-start | bytes 786440 | tf_op jit(solution)/shard_map/ppermute | solution.py:455
  4.7 0.1 pad_add_fusion.place_ref
  4.7 1.8 %shard_map.110 = (bf16[32,256]{1,0:T(8,128)(2,1)S(1)}, bf16[512,512]{1,0:T(8,128)(2,1)S(1)}, bf16[8,512]{1,0:T(8,128)(2,1)S(1)}, bf16[8,512]{1,0:T(8,128)(2,1)S(1)}) custom-call(s32[4]{0:T(128)S(1)} %pad_add_fusion.place_ref, bf16[512,512]{1,0:T(8,128)(2,1)S(1)} %bitcast.11, bf16[4,512]{1,0:T(4,128)(2,1)} %bitcast.14, bf16[4,256]{1,0:T(4,128)(2,1)} %taps_hbm.1, ...), custom_call_target="tpu_custom_call" | custom-call | flops 1000000 | bytes 1000000 | tf_op jit(solution)/shard_map/pallas_call | solution.py:457
  6.6 0.1 collective-permute-start.3
  6.7 0.6 collective-permute-start.1
  7.3 4.1 %collective-permute-start.2 = (bf16[8,512]{1,0:T(8,128)(2,1)S(1)}, bf16[8,512]{1,0:T(8,128)(2,1)S(1)}, u32[]{:S(2)}, u32[]{:S(2)}) collective-permute-start(bf16[8,512]{1,0:T(8,128)(2,1)S(1)} %get-tuple-element.79), channel_id=1, source_target_pairs={{0,4},{4,0},{8,12},{12,8},{16,20},{20,16},{24,28},{28,24},{32,36},... | collective-permute-start | bytes 24584 | tf_op jit(solution)/shard_map/ppermute | solution.py:493
  11.4 2.5 %collective-permute-start.4 = (bf16[512,512]{1,0:T(8,128)(2,1)S(1)}, bf16[512,512]{1,0:T(8,128)(2,1)S(1)}, u32[]{:S(2)}, u32[]{:S(2)}) collective-permute-start(bf16[512,512]{1,0:T(8,128)(2,1)S(1)} %get-tuple-element.97), channel_id=1, source_target_pairs={{0,18},{18,0},{2,16},{16,2},{1,19},{19,1},{3,17},{17,3},{4,22},{22... | collective-permute-start | bytes 1572872 | tf_op jit(solution)/shard_map/ppermute | solution.py:495
  13.9 0.0 collective-permute-done.1.far_ref
  13.9 0.0 collective-permute-done.2.near_ref
  13.9 0.0 collective-permute-done.3.other_ref
  13.9 0.0 collective-permute-done.other_x_ref
  13.9 0.0 copy-done
  13.9 0.0 copy-done.3
  14.0 0.0 copy-done.2
  14.0 5.8 %shard_map.111 = (bf16[512,512]{1,0:T(8,128)(2,1)S(1)}, f32[512,256]{1,0:T(8,128)S(1)}, f32[2,512,512]{2,1,0:T(8,128)S(1)}, bf16[2,512,128]{2,1,0:T(8,128)(2,1)S...) custom-call(s32[4]{0:T(128)S(1)} %pad_add_fusion.place_ref, ...), custom_call_target="tpu_custom_call" | custom-call | flops 8000000000 | bytes 24000000 | tf_op jit(solution)/shard_map/pallas_call | solution.py:496
  19.7 0.0 copy-start.1
  19.7 37.3 %conditional.1 = (bf16[64,8,128]{2,1,0:T(8,128)(2,1)S(1)}, f32[2,512,512]{2,1,0:T(8,128)S(1)}, bf16[2,512,128]{2,1,0:T(8,128)(2,1)S(1)}, f32[512,128]{1,0:T(8,12...) conditional(s32[]{:T(128)} %convert_element_type.9, ...), branch_computations={%region_0.0_spmd, %region_1.0_spmd} | conditional | flops 1000000 | bytes 8159296 | solution.py:531
  19.7 22.3 %all_to_all.8.got_ref = bf16[64,16,128]{2,1,0:T(8,128)(2,1)S(1)} all-to-all(bf16[64,16,128]{2,1,0:T(8,128)(2,1)S(1)} %get-tuple-element.48), channel_id=1, replica_groups=mesh['seq_0'=8,'seq_1'=2,'seq_2'=4,'x_hi'=2,'core'=2] {'seq_0','seq_1','..., dimensions={0} | all-to-all | bytes 524288 | tf_op jit(solution)/shard_map/cond/branch_1_fun/all_to_all | solution.py:521
  42.0 0.7 %branch_1_fun.1 = bf16[64,8,128]{2,1,0:T(8,128)(2,1)S(1)} custom-call(s32[4]{0:T(128)S(1)} %get-tuple-element.47.place_ref, bf16[64,16,128]{2,1,0:T(8,128)(2,1)S(1)} %all_to_all.8.got_ref), custom_call_target="tpu_custom_call" | custom-call | flops 1000000 | bytes 400000 | tf_op jit(solution)/shard_map/cond/branch_1_fun/pallas_call | solution.py:522
  42.7 14.3 %all_to_all.9 = bf16[64,8,128]{2,1,0:T(8,128)(2,1)S(1)} all-to-all(bf16[64,8,128]{2,1,0:T(8,128)(2,1)S(1)} %branch_1_fun.1), channel_id=1, replica_groups=mesh['seq_0'=8,'seq_1'=2,'seq_2'=4,'x_hi'=2,'core'=2] {'seq_0','seq_1','..., dimensions={0} | all-to-all | bytes 262144 | tf_op jit(solution)/shard_map/cond/branch_1_fun/all_to_all | solution.py:529
  57.0 0.0 collective-permute-done.4.late_ref
  57.0 0.0 copy-done.1
  57.0 2.5 %shard_map.112 = (f32[512,256]{1,0:T(8,128)S(1)}, bf16[512,256]{1,0:T(8,128)(2,1)S(1)}) custom-call(s32[4]{0:T(128)S(1)} %pad_add_fusion.place_ref, f32[2,512,512]{2,1,0:T(8,128)S(1)} %get-tuple-element.89.y_ref, bf16[2,512,128]{2,1,0:T(8,128)(2,1)S(1)} %get-tuple-element.90.c_ref, bf16[64,8,128]{2,1,0:T(8,128)(2,1)S(1)} %get-tuple-element.91.came_ref, ...), custom_call_target="tpu_custom_call" | custom-call | flops 2000000000 | bytes 6000000 | tf_op jit(solution)/shard_map/pallas_call | solution.py:538
  59.6 5.0 %collective-permute-start.5 = (bf16[512,256]{1,0:T(8,128)(2,1)S(1)}, bf16[512,256]{1,0:T(8,128)(2,1)S(1)}, u32[]{:S(2)}, u32[]{:S(2)}) collective-permute-start(bf16[512,256]{1,0:T(8,128)(2,1)S(1)} %get-tuple-element.99), channel_id=1, source_target_pairs={{0,1},{1,0},{2,3},{3,2},{4,5},{5,4},{6,7},{7,6},{8,9},{9,8},{10,11... | collective-permute-start | bytes 786440 | tf_op jit(solution)/shard_map/ppermute | solution.py:551
  64.6 1.2 %collective-permute-done.5 = bf16[512,256]{1,0:T(8,128)(2,1)S(1)} collective-permute-done((bf16[512,256]{1,0:T(8,128)(2,1)S(1)}, bf16[512,256]{1,0:T(8,128)(2,1)S(1)}, u32[]{:S(2)}, u32[]{:S(2)}) %collective-permute-start.5) | collective-permute-done | bytes 262176 | tf_op jit(solution)/shard_map/ppermute | solution.py:551
  65.7 0.8 %add_convert_fusion = bf16[512,256]{1,0:T(8,128)(2,1)} fusion(f32[512,256]{1,0:T(8,128)S(1)} %get-tuple-element.98, bf16[512,256]{1,0:T(8,128)(2,1)S(1)} %collective-permute-done.5), kind=kLoop, calls=%fused_computation | loop fusion | flops 393216 | bytes 1048576 | tf_op jit(solution)/shard_map/convert_element_type | solution.py:552
  (1 shorter events, 0.0 us)
Async XLA Ops:
  0.0 13.9 %copy-start = (bf16[512,1024]{1,0:T(8,128)(2,1)S(1)}, bf16[512,1024]{1,0:T(8,128)(2,1)}, u32[]{:S(2)}) copy-start(bf16[512,1024]{1,0:T(8,128)(2,1)} %hidden_ref.3) | copy-start | bytes 3145732
  0.0 13.9 %copy-start.3 = (bf16[4,128]{1,0:T(4,128)(2,1)S(1)}, bf16[4,128]{1,0:T(4,128)(2,1)}, u32[]{:S(2)}) copy-start(bf16[4,128]{1,0:T(4,128)(2,1)} %tapbc_ref.1) | copy-start | bytes 3076
  0.0 13.9 %copy-start.2 = (bf16[512,128]{1,0:T(8,128)(2,1)S(1)}, bf16[512,128]{1,0:T(8,128)(2,1)}, u32[]{:S(2)}) copy-start(bf16[512,128]{1,0:T(8,128)(2,1)} %bc_ref.1) | copy-start | bytes 393220
  1.3 12.7 %collective-permute-start = (bf16[512,256]{1,0:T(8,128)(2,1)S(1)}, bf16[512,256]{1,0:T(8,128)(2,1)S(1)}, u32[]{:S(2)}, u32[]{:S(2)}) collective-permute-start(bf16[512,256]{1,0:T(8,128)(2,1)S(1)} %shard_map.109), channel_id=1, source_target_pairs={{0,18},{18,0},{2,16},{16,2},{1,19},{19,1},{3,17},{17,3},{4,22},{22... | collective-permute-start | bytes 786440 | tf_op jit(solution)/shard_map/ppermute | solution.py:455
  6.6 7.4 %collective-permute-start.3 = (bf16[32,256]{1,0:T(8,128)(2,1)S(1)}, bf16[32,256]{1,0:T(8,128)(2,1)S(1)}, u32[]{:S(2)}, u32[]{:S(2)}) collective-permute-start(bf16[32,256]{1,0:T(8,128)(2,1)S(1)} %get-tuple-element.80.own_ref), channel_id=1, source_target_pairs={{0,18},{18,0},{2,16},{16,2},{1,19},{19,1},{3,17},{17,3},{4,22},{22... | collective-permute-start | bytes 49160 | tf_op jit(solution)/shard_map/ppermute | solution.py:491
  6.7 7.2 %collective-permute-start.1 = (bf16[8,512]{1,0:T(8,128)(2,1)S(1)}, bf16[8,512]{1,0:T(8,128)(2,1)S(1)}, u32[]{:S(2)}, u32[]{:S(2)}) collective-permute-start(bf16[8,512]{1,0:T(8,128)(2,1)S(1)} %get-tuple-element.78), channel_id=1, source_target_pairs={{4,8},{8,4},{12,16},{16,12},{20,24},{24,20},{28,32},{32,28},{36,40... | collective-permute-start | bytes 24584 | tf_op jit(solution)/shard_map/ppermute | solution.py:492
  7.3 6.6 %collective-permute-start.2 = (bf16[8,512]{1,0:T(8,128)(2,1)S(1)}, bf16[8,512]{1,0:T(8,128)(2,1)S(1)}, u32[]{:S(2)}, u32[]{:S(2)}) collective-permute-start(bf16[8,512]{1,0:T(8,128)(2,1)S(1)} %get-tuple-element.79), channel_id=1, source_target_pairs={{0,4},{4,0},{8,12},{12,8},{16,20},{20,16},{24,28},{28,24},{32,36},... | collective-permute-start | bytes 24584 | tf_op jit(solution)/shard_map/ppermute | solution.py:493
  11.4 45.6 %collective-permute-start.4 = (bf16[512,512]{1,0:T(8,128)(2,1)S(1)}, bf16[512,512]{1,0:T(8,128)(2,1)S(1)}, u32[]{:S(2)}, u32[]{:S(2)}) collective-permute-start(bf16[512,512]{1,0:T(8,128)(2,1)S(1)} %get-tuple-element.97), channel_id=1, source_target_pairs={{0,18},{18,0},{2,16},{16,2},{1,19},{19,1},{3,17},{17,3},{4,22},{22... | collective-permute-start | bytes 1572872 | tf_op jit(solution)/shard_map/ppermute | solution.py:495
  19.7 37.3 %copy-start.1 = (bf16[256,512]{1,0:T(8,128)(2,1)S(1)}, bf16[256,512]{1,0:T(8,128)(2,1)}, u32[]{:S(2)}) copy-start(bf16[256,512]{1,0:T(8,128)(2,1)} %own_out_ref.1) | copy-start | bytes 786436
  59.6 6.2 %collective-permute-start.5 = (bf16[512,256]{1,0:T(8,128)(2,1)S(1)}, bf16[512,256]{1,0:T(8,128)(2,1)S(1)}, u32[]{:S(2)}, u32[]{:S(2)}) collective-permute-start(bf16[512,256]{1,0:T(8,128)(2,1)S(1)} %get-tuple-element.99), channel_id=1, source_target_pairs={{0,1},{1,0},{2,3},{3,2},{4,5},{5,4},{6,7},{7,6},{8,9},{9,8},{10,11... | collective-permute-start | bytes 786440 | tf_op jit(solution)/shard_map/ppermute | solution.py:551

commit v10 on v9

--- a/solution.py
+++ b/solution.py
@@ -93,11 +93,7 @@
     return (source == jnp.where(strand == 0, target, n - 1 - target)).astype(BF16)
 
 
-DT_AT, TAP_AT, SMALL_AT, PACKED = 0, 8, 16, 32
-
-
-def half_kernel(zx_ref, x_ref):
-    x_ref[...] = zx_ref[:, x_ref.shape[1] :]
+DT_AT, TAP_AT, SMALL_AT, PACKED = 512, 520, 528, 544
 
 
 def pack_kernel(
@@ -124,6 +120,7 @@
         ),
         sems,
     )
+    pack_ref[:DT_AT] = zx_ref[:, inner:]
     late_ref[:, :inner] = zx_ref[:, :inner]
     for copy in copies:
         copy.wait()
@@ -137,7 +134,7 @@
     packed.append(jnp.zeros((SMALL_AT - TAP_AT - taps_ref.shape[0], inner), F32))
     packed += parts_of(small) + parts_of(gain_ref[...])
     packed.append(jnp.zeros((PACKED - SMALL_AT - 6, inner), F32))
-    pack_ref[...] = jnp.concatenate(packed, axis=0).astype(BF16)
+    pack_ref[DT_AT:] = jnp.concatenate(packed, axis=0).astype(BF16)
 
 
 def unpack(ref):
@@ -177,8 +174,7 @@
 
 
 def front_kernel(
-    place_ref, hidden_ref, zx_ref, other_x_ref, far_ref, near_ref, own_ref, other_ref, bc_ref,
-    tapbc_ref,
+    place_ref, hidden_ref, zx_ref, far_ref, near_ref, own_ref, other_ref, bc_ref, tapbc_ref,
     u_ref, gate_ref, y_ref, c_ref, cols_ref, first_ref, gains_ref, send_ref,
     x_ref, b_ref, rows_ref, pad_ref,
 ):
@@ -248,7 +244,7 @@
     chunk = 32
     tiles = inner // LANES
     for g in range(3):
-        w = (zx_ref[:, inner:], other_x_ref[...], bc_ref[...])[g]
+        w = packs[g][:DT_AT] if g < 2 else bc_ref[...]
         middle = dot(u, w).astype(BF16).astype(F32)
         outer = dot(edge, w).astype(BF16).astype(F32)
         for k in range(w.shape[1] // LANES):
@@ -447,12 +443,7 @@
     swap = [(0, 1), (1, 0)]
     x_hi, core = lax.axis_index("x_hi"), lax.axis_index("core")
     place = jnp.stack([x_hi, core, lax.axis_index(SEQ), jnp.int32(count)]).astype(jnp.int32)
-    beside = (("seq_1", "x_hi"), [(0, 3), (3, 0), (1, 2), (2, 1)])
     zx = proj_zx.reshape(width, 2 * inner)
-    own_x = call(
-        half_kernel, struct((width, inner), BF16), [VMEM], VMEM, cost(1_000, 0, 500_000), mib=2
-    )(zx)
-    other_x = lax.ppermute(own_x, *beside)
 
     pack, late, far, near = call(
         pack_kernel,
@@ -488,10 +479,12 @@
             out_proj,
         ),
     )
+    beside = (("seq_1", "x_hi"), [(0, 3), (3, 0), (1, 2), (2, 1)])
     other_pack = lax.ppermute(pack, *beside)
     got_far = lax.ppermute(far, SEQ, outer)
     got_near = lax.ppermute(near, SEQ, inside_pairs)
 
+    late, got_far, got_near = lax.optimization_barrier((late, got_far, got_near))
     other_late = lax.ppermute(late, *beside)
     u, own_gate, y, c, cols, first, gains, send = call(
         front_kernel,
@@ -505,7 +498,7 @@
             struct((8, 2 * inner), F32),
             struct((count, 16, LANES), BF16),
         ),
-        [SMEM] + [VMEM] * 9,
+        [SMEM] + [VMEM] * 8,
         (VMEM,) * 8,
         cost(8_000_000_000, 3_000_000, 24_000_000),
         scratch=[
@@ -514,9 +507,7 @@
             pltpu.VMEM((48, rows), F32),
             pltpu.VMEM((2 * inner // LANES + 1, rows + 2 * HALO, LANES), F32),
         ],
-    )(
-        place, hidden_in, zx, other_x, got_far, got_near, pack, other_pack, proj_bc, conv_bc
-    )
+    )(place, hidden_in, zx, got_far, got_near, pack, other_pack, proj_bc, conv_bc)
     def passed_on(place, send, *others):
         got = lax.all_to_all(send, SEQ, 0, 0, tiled=True)
         scanned = call(

time: 66.8 us -> 66.9 us (level)
  waiting for transfers between devices: 1.18 us -> 2.5 us
    ppermute x1 -> x0, starting transfers between devices: 3.39 us -> none  [shards(): other_x = lax.ppermute(own_x, *beside)]
    ppermute x1, starting transfers between devices: 0.11 us -> 3.39 us  [shards(): other_pack = lax.ppermute(pack, *beside)]
    ppermute x1, waiting for transfers between devices: 0.01 us -> 1.33 us  [shards(): got_near = lax.ppermute(near, SEQ, inside_pairs)]
  transfers between devices with their start and end apart: 6 -> 5, of which waited for: 1 -> 2; matrix products, arithmetic and copies ran while one was open for 0% -> 0% of each run, Pallas kernels for 12% -> 10%
where the time goes in v10:
time: 66.9 us; the launch traced here: 66.7 us
  blocking collectives  36.1 us (54%)
  starting transfers between devices  15.1 us (23%)
  Pallas kernels  10.8 us (16%)
  waiting for transfers between devices  2.5 us (4%)
  local copies, waits for them, and re-layouts  1.24 us (2%)
  other arithmetic  0.84 us (1%)
    all_to_all x1, blocking collectives, passed_on(): got = lax.all_to_all(send, SEQ, 0, 0, tiled=True)  21.8 us
    all_to_all x1, blocking collectives, passed_on(): return (lax.all_to_all(scanned, SEQ, 0, 0, tiled=True), *others)  14.3 us
    pallas_call x1, Pallas kernels, shards(): call(front_kernel, (struct((rows, width), BF16), struct((rows, inner), F3...  5.76 us
    ppermute x1, starting transfers between devices, shards(): taken = lax.ppermute(give, 'core', swap)  5 us
    ppermute x1, starting transfers between devices, shards(): got_near = lax.ppermute(near, SEQ, inside_pairs)  3.93 us
    ppermute x1, starting transfers between devices, shards(): other_pack = lax.ppermute(pack, *beside)  3.39 us
    pallas_call x1, Pallas kernels, shards(): call(back_kernel, (struct((rows, inner), F32), struct((rows, inner), BF16...  2.54 us
    ppermute x1, starting transfers between devices, shards(): other_late = lax.ppermute(late, *beside)  2.12 us
  transfers between devices with their start and end apart: 5, of which 2 were waited for; matrix products, arithmetic and copies ran while one was open for 0% of the time, Pallas kernels for 10%

profile of v10, /device:TPU:1, one launch (start us, length us, event | category | flops | bytes accessed | tf_op | source)
XLA Modules:
  0.0 66.7 jit_solution(3491081980712914802)
XLA Ops:
  0.0 0.0 copy-start
  0.0 0.0 copy-start.3
  0.0 0.0 copy-start.2
  0.0 1.2 %copy.12 = bf16[64,8,2,256]{3,1,2,0:T(8,128)(2,1)S(1)} copy(bf16[64,8,2,256]{3,2,1,0:T(2,128)(2,1)} %bitcast.12) | data formatting | bytes 1048576
  1.3 0.1 pad_add_fusion.place_ref
  1.3 1.8 %shard_map.109 = (bf16[544,256]{1,0:T(8,128)(2,1)S(1)}, bf16[512,512]{1,0:T(8,128)(2,1)S(1)}, bf16[8,512]{1,0:T(8,128)(2,1)S(1)}, bf16[8,512]{1,0:T(8,128)(2,1)S(1)}) custom-call(s32[4]{0:T(128)S(1)} %pad_add_fusion.place_ref, bf16[512,512]{1,0:T(8,128)(2,1)S(1)} %bitcast.10, bf16[4,512]{1,0:T(4,128)(2,1)} %bitcast.13, bf16[4,256]{1,0:T(4,128)(2,1)} %taps_hbm.1, ...), custom_call_target="tpu_custom_call" | custom-call | flops 1000000 | bytes 1000000 | tf_op jit(solution)/shard_map/pallas_call | solution.py:448
  3.2 3.4 %collective-permute-start.2 = (bf16[544,256]{1,0:T(8,128)(2,1)S(1)}, bf16[544,256]{1,0:T(8,128)(2,1)S(1)}, u32[]{:S(2)}, u32[]{:S(2)}) collective-permute-start(bf16[544,256]{1,0:T(8,128)(2,1)S(1)} %get-tuple-element.86.own_ref), channel_id=1, source_target_pairs={{0,18},{18,0},{2,16},{16,2},{1,19},{19,1},{3,17},{17,3},{4,22},{22... | collective-permute-start | bytes 835592 | tf_op jit(solution)/shard_map/ppermute | solution.py:483
  6.6 0.6 collective-permute-start
  7.2 3.9 %collective-permute-start.1 = (bf16[8,512]{1,0:T(8,128)(2,1)S(1)}, bf16[8,512]{1,0:T(8,128)(2,1)S(1)}, u32[]{:S(2)}, u32[]{:S(2)}) collective-permute-start(bf16[8,512]{1,0:T(8,128)(2,1)S(1)} %get-tuple-element.83), channel_id=1, source_target_pairs={{0,4},{4,0},{8,12},{12,8},{16,20},{20,16},{24,28},{28,24},{32,36},... | collective-permute-start | bytes 24584 | tf_op jit(solution)/shard_map/ppermute | solution.py:485
  11.1 0.0 collective-permute-done.far_ref
  11.1 1.3 %collective-permute-done.1.near_ref = bf16[8,512]{1,0:T(8,128)(2,1)S(1)} collective-permute-done((bf16[8,512]{1,0:T(8,128)(2,1)S(1)}, bf16[8,512]{1,0:T(8,128)(2,1)S(1)}, u32[]{:S(2)}, u32[]{:S(2)}) %collective-permute-start.1) | collective-permute-done | bytes 8224 | tf_op jit(solution)/shard_map/ppermute | solution.py:485
  12.5 2.1 %collective-permute-start.3 = (bf16[512,512]{1,0:T(8,128)(2,1)S(1)}, bf16[512,512]{1,0:T(8,128)(2,1)S(1)}, u32[]{:S(2)}, u32[]{:S(2)}) collective-permute-start(bf16[512,512]{1,0:T(8,128)(2,1)S(1)} %get-tuple-element.103), channel_id=1, source_target_pairs={{0,18},{18,0},{2,16},{16,2},{1,19},{19,1},{3,17},{17,3},{4,22},{22... | collective-permute-start | bytes 1572872 | tf_op jit(solution)/shard_map/ppermute | solution.py:488
  14.6 0.0 collective-permute-done.2.other_ref
  14.6 0.0 copy-done
  14.6 0.0 copy-done.3
  14.6 0.0 copy-done.2
  14.6 5.8 %shard_map.110 = (bf16[512,512]{1,0:T(8,128)(2,1)S(1)}, f32[512,256]{1,0:T(8,128)S(1)}, f32[2,512,512]{2,1,0:T(8,128)S(1)}, bf16[2,512,128]{2,1,0:T(8,128)(2,1)S...) custom-call(s32[4]{0:T(128)S(1)} %pad_add_fusion.place_ref, ...), custom_call_target="tpu_custom_call" | custom-call | flops 8000000000 | bytes 24000000 | tf_op jit(solution)/shard_map/pallas_call | solution.py:489
  20.4 0.0 copy-start.1
  20.4 36.8 %conditional.1 = (bf16[64,8,128]{2,1,0:T(8,128)(2,1)S(1)}, f32[2,512,512]{2,1,0:T(8,128)S(1)}, bf16[2,512,128]{2,1,0:T(8,128)(2,1)S(1)}, f32[512,128]{1,0:T(8,12...) conditional(s32[]{:T(128)} %convert_element_type.9, ...), branch_computations={%region_0.0_spmd, %region_1.0_spmd} | conditional | flops 1000000 | bytes 8159296 | solution.py:522
  20.4 21.8 %all_to_all.8.got_ref = bf16[64,16,128]{2,1,0:T(8,128)(2,1)S(1)} all-to-all(bf16[64,16,128]{2,1,0:T(8,128)(2,1)S(1)} %get-tuple-element.48), channel_id=1, replica_groups=mesh['seq_0'=8,'seq_1'=2,'seq_2'=4,'x_hi'=2,'core'=2] {'seq_0','seq_1','..., dimensions={0} | all-to-all | bytes 524288 | tf_op jit(solution)/shard_map/cond/branch_1_fun/all_to_all | solution.py:512
  42.2 0.7 %branch_1_fun.1 = bf16[64,8,128]{2,1,0:T(8,128)(2,1)S(1)} custom-call(s32[4]{0:T(128)S(1)} %get-tuple-element.47.place_ref, bf16[64,16,128]{2,1,0:T(8,128)(2,1)S(1)} %all_to_all.8.got_ref), custom_call_target="tpu_custom_call" | custom-call | flops 1000000 | bytes 400000 | tf_op jit(solution)/shard_map/cond/branch_1_fun/pallas_call | solution.py:513
  42.9 14.3 %all_to_all.9 = bf16[64,8,128]{2,1,0:T(8,128)(2,1)S(1)} all-to-all(bf16[64,8,128]{2,1,0:T(8,128)(2,1)S(1)} %branch_1_fun.1), channel_id=1, replica_groups=mesh['seq_0'=8,'seq_1'=2,'seq_2'=4,'x_hi'=2,'core'=2] {'seq_0','seq_1','..., dimensions={0} | all-to-all | bytes 262144 | tf_op jit(solution)/shard_map/cond/branch_1_fun/all_to_all | solution.py:520
  57.2 0.0 collective-permute-done.3.late_ref
  57.2 0.0 copy-done.1
  57.2 2.5 %shard_map.111 = (f32[512,256]{1,0:T(8,128)S(1)}, bf16[512,256]{1,0:T(8,128)(2,1)S(1)}) custom-call(s32[4]{0:T(128)S(1)} %pad_add_fusion.place_ref, f32[2,512,512]{2,1,0:T(8,128)S(1)} %get-tuple-element.95.y_ref, bf16[2,512,128]{2,1,0:T(8,128)(2,1)S(1)} %get-tuple-element.96.c_ref, bf16[64,8,128]{2,1,0:T(8,128)(2,1)S(1)} %get-tuple-element.97.came_ref, ...), custom_call_target="tpu_custom_call" | custom-call | flops 2000000000 | bytes 6000000 | tf_op jit(solution)/shard_map/pallas_call | solution.py:529
  59.8 5.0 %collective-permute-start.4 = (bf16[512,256]{1,0:T(8,128)(2,1)S(1)}, bf16[512,256]{1,0:T(8,128)(2,1)S(1)}, u32[]{:S(2)}, u32[]{:S(2)}) collective-permute-start(bf16[512,256]{1,0:T(8,128)(2,1)S(1)} %get-tuple-element.105), channel_id=1, source_target_pairs={{0,1},{1,0},{2,3},{3,2},{4,5},{5,4},{6,7},{7,6},{8,9},{9,8},{10,11... | collective-permute-start | bytes 786440 | tf_op jit(solution)/shard_map/ppermute | solution.py:542
  64.8 1.2 %collective-permute-done.4 = bf16[512,256]{1,0:T(8,128)(2,1)S(1)} collective-permute-done((bf16[512,256]{1,0:T(8,128)(2,1)S(1)}, bf16[512,256]{1,0:T(8,128)(2,1)S(1)}, u32[]{:S(2)}, u32[]{:S(2)}) %collective-permute-start.4) | collective-permute-done | bytes 262176 | tf_op jit(solution)/shard_map/ppermute | solution.py:542
  65.9 0.8 %add_convert_fusion = bf16[512,256]{1,0:T(8,128)(2,1)} fusion(f32[512,256]{1,0:T(8,128)S(1)} %get-tuple-element.104, bf16[512,256]{1,0:T(8,128)(2,1)S(1)} %collective-permute-done.4), kind=kLoop, calls=%fused_computation | loop fusion | flops 393216 | bytes 1048576 | tf_op jit(solution)/shard_map/convert_element_type | solution.py:543
Async XLA Ops:
  0.0 14.6 %copy-start = (bf16[512,1024]{1,0:T(8,128)(2,1)S(1)}, bf16[512,1024]{1,0:T(8,128)(2,1)}, u32[]{:S(2)}) copy-start(bf16[512,1024]{1,0:T(8,128)(2,1)} %hidden_ref.3) | copy-start | bytes 3145732
  0.0 14.6 %copy-start.3 = (bf16[4,128]{1,0:T(4,128)(2,1)S(1)}, bf16[4,128]{1,0:T(4,128)(2,1)}, u32[]{:S(2)}) copy-start(bf16[4,128]{1,0:T(4,128)(2,1)} %tapbc_ref.1) | copy-start | bytes 3076
  0.0 14.6 %copy-start.2 = (bf16[512,128]{1,0:T(8,128)(2,1)S(1)}, bf16[512,128]{1,0:T(8,128)(2,1)}, u32[]{:S(2)}) copy-start(bf16[512,128]{1,0:T(8,128)(2,1)} %bc_ref.1) | copy-start | bytes 393220
  3.2 11.4 %collective-permute-start.2 = (bf16[544,256]{1,0:T(8,128)(2,1)S(1)}, bf16[544,256]{1,0:T(8,128)(2,1)S(1)}, u32[]{:S(2)}, u32[]{:S(2)}) collective-permute-start(bf16[544,256]{1,0:T(8,128)(2,1)S(1)} %get-tuple-element.86.own_ref), channel_id=1, source_target_pairs={{0,18},{18,0},{2,16},{16,2},{1,19},{19,1},{3,17},{17,3},{4,22},{22... | collective-permute-start | bytes 835592 | tf_op jit(solution)/shard_map/ppermute | solution.py:483
  6.6 4.6 %collective-permute-start = (bf16[8,512]{1,0:T(8,128)(2,1)S(1)}, bf16[8,512]{1,0:T(8,128)(2,1)S(1)}, u32[]{:S(2)}, u32[]{:S(2)}) collective-permute-start(bf16[8,512]{1,0:T(8,128)(2,1)S(1)} %get-tuple-element.82), channel_id=1, source_target_pairs={{4,8},{8,4},{12,16},{16,12},{20,24},{24,20},{28,32},{32,28},{36,40... | collective-permute-start | bytes 24584 | tf_op jit(solution)/shard_map/ppermute | solution.py:484
  7.2 5.3 %collective-permute-start.1 = (bf16[8,512]{1,0:T(8,128)(2,1)S(1)}, bf16[8,512]{1,0:T(8,128)(2,1)S(1)}, u32[]{:S(2)}, u32[]{:S(2)}) collective-permute-start(bf16[8,512]{1,0:T(8,128)(2,1)S(1)} %get-tuple-element.83), channel_id=1, source_target_pairs={{0,4},{4,0},{8,12},{12,8},{16,20},{20,16},{24,28},{28,24},{32,36},... | collective-permute-start | bytes 24584 | tf_op jit(solution)/shard_map/ppermute | solution.py:485
  12.5 44.7 %collective-permute-start.3 = (bf16[512,512]{1,0:T(8,128)(2,1)S(1)}, bf16[512,512]{1,0:T(8,128)(2,1)S(1)}, u32[]{:S(2)}, u32[]{:S(2)}) collective-permute-start(bf16[512,512]{1,0:T(8,128)(2,1)S(1)} %get-tuple-element.103), channel_id=1, source_target_pairs={{0,18},{18,0},{2,16},{16,2},{1,19},{19,1},{3,17},{17,3},{4,22},{22... | collective-permute-start | bytes 1572872 | tf_op jit(solution)/shard_map/ppermute | solution.py:488
  20.4 36.8 %copy-start.1 = (bf16[256,512]{1,0:T(8,128)(2,1)S(1)}, bf16[256,512]{1,0:T(8,128)(2,1)}, u32[]{:S(2)}) copy-start(bf16[256,512]{1,0:T(8,128)(2,1)} %own_out_ref.1) | copy-start | bytes 786436
  59.8 6.2 %collective-permute-start.4 = (bf16[512,256]{1,0:T(8,128)(2,1)S(1)}, bf16[512,256]{1,0:T(8,128)(2,1)S(1)}, u32[]{:S(2)}, u32[]{:S(2)}) collective-permute-start(bf16[512,256]{1,0:T(8,128)(2,1)S(1)} %get-tuple-element.105), channel_id=1, source_target_pairs={{0,1},{1,0},{2,3},{3,2},{4,5},{5,4},{6,7},{7,6},{8,9},{9,8},{10,11... | collective-permute-start | bytes 786440 | tf_op jit(solution)/shard_map/ppermute | solution.py:542

commit v11 on v10

--- a/solution.py
+++ b/solution.py
@@ -484,7 +484,6 @@
     got_far = lax.ppermute(far, SEQ, outer)
     got_near = lax.ppermute(near, SEQ, inside_pairs)
 
-    late, got_far, got_near = lax.optimization_barrier((late, got_far, got_near))
     other_late = lax.ppermute(late, *beside)
     u, own_gate, y, c, cols, first, gains, send = call(
         front_kernel,

time: 66.9 us -> 66.1 us (0.988)
  blocking collectives: 36.1 us -> 37.7 us
  starting transfers between devices: 15.1 us -> 13.5 us
  waiting for transfers between devices: 2.5 us -> 1.74 us
    all_to_all x1, blocking collectives: 21.8 us -> 23.4 us  [passed_on(): got = lax.all_to_all(send, SEQ, 0, 0, tiled=True)]
    ppermute x1, starting transfers between devices: 2.12 us -> 0.76 us  [shards(): other_late = lax.ppermute(late, *beside)]
    ppermute x1, waiting for transfers between devices: 1.33 us -> 0.57 us  [shards(): got_near = lax.ppermute(near, SEQ, inside_pairs)]
where the time goes in v11:
time: 66.1 us; the launch traced here: 65.9 us
  blocking collectives  37.7 us (57%)
  starting transfers between devices  13.5 us (20%)
  Pallas kernels  10.8 us (16%)
  waiting for transfers between devices  1.74 us (3%)
  local copies, waits for them, and re-layouts  1.24 us (2%)
  other arithmetic  0.84 us (1%)
    all_to_all x1, blocking collectives, passed_on(): got = lax.all_to_all(send, SEQ, 0, 0, tiled=True)  23.4 us
    all_to_all x1, blocking collectives, passed_on(): return (lax.all_to_all(scanned, SEQ, 0, 0, tiled=True), *others)  14.3 us
    pallas_call x1, Pallas kernels, shards(): call(front_kernel, (struct((rows, width), BF16), struct((rows, inner), F3...  5.76 us
    ppermute x1, starting transfers between devices, shards(): taken = lax.ppermute(give, 'core', swap)  4.76 us
    ppermute x1, starting transfers between devices, shards(): got_near = lax.ppermute(near, SEQ, inside_pairs)  3.93 us
    ppermute x1, starting transfers between devices, shards(): other_pack = lax.ppermute(pack, *beside)  3.39 us
    pallas_call x1, Pallas kernels, shards(): call(back_kernel, (struct((rows, inner), F32), struct((rows, inner), BF16...  2.55 us
    pallas_call x1, Pallas kernels, shards(): call(pack_kernel, (struct((PACKED, inner), BF16), struct((width, 2 * inne...  1.82 us
  transfers between devices with their start and end apart: 5, of which 2 were waited for; matrix products, arithmetic and copies ran while one was open for 0% of the time, Pallas kernels for 10%

profile of v11, /device:TPU:1, one launch (start us, length us, event | category | flops | bytes accessed | tf_op | source)
XLA Modules:
  0.0 65.9 jit_solution(8843905526134249920)
XLA Ops:
  0.0 0.0 copy-start
  0.0 0.0 copy-start.3
  0.0 0.0 copy-start.2
  0.0 1.2 %copy.12 = bf16[64,8,2,256]{3,1,2,0:T(8,128)(2,1)S(1)} copy(bf16[64,8,2,256]{3,2,1,0:T(2,128)(2,1)} %bitcast.12) | data formatting | bytes 1048576
  1.3 0.1 pad_add_fusion.place_ref
  1.3 1.8 %shard_map.109 = (bf16[544,256]{1,0:T(8,128)(2,1)S(1)}, bf16[512,512]{1,0:T(8,128)(2,1)S(1)}, bf16[8,512]{1,0:T(8,128)(2,1)S(1)}, bf16[8,512]{1,0:T(8,128)(2,1)S(1)}) custom-call(s32[4]{0:T(128)S(1)} %pad_add_fusion.place_ref, bf16[512,512]{1,0:T(8,128)(2,1)S(1)} %bitcast.10, bf16[4,512]{1,0:T(4,128)(2,1)} %bitcast.13, bf16[4,256]{1,0:T(4,128)(2,1)} %taps_hbm.1, ...), custom_call_target="tpu_custom_call" | custom-call | flops 1000000 | bytes 1000000 | tf_op jit(solution)/shard_map/pallas_call | solution.py:448
  3.2 3.4 %collective-permute-start.2 = (bf16[544,256]{1,0:T(8,128)(2,1)S(1)}, bf16[544,256]{1,0:T(8,128)(2,1)S(1)}, u32[]{:S(2)}, u32[]{:S(2)}) collective-permute-start(bf16[544,256]{1,0:T(8,128)(2,1)S(1)} %get-tuple-element.80.own_ref), channel_id=1, source_target_pairs={{0,18},{18,0},{2,16},{16,2},{1,19},{19,1},{3,17},{17,3},{4,22},{22... | collective-permute-start | bytes 835592 | tf_op jit(solution)/shard_map/ppermute | solution.py:483
  6.6 0.6 collective-permute-start
  7.2 3.9 %collective-permute-start.1 = (bf16[8,512]{1,0:T(8,128)(2,1)S(1)}, bf16[8,512]{1,0:T(8,128)(2,1)S(1)}, u32[]{:S(2)}, u32[]{:S(2)}) collective-permute-start(bf16[8,512]{1,0:T(8,128)(2,1)S(1)} %get-tuple-element.79), channel_id=1, source_target_pairs={{0,4},{4,0},{8,12},{12,8},{16,20},{20,16},{24,28},{28,24},{32,36},... | collective-permute-start | bytes 24584 | tf_op jit(solution)/shard_map/ppermute | solution.py:485
  11.1 0.8 %collective-permute-start.3 = (bf16[512,512]{1,0:T(8,128)(2,1)S(1)}, bf16[512,512]{1,0:T(8,128)(2,1)S(1)}, u32[]{:S(2)}, u32[]{:S(2)}) collective-permute-start(bf16[512,512]{1,0:T(8,128)(2,1)S(1)} %get-tuple-element.97), channel_id=1, source_target_pairs={{0,18},{18,0},{2,16},{16,2},{1,19},{19,1},{3,17},{17,3},{4,22},{22... | collective-permute-start | bytes 1572872 | tf_op jit(solution)/shard_map/ppermute | solution.py:487
  11.9 0.0 collective-permute-done.far_ref
  11.9 0.6 collective-permute-done.1.near_ref
  12.5 0.0 collective-permute-done.2.other_ref
  12.5 0.0 copy-done
  12.5 0.0 copy-done.3
  12.5 0.0 copy-done.2
  12.5 5.8 %shard_map.110 = (bf16[512,512]{1,0:T(8,128)(2,1)S(1)}, f32[512,256]{1,0:T(8,128)S(1)}, f32[2,512,512]{2,1,0:T(8,128)S(1)}, bf16[2,512,128]{2,1,0:T(8,128)(2,1)S...) custom-call(s32[4]{0:T(128)S(1)} %pad_add_fusion.place_ref, ...), custom_call_target="tpu_custom_call" | custom-call | flops 8000000000 | bytes 24000000 | tf_op jit(solution)/shard_map/pallas_call | solution.py:488
  18.3 0.0 copy-start.1
  18.3 38.4 %conditional.1 = (bf16[64,8,128]{2,1,0:T(8,128)(2,1)S(1)}, f32[2,512,512]{2,1,0:T(8,128)S(1)}, bf16[2,512,128]{2,1,0:T(8,128)(2,1)S(1)}, f32[512,128]{1,0:T(8,12...) conditional(s32[]{:T(128)} %convert_element_type.9, ...), branch_computations={%region_0.0_spmd, %region_1.0_spmd} | conditional | flops 1000000 | bytes 8159296 | solution.py:521
  18.3 23.4 %all_to_all.8.got_ref = bf16[64,16,128]{2,1,0:T(8,128)(2,1)S(1)} all-to-all(bf16[64,16,128]{2,1,0:T(8,128)(2,1)S(1)} %get-tuple-element.48), channel_id=1, replica_groups=mesh['seq_0'=8,'seq_1'=2,'seq_2'=4,'x_hi'=2,'core'=2] {'seq_0','seq_1','..., dimensions={0} | all-to-all | bytes 524288 | tf_op jit(solution)/shard_map/cond/branch_1_fun/all_to_all | solution.py:511
  41.7 0.7 %branch_1_fun.1 = bf16[64,8,128]{2,1,0:T(8,128)(2,1)S(1)} custom-call(s32[4]{0:T(128)S(1)} %get-tuple-element.47.place_ref, bf16[64,16,128]{2,1,0:T(8,128)(2,1)S(1)} %all_to_all.8.got_ref), custom_call_target="tpu_custom_call" | custom-call | flops 1000000 | bytes 400000 | tf_op jit(solution)/shard_map/cond/branch_1_fun/pallas_call | solution.py:512
  42.3 14.3 %all_to_all.9 = bf16[64,8,128]{2,1,0:T(8,128)(2,1)S(1)} all-to-all(bf16[64,8,128]{2,1,0:T(8,128)(2,1)S(1)} %branch_1_fun.1), channel_id=1, replica_groups=mesh['seq_0'=8,'seq_1'=2,'seq_2'=4,'x_hi'=2,'core'=2] {'seq_0','seq_1','..., dimensions={0} | all-to-all | bytes 262144 | tf_op jit(solution)/shard_map/cond/branch_1_fun/all_to_all | solution.py:519
  56.6 0.0 collective-permute-done.3.late_ref
  56.6 0.0 copy-done.1
  56.6 2.5 %shard_map.111 = (f32[512,256]{1,0:T(8,128)S(1)}, bf16[512,256]{1,0:T(8,128)(2,1)S(1)}) custom-call(s32[4]{0:T(128)S(1)} %pad_add_fusion.place_ref, f32[2,512,512]{2,1,0:T(8,128)S(1)} %get-tuple-element.89.y_ref, bf16[2,512,128]{2,1,0:T(8,128)(2,1)S(1)} %get-tuple-element.90.c_ref, bf16[64,8,128]{2,1,0:T(8,128)(2,1)S(1)} %get-tuple-element.91.came_ref, ...), custom_call_target="tpu_custom_call" | custom-call | flops 2000000000 | bytes 6000000 | tf_op jit(solution)/shard_map/pallas_call | solution.py:528
  59.2 4.8 %collective-permute-start.4 = (bf16[512,256]{1,0:T(8,128)(2,1)S(1)}, bf16[512,256]{1,0:T(8,128)(2,1)S(1)}, u32[]{:S(2)}, u32[]{:S(2)}) collective-permute-start(bf16[512,256]{1,0:T(8,128)(2,1)S(1)} %get-tuple-element.99), channel_id=1, source_target_pairs={{0,1},{1,0},{2,3},{3,2},{4,5},{5,4},{6,7},{7,6},{8,9},{9,8},{10,11... | collective-permute-start | bytes 786440 | tf_op jit(solution)/shard_map/ppermute | solution.py:541
  63.9 1.2 %collective-permute-done.4 = bf16[512,256]{1,0:T(8,128)(2,1)S(1)} collective-permute-done((bf16[512,256]{1,0:T(8,128)(2,1)S(1)}, bf16[512,256]{1,0:T(8,128)(2,1)S(1)}, u32[]{:S(2)}, u32[]{:S(2)}) %collective-permute-start.4) | collective-permute-done | bytes 262176 | tf_op jit(solution)/shard_map/ppermute | solution.py:541
  65.1 0.8 %add_convert_fusion = bf16[512,256]{1,0:T(8,128)(2,1)} fusion(f32[512,256]{1,0:T(8,128)S(1)} %get-tuple-element.98, bf16[512,256]{1,0:T(8,128)(2,1)S(1)} %collective-permute-done.4), kind=kLoop, calls=%fused_computation | loop fusion | flops 393216 | bytes 1048576 | tf_op jit(solution)/shard_map/convert_element_type | solution.py:542
Async XLA Ops:
  0.0 12.5 %copy-start = (bf16[512,1024]{1,0:T(8,128)(2,1)S(1)}, bf16[512,1024]{1,0:T(8,128)(2,1)}, u32[]{:S(2)}) copy-start(bf16[512,1024]{1,0:T(8,128)(2,1)} %hidden_ref.3) | copy-start | bytes 3145732
  0.0 12.5 %copy-start.3 = (bf16[4,128]{1,0:T(4,128)(2,1)S(1)}, bf16[4,128]{1,0:T(4,128)(2,1)}, u32[]{:S(2)}) copy-start(bf16[4,128]{1,0:T(4,128)(2,1)} %tapbc_ref.1) | copy-start | bytes 3076
  0.0 12.5 %copy-start.2 = (bf16[512,128]{1,0:T(8,128)(2,1)S(1)}, bf16[512,128]{1,0:T(8,128)(2,1)}, u32[]{:S(2)}) copy-start(bf16[512,128]{1,0:T(8,128)(2,1)} %bc_ref.1) | copy-start | bytes 393220
  3.2 9.3 %collective-permute-start.2 = (bf16[544,256]{1,0:T(8,128)(2,1)S(1)}, bf16[544,256]{1,0:T(8,128)(2,1)S(1)}, u32[]{:S(2)}, u32[]{:S(2)}) collective-permute-start(bf16[544,256]{1,0:T(8,128)(2,1)S(1)} %get-tuple-element.80.own_ref), channel_id=1, source_target_pairs={{0,18},{18,0},{2,16},{16,2},{1,19},{19,1},{3,17},{17,3},{4,22},{22... | collective-permute-start | bytes 835592 | tf_op jit(solution)/shard_map/ppermute | solution.py:483
  6.6 5.3 %collective-permute-start = (bf16[8,512]{1,0:T(8,128)(2,1)S(1)}, bf16[8,512]{1,0:T(8,128)(2,1)S(1)}, u32[]{:S(2)}, u32[]{:S(2)}) collective-permute-start(bf16[8,512]{1,0:T(8,128)(2,1)S(1)} %get-tuple-element.78), channel_id=1, source_target_pairs={{4,8},{8,4},{12,16},{16,12},{20,24},{24,20},{28,32},{32,28},{36,40... | collective-permute-start | bytes 24584 | tf_op jit(solution)/shard_map/ppermute | solution.py:484
  7.2 5.3 %collective-permute-start.1 = (bf16[8,512]{1,0:T(8,128)(2,1)S(1)}, bf16[8,512]{1,0:T(8,128)(2,1)S(1)}, u32[]{:S(2)}, u32[]{:S(2)}) collective-permute-start(bf16[8,512]{1,0:T(8,128)(2,1)S(1)} %get-tuple-element.79), channel_id=1, source_target_pairs={{0,4},{4,0},{8,12},{12,8},{16,20},{20,16},{24,28},{28,24},{32,36},... | collective-permute-start | bytes 24584 | tf_op jit(solution)/shard_map/ppermute | solution.py:485
  11.1 45.5 %collective-permute-start.3 = (bf16[512,512]{1,0:T(8,128)(2,1)S(1)}, bf16[512,512]{1,0:T(8,128)(2,1)S(1)}, u32[]{:S(2)}, u32[]{:S(2)}) collective-permute-start(bf16[512,512]{1,0:T(8,128)(2,1)S(1)} %get-tuple-element.97), channel_id=1, source_target_pairs={{0,18},{18,0},{2,16},{16,2},{1,19},{19,1},{3,17},{17,3},{4,22},{22... | collective-permute-start | bytes 1572872 | tf_op jit(solution)/shard_map/ppermute | solution.py:487
  18.3 38.4 %copy-start.1 = (bf16[256,512]{1,0:T(8,128)(2,1)S(1)}, bf16[256,512]{1,0:T(8,128)(2,1)}, u32[]{:S(2)}) copy-start(bf16[256,512]{1,0:T(8,128)(2,1)} %own_out_ref.1) | copy-start | bytes 786436
  59.2 5.9 %collective-permute-start.4 = (bf16[512,256]{1,0:T(8,128)(2,1)S(1)}, bf16[512,256]{1,0:T(8,128)(2,1)S(1)}, u32[]{:S(2)}, u32[]{:S(2)}) collective-permute-start(bf16[512,256]{1,0:T(8,128)(2,1)S(1)} %get-tuple-element.99), channel_id=1, source_target_pairs={{0,1},{1,0},{2,3},{3,2},{4,5},{5,4},{6,7},{7,6},{8,9},{9,8},{10,11... | collective-permute-start | bytes 786440 | tf_op jit(solution)/shard_map/ppermute | solution.py:541

commit v12 on v11

--- a/solution.py
+++ b/solution.py
@@ -96,9 +96,23 @@
 DT_AT, TAP_AT, SMALL_AT, PACKED = 512, 520, 528, 544
 
 
+def late_kernel(zx_ref, after_ref, out_hbm, late_ref, sems):
+    inner = out_hbm.shape[0]
+    copies = start_copies(
+        (
+            (out_hbm.at[:, :inner], late_ref.at[:inner, inner:]),
+            (out_hbm.at[:, inner:], late_ref.at[inner:, inner:]),
+        ),
+        sems,
+    )
+    late_ref[:, :inner] = zx_ref[:, :inner]
+    for copy in copies:
+        copy.wait()
+
+
 def pack_kernel(
-    place_ref, zx_ref, dt_hbm, taps_hbm, bias_hbm, exp_hbm, skip_hbm, gain_hbm, hidden_hbm, out_hbm,
-    pack_ref, late_ref, far_ref, near_ref,
+    place_ref, zx_ref, dt_hbm, taps_hbm, bias_hbm, exp_hbm, skip_hbm, gain_hbm, hidden_hbm,
+    pack_ref, far_ref, near_ref,
     dt_ref, taps_ref, bias_ref, exp_ref, skip_ref, gain_ref, sems,
 ):
     inner, heads = pack_ref.shape[1], dt_ref.shape[0]
@@ -115,13 +129,10 @@
             (gain_hbm, gain_ref),
             (hidden_hbm.at[pl.ds(pl.multiple_of(odd * last, HALO), HALO), columns], far_ref),
             (hidden_hbm.at[pl.ds(pl.multiple_of((1 - odd) * last, HALO), HALO), columns], near_ref),
-            (out_hbm.at[:, :inner], late_ref.at[:inner, inner:]),
-            (out_hbm.at[:, inner:], late_ref.at[inner:, inner:]),
         ),
         sems,
     )
     pack_ref[:DT_AT] = zx_ref[:, inner:]
-    late_ref[:, :inner] = zx_ref[:, :inner]
     for copy in copies:
         copy.wait()
     lane = iota((1, inner), 1)
@@ -445,16 +456,15 @@
     place = jnp.stack([x_hi, core, lax.axis_index(SEQ), jnp.int32(count)]).astype(jnp.int32)
     zx = proj_zx.reshape(width, 2 * inner)
 
-    pack, late, far, near = call(
+    pack, far, near = call(
         pack_kernel,
         (
             struct((PACKED, inner), BF16),
-            struct((width, 2 * inner), BF16),
             struct((HALO, width), BF16),
             struct((HALO, width), BF16),
         ),
-        [SMEM, VMEM] + [HBM] * 8,
-        (VMEM,) * 4,
+        [SMEM, VMEM] + [HBM] * 7,
+        (VMEM,) * 3,
         cost(1_000_000, 0, 1_000_000),
         scratch=[
             pltpu.VMEM((4, width), BF16),
@@ -463,7 +473,7 @@
             pltpu.VMEM((1, 4), jnp.int32),
             pltpu.VMEM((1, 4), F32),
             pltpu.VMEM((1, inner), F32),
-            dma(10),
+            dma(8),
         ],
     )(
         place,
@@ -476,7 +486,6 @@
             skip_gain.reshape(1, 4),
             norm_gain.reshape(1, inner),
             hidden_in,
-            out_proj,
         ),
     )
     beside = (("seq_1", "x_hi"), [(0, 3), (3, 0), (1, 2), (2, 1)])
@@ -484,6 +493,15 @@
     got_far = lax.ppermute(far, SEQ, outer)
     got_near = lax.ppermute(near, SEQ, inside_pairs)
 
+    late = call(
+        late_kernel,
+        struct((width, 2 * inner), BF16),
+        [VMEM, VMEM, HBM],
+        VMEM,
+        cost(1_000_000, 0, 1_000_000),
+        mib=4,
+        scratch=[dma(2)],
+    )(zx, near, *lying(out_proj))
     other_late = lax.ppermute(late, *beside)
     u, own_gate, y, c, cols, first, gains, send = call(
         front_kernel,

time: 66.1 us -> 65.8 us (level)
  Pallas kernels: 10.8 us -> 11.5 us
    pallas_call x1 -> x2, Pallas kernels: 1.82 us -> 2.5 us  [the longest x1 1.51 us: shards(): call(pack_kernel, (struct((PACKED, inner), BF16), struct((HALO, width), B...]
  transfers between devices with their start and end apart: 5 -> 5, of which waited for: 2 -> 1; matrix products, arithmetic and copies ran while one was open for 0% -> 0% of each run, Pallas kernels for 10% -> 11%
where the time goes in v12:
time: 65.8 us; the launch traced here: 65.6 us
  blocking collectives  37.2 us (57%)
  starting transfers between devices  13.5 us (21%)
  Pallas kernels  11.5 us (17%)
  local copies, waits for them, and re-layouts  1.24 us (2%)
  waiting for transfers between devices  1.17 us (2%)
  other arithmetic  0.84 us (1%)
    all_to_all x1, blocking collectives, passed_on(): got = lax.all_to_all(send, SEQ, 0, 0, tiled=True)  22.9 us
    all_to_all x1, blocking collectives, passed_on(): return (lax.all_to_all(scanned, SEQ, 0, 0, tiled=True), *others)  14.3 us
    pallas_call x1, Pallas kernels, shards(): call(front_kernel, (struct((rows, width), BF16), struct((rows, inner), F3...  5.75 us
    ppermute x1, starting transfers between devices, shards(): taken = lax.ppermute(give, 'core', swap)  4.75 us
    ppermute x1, starting transfers between devices, shards(): got_near = lax.ppermute(near, SEQ, inside_pairs)  3.93 us
    ppermute x1, starting transfers between devices, shards(): other_pack = lax.ppermute(pack, *beside)  3.39 us
    pallas_call x1, Pallas kernels, shards(): call(back_kernel, (struct((rows, inner), F32), struct((rows, inner), BF16...  2.55 us
    pallas_call x1, Pallas kernels, shards(): call(pack_kernel, (struct((PACKED, inner), BF16), struct((HALO, width), B...  1.51 us
  transfers between devices with their start and end apart: 5, of which 1 were waited for; matrix products, arithmetic and copies ran while one was open for 0% of the time, Pallas kernels for 11%

profile of v12, /device:TPU:1, one launch (start us, length us, event | category | flops | bytes accessed | tf_op | source)
XLA Modules:
  0.0 65.6 jit_solution(14039564947497181912)
XLA Ops:
  0.0 0.0 copy-start
  0.0 0.0 copy-start.3
  0.0 0.0 copy-start.2
  0.0 1.2 %copy.12 = bf16[64,8,2,256]{3,1,2,0:T(8,128)(2,1)S(1)} copy(bf16[64,8,2,256]{3,2,1,0:T(2,128)(2,1)} %bitcast.13) | data formatting | bytes 1048576
  1.3 0.1 pad_add_fusion.place_ref
  1.3 1.5 %shard_map.109 = (bf16[544,256]{1,0:T(8,128)(2,1)S(1)}, bf16[8,512]{1,0:T(8,128)(2,1)S(1)}, bf16[8,512]{1,0:T(8,128)(2,1)S(1)}) custom-call(s32[4]{0:T(128)S(1)} %pad_add_fusion.place_ref, bf16[512,512]{1,0:T(8,128)(2,1)S(1)} %bitcast.10, bf16[4,512]{1,0:T(4,128)(2,1)} %bitcast.14, bf16[4,256]{1,0:T(4,128)(2,1)} %taps_hbm.1, f32[1,4]{1,0:T(1,128)} %bitcast.16, ...), custom_call_target="tpu_custom_call" | custom-call | flops 1000000 | bytes 1000000 | tf_op jit(solution)/shard_map/pallas_call | solution.py:459
  2.9 3.4 %collective-permute-start.2 = (bf16[544,256]{1,0:T(8,128)(2,1)S(1)}, bf16[544,256]{1,0:T(8,128)(2,1)S(1)}, u32[]{:S(2)}, u32[]{:S(2)}) collective-permute-start(bf16[544,256]{1,0:T(8,128)(2,1)S(1)} %get-tuple-element.79.own_ref), channel_id=1, source_target_pairs={{0,18},{18,0},{2,16},{16,2},{1,19},{19,1},{3,17},{17,3},{4,22},{22... | collective-permute-start | bytes 835592 | tf_op jit(solution)/shard_map/ppermute | solution.py:492
  6.3 0.6 collective-permute-start
  6.9 3.9 %collective-permute-start.1 = (bf16[8,512]{1,0:T(8,128)(2,1)S(1)}, bf16[8,512]{1,0:T(8,128)(2,1)S(1)}, u32[]{:S(2)}, u32[]{:S(2)}) collective-permute-start(bf16[8,512]{1,0:T(8,128)(2,1)S(1)} %get-tuple-element.78.after_ref), channel_id=1, source_target_pairs={{0,4},{4,0},{8,12},{12,8},{16,20},{20,16},{24,28},{28,24},{32,36},... | collective-permute-start | bytes 24584 | tf_op jit(solution)/shard_map/ppermute | solution.py:494
  10.8 1.0 %shard_map.111 = bf16[512,512]{1,0:T(8,128)(2,1)S(1)} custom-call(bf16[512,512]{1,0:T(8,128)(2,1)S(1)} %bitcast.11, bf16[8,512]{1,0:T(8,128)(2,1)S(1)} %get-tuple-element.78.after_ref, bf16[256,512]{1,0:T(8,128)(2,1)} %own_out_ref.1), custom_call_target="tpu_custom_call" | custom-call | flops 1000000 | bytes 1000000 | tf_op jit(solution)/shard_map/pallas_call | solution.py:496
  11.8 0.8 %collective-permute-start.3 = (bf16[512,512]{1,0:T(8,128)(2,1)S(1)}, bf16[512,512]{1,0:T(8,128)(2,1)S(1)}, u32[]{:S(2)}, u32[]{:S(2)}) collective-permute-start(bf16[512,512]{1,0:T(8,128)(2,1)S(1)} %shard_map.111), channel_id=1, source_target_pairs={{0,18},{18,0},{2,16},{16,2},{1,19},{19,1},{3,17},{17,3},{4,22},{22... | collective-permute-start | bytes 1572872 | tf_op jit(solution)/shard_map/ppermute | solution.py:505
  12.6 0.0 collective-permute-done.far_ref
  12.6 0.0 collective-permute-done.1.near_ref
  12.6 0.0 collective-permute-done.2.other_ref
  12.6 0.0 copy-done
  12.6 0.0 copy-done.3
  12.6 0.0 copy-done.2
  12.6 5.8 %shard_map.110 = (bf16[512,512]{1,0:T(8,128)(2,1)S(1)}, f32[512,256]{1,0:T(8,128)S(1)}, f32[2,512,512]{2,1,0:T(8,128)S(1)}, bf16[2,512,128]{2,1,0:T(8,128)(2,1)S...) custom-call(s32[4]{0:T(128)S(1)} %pad_add_fusion.place_ref, ...), custom_call_target="tpu_custom_call" | custom-call | flops 8000000000 | bytes 24000000 | tf_op jit(solution)/shard_map/pallas_call | solution.py:506
  18.4 0.0 copy-start.1
  18.4 37.9 %conditional.1 = (bf16[64,8,128]{2,1,0:T(8,128)(2,1)S(1)}, f32[2,512,512]{2,1,0:T(8,128)S(1)}, bf16[2,512,128]{2,1,0:T(8,128)(2,1)S(1)}, f32[512,128]{1,0:T(8,12...) conditional(s32[]{:T(128)} %convert_element_type.9, ...), branch_computations={%region_0.0_spmd, %region_1.0_spmd} | conditional | flops 1000000 | bytes 8159296 | solution.py:539
  18.4 22.9 %all_to_all.8.got_ref = bf16[64,16,128]{2,1,0:T(8,128)(2,1)S(1)} all-to-all(bf16[64,16,128]{2,1,0:T(8,128)(2,1)S(1)} %get-tuple-element.48), channel_id=1, replica_groups=mesh['seq_0'=8,'seq_1'=2,'seq_2'=4,'x_hi'=2,'core'=2] {'seq_0','seq_1','..., dimensions={0} | all-to-all | bytes 524288 | tf_op jit(solution)/shard_map/cond/branch_1_fun/all_to_all | solution.py:529
  41.3 0.7 %branch_1_fun.1 = bf16[64,8,128]{2,1,0:T(8,128)(2,1)S(1)} custom-call(s32[4]{0:T(128)S(1)} %get-tuple-element.47.place_ref, bf16[64,16,128]{2,1,0:T(8,128)(2,1)S(1)} %all_to_all.8.got_ref), custom_call_target="tpu_custom_call" | custom-call | flops 1000000 | bytes 400000 | tf_op jit(solution)/shard_map/cond/branch_1_fun/pallas_call | solution.py:530
  42.0 14.3 %all_to_all.9 = bf16[64,8,128]{2,1,0:T(8,128)(2,1)S(1)} all-to-all(bf16[64,8,128]{2,1,0:T(8,128)(2,1)S(1)} %branch_1_fun.1), channel_id=1, replica_groups=mesh['seq_0'=8,'seq_1'=2,'seq_2'=4,'x_hi'=2,'core'=2] {'seq_0','seq_1','..., dimensions={0} | all-to-all | bytes 262144 | tf_op jit(solution)/shard_map/cond/branch_1_fun/all_to_all | solution.py:537
  56.3 0.0 collective-permute-done.3.late_ref
  56.3 0.0 copy-done.1
  56.3 2.5 %shard_map.112 = (f32[512,256]{1,0:T(8,128)S(1)}, bf16[512,256]{1,0:T(8,128)(2,1)S(1)}) custom-call(s32[4]{0:T(128)S(1)} %pad_add_fusion.place_ref, f32[2,512,512]{2,1,0:T(8,128)S(1)} %get-tuple-element.88.y_ref, bf16[2,512,128]{2,1,0:T(8,128)(2,1)S(1)} %get-tuple-element.89.c_ref, bf16[64,8,128]{2,1,0:T(8,128)(2,1)S(1)} %get-tuple-element.90.came_ref, ...), custom_call_target="tpu_custom_call" | custom-call | flops 2000000000 | bytes 6000000 | tf_op jit(solution)/shard_map/pallas_call | solution.py:546
  58.9 4.7 %collective-permute-start.4 = (bf16[512,256]{1,0:T(8,128)(2,1)S(1)}, bf16[512,256]{1,0:T(8,128)(2,1)S(1)}, u32[]{:S(2)}, u32[]{:S(2)}) collective-permute-start(bf16[512,256]{1,0:T(8,128)(2,1)S(1)} %get-tuple-element.97), channel_id=1, source_target_pairs={{0,1},{1,0},{2,3},{3,2},{4,5},{5,4},{6,7},{7,6},{8,9},{9,8},{10,11... | collective-permute-start | bytes 786440 | tf_op jit(solution)/shard_map/ppermute | solution.py:559
  63.6 1.2 %collective-permute-done.4 = bf16[512,256]{1,0:T(8,128)(2,1)S(1)} collective-permute-done((bf16[512,256]{1,0:T(8,128)(2,1)S(1)}, bf16[512,256]{1,0:T(8,128)(2,1)S(1)}, u32[]{:S(2)}, u32[]{:S(2)}) %collective-permute-start.4) | collective-permute-done | bytes 262176 | tf_op jit(solution)/shard_map/ppermute | solution.py:559
  64.8 0.8 %add_convert_fusion = bf16[512,256]{1,0:T(8,128)(2,1)} fusion(f32[512,256]{1,0:T(8,128)S(1)} %get-tuple-element.96, bf16[512,256]{1,0:T(8,128)(2,1)S(1)} %collective-permute-done.4), kind=kLoop, calls=%fused_computation | loop fusion | flops 393216 | bytes 1048576 | tf_op jit(solution)/shard_map/convert_element_type | solution.py:560
Async XLA Ops:
  0.0 12.6 %copy-start = (bf16[512,1024]{1,0:T(8,128)(2,1)S(1)}, bf16[512,1024]{1,0:T(8,128)(2,1)}, u32[]{:S(2)}) copy-start(bf16[512,1024]{1,0:T(8,128)(2,1)} %hidden_ref.3) | copy-start | bytes 3145732
  0.0 12.6 %copy-start.3 = (bf16[4,128]{1,0:T(4,128)(2,1)S(1)}, bf16[4,128]{1,0:T(4,128)(2,1)}, u32[]{:S(2)}) copy-start(bf16[4,128]{1,0:T(4,128)(2,1)} %tapbc_ref.1) | copy-start | bytes 3076
  0.0 12.6 %copy-start.2 = (bf16[512,128]{1,0:T(8,128)(2,1)S(1)}, bf16[512,128]{1,0:T(8,128)(2,1)}, u32[]{:S(2)}) copy-start(bf16[512,128]{1,0:T(8,128)(2,1)} %bc_ref.1) | copy-start | bytes 393220
  2.9 9.7 %collective-permute-start.2 = (bf16[544,256]{1,0:T(8,128)(2,1)S(1)}, bf16[544,256]{1,0:T(8,128)(2,1)S(1)}, u32[]{:S(2)}, u32[]{:S(2)}) collective-permute-start(bf16[544,256]{1,0:T(8,128)(2,1)S(1)} %get-tuple-element.79.own_ref), channel_id=1, source_target_pairs={{0,18},{18,0},{2,16},{16,2},{1,19},{19,1},{3,17},{17,3},{4,22},{22... | collective-permute-start | bytes 835592 | tf_op jit(solution)/shard_map/ppermute | solution.py:492
  6.3 6.3 %collective-permute-start = (bf16[8,512]{1,0:T(8,128)(2,1)S(1)}, bf16[8,512]{1,0:T(8,128)(2,1)S(1)}, u32[]{:S(2)}, u32[]{:S(2)}) collective-permute-start(bf16[8,512]{1,0:T(8,128)(2,1)S(1)} %get-tuple-element.77), channel_id=1, source_target_pairs={{4,8},{8,4},{12,16},{16,12},{20,24},{24,20},{28,32},{32,28},{36,40... | collective-permute-start | bytes 24584 | tf_op jit(solution)/shard_map/ppermute | solution.py:493
  6.9 5.7 %collective-permute-start.1 = (bf16[8,512]{1,0:T(8,128)(2,1)S(1)}, bf16[8,512]{1,0:T(8,128)(2,1)S(1)}, u32[]{:S(2)}, u32[]{:S(2)}) collective-permute-start(bf16[8,512]{1,0:T(8,128)(2,1)S(1)} %get-tuple-element.78.after_ref), channel_id=1, source_target_pairs={{0,4},{4,0},{8,12},{12,8},{16,20},{20,16},{24,28},{28,24},{32,36},... | collective-permute-start | bytes 24584 | tf_op jit(solution)/shard_map/ppermute | solution.py:494
  11.8 44.5 %collective-permute-start.3 = (bf16[512,512]{1,0:T(8,128)(2,1)S(1)}, bf16[512,512]{1,0:T(8,128)(2,1)S(1)}, u32[]{:S(2)}, u32[]{:S(2)}) collective-permute-start(bf16[512,512]{1,0:T(8,128)(2,1)S(1)} %shard_map.111), channel_id=1, source_target_pairs={{0,18},{18,0},{2,16},{16,2},{1,19},{19,1},{3,17},{17,3},{4,22},{22... | collective-permute-start | bytes 1572872 | tf_op jit(solution)/shard_map/ppermute | solution.py:505
  18.4 37.9 %copy-start.1 = (bf16[256,512]{1,0:T(8,128)(2,1)S(1)}, bf16[256,512]{1,0:T(8,128)(2,1)}, u32[]{:S(2)}) copy-start(bf16[256,512]{1,0:T(8,128)(2,1)} %own_out_ref.1) | copy-start | bytes 786436
  58.9 5.9 %collective-permute-start.4 = (bf16[512,256]{1,0:T(8,128)(2,1)S(1)}, bf16[512,256]{1,0:T(8,128)(2,1)S(1)}, u32[]{:S(2)}, u32[]{:S(2)}) collective-permute-start(bf16[512,256]{1,0:T(8,128)(2,1)S(1)} %get-tuple-element.97), channel_id=1, source_target_pairs={{0,1},{1,0},{2,3},{3,2},{4,5},{5,4},{6,7},{7,6},{8,9},{9,8},{10,11... | collective-permute-start | bytes 786440 | tf_op jit(solution)/shard_map/ppermute | solution.py:559
